TPU v7x, 256 devices: a whole 4x4x8 slice. The times are simulated.
256 devices in a mesh: rows: 8 (over y, core), labels: 32 (over x, z).
Axes of the slice: x: 4, y: 4, z: 8, core: 2. Of those that a mesh axis runs over, the one named last changes fastest.
Arguments:
- embeddings: bfloat16 [8192, 768], P(('rows', 'labels')), may hold values from -6 to 6
- class_weight: bfloat16 [65536, 768], P('labels'), may hold values from -0.4375 to 0.4375
- class_bias: float32 [65536], P('labels'), may hold values from -10 to -8
- propensity: float32 [65536], P('labels'), may hold values from 0.1 to 0.9
- label_ids: int32 [8192, 32], P('rows'), may hold values from 0 to 65535
- label_count: int32 [8192], P('rows'), may hold values from 1 to 32
- label_bins: int32 [65536], P('labels'), may hold values from 0 to 15
- prior_mean: float32 [16], replicated, may hold values from 0.1 to 0.9
Outputs:
- new_propensity: float32 [65536], P('labels')
- weight_grad: bfloat16 [65536, 768], P('labels', 'rows')
- embed_grad: bfloat16 [8192, 768], P(('rows', 'labels'))
Inputs may be any that keep to these rules, and one draw needn't show every extreme that they name: `label_ids`: entries past a row's count are padding and are ignored; ids may repeat.
All inputs are finite; a program needn't handle non-finite values.
Results may differ from a plain program's by a relative error of at most 0.014.
Values may be sent and summed in bfloat16 or wider, within the bound.
No kernel may reach another device: no remote copies, remote signals or barrier semaphores. Data moves between devices by JAX's collectives and lax.ppermute only.
A program may use at most 64 MiB of HBM per device.

v0:
```python
import functools

import jax
import jax.numpy as jnp
from jax import lax
from jax.experimental import pallas as pl
from jax.experimental.pallas import tpu as pltpu
from jax.sharding import Mesh, PartitionSpec as P

BF = jnp.bfloat16
F32 = jnp.float32
LANES = 128
LOG2E = 1.4426950408889634
NX, NZ, NY, NC = 4, 8, 4, 2


def ring(n, d):
    return [(i, (i + d) % n) for i in range(n)]


def mm(a, b, dims):
    return lax.dot_general(a, b, (dims, ((), ())), preferred_element_type=F32)


def words_kernel(at_ref, ids_ref, count_ref, words_ref, obs_ref, *, width):
    slots, rows = ids_ref.shape
    lanes = lax.broadcasted_iota(jnp.int32, (LANES, LANES), 1)
    slot = lax.broadcasted_iota(jnp.int32, (slots, LANES), 0)
    counts = [jnp.zeros((8, LANES), jnp.int32) for _ in range(width // LANES)]
    for first in range(0, rows, LANES):
        turned = lax.rem(at_ref[1] + first, rows)
        source = pl.ds(pl.multiple_of(turned, LANES), LANES)
        local = ids_ref[:, source] - at_ref[0]
        valid = (slot < count_ref[:, source]) & (local >= 0) & (local < width)
        bit = jnp.left_shift(jnp.int32(256), jnp.where(valid, local >> 7, 0))
        code = jnp.where(valid, bit | (local & (LANES - 1)), 255).T
        words = jnp.zeros((LANES, LANES), jnp.int32)
        for i in range(slots):
            here = jnp.broadcast_to(code[:, i : i + 1], (LANES, LANES))
            words = words | jnp.where((here & 255) == lanes, here >> 8, 0)
        words_ref[first : first + LANES, :] = words
        for b in range(width // LANES):
            hit = (words >> b) & 1
            counts[b] = counts[b] + jnp.sum(hit.reshape(LANES // 8, 8, LANES), axis=0)
    for b in range(width // LANES):
        obs_ref[:, b * LANES : (b + 1) * LANES] = jnp.sum(
            counts[b].astype(F32), axis=0, keepdims=True
        )


def words_call(at, ids, count, width):
    rows = ids.shape[1]
    return pl.pallas_call(
        functools.partial(words_kernel, width=width),
        in_specs=[pl.BlockSpec(memory_space=pltpu.SMEM)] + in_vmem(2),
        out_specs=in_vmem(2),
        out_shape=[
            jax.ShapeDtypeStruct((rows, LANES), jnp.int32),
            jax.ShapeDtypeStruct((1, width), F32),
        ],
        cost_estimate=pl.CostEstimate(
            flops=200 * rows * LANES, bytes_accessed=8 * rows * LANES, transcendentals=0
        ),
        compiler_params=pltpu.CompilerParams(vmem_limit_bytes=16 << 20),
        name="words",
    )(at, ids, count)


def score_kernel(*refs, at, chunk, tile):
    count = len(at)
    x_refs, words_ref = refs[:count], refs[count]
    w_ref, bias_ref, prop_ref = refs[count + 1 : count + 4]
    res_refs, post_ref = refs[count + 4 : 2 * count + 4], refs[2 * count + 4]
    slots, sems = refs[2 * count + 5 : 3 * count + 5], refs[3 * count + 5]
    copies = []
    for t in range(w_ref.shape[0] // tile):
        cols = slice(t * tile, (t + 1) * tile)
        bias = bias_ref[:, cols] * -LOG2E
        prop = prop_ref[:, cols]
        rest = 1.0 - prop
        total = jnp.zeros((8, tile), F32)
        for k in range(count):
            size = min(chunk, x_refs[k].shape[0])
            for start in range(0, x_refs[k].shape[0], size):
                rows = slice(start, start + size)
                scores = mm(x_refs[k][rows, :], w_ref[cols, :], ((1,), (1,)))
                grown = 1.0 + jnp.exp2(scores * -LOG2E + bias)
                prob = 1.0 / grown
                unseen = rest / (grown - prop)
                words = words_ref[at[k] + start : at[k] + start + size, :]
                bits = range(t * tile // LANES, (t + 1) * tile // LANES)
                seen = jnp.concatenate([words & (1 << b) for b in bits], axis=1)
                posterior = jnp.where(seen != 0, 1.0, unseen)
                slots[k][t, rows, :] = (prob - posterior).astype(BF)
                total = total + jnp.sum(posterior.reshape(size // 8, 8, tile), axis=0)
            copy = pltpu.make_async_copy(slots[k].at[t], res_refs[k].at[:, cols], sems.at[k, t])
            copy.start()
            copies.append(copy)
        post_ref[:, cols] = jnp.sum(total, axis=0, keepdims=True)
    for copy in copies:
        copy.wait()


def in_vmem(count):
    return [pl.BlockSpec(memory_space=pltpu.VMEM)] * count


def score_call(xs, at, words, w, bias, prop, chunk=256, tile=512):
    width, depth = w.shape
    rows = sum(x.shape[0] for x in xs)
    tiles = width // tile
    *res, post = pl.pallas_call(
        functools.partial(score_kernel, at=at, chunk=chunk, tile=tile),
        in_specs=in_vmem(len(xs) + 4),
        out_specs=[pl.BlockSpec(memory_space=pltpu.HBM)] * len(xs) + in_vmem(1),
        out_shape=[pltpu.HBM((x.shape[0], width), BF) for x in xs]
        + [jax.ShapeDtypeStruct((1, width), F32)],
        scratch_shapes=[pltpu.VMEM((tiles, x.shape[0], tile), BF) for x in xs]
        + [pltpu.SemaphoreType.DMA((len(xs), tiles))],
        cost_estimate=pl.CostEstimate(
            flops=2 * rows * width * depth,
            bytes_accessed=2 * (rows * depth + width * depth + rows * width),
            transcendentals=3 * rows * width,
        ),
        compiler_params=pltpu.CompilerParams(vmem_limit_bytes=24 << 20),
        name="scores",
    )(*xs, words, w, bias, prop)
    return res, post


def weight_kernel(core_ref, *refs, count):
    x_refs, r_refs = refs[:count], refs[count : 2 * count]
    kept_ref, given_ref, x_all, r_all, out = refs[2 * count :]
    mine = core_ref[0]

    @pl.when(pl.program_id(0) == 0)
    def _():
        at = 0
        for x_ref in x_refs:
            x_all[at : at + x_ref.shape[0], :] = x_ref[...]
            at += x_ref.shape[0]

    at = 0
    for r_ref in r_refs:
        r_all[at : at + r_ref.shape[0], :] = r_ref[...]
        at += r_ref.shape[0]
    out[...] = mm(x_all[...], r_all[...], ((0,), (0,))).astype(BF)
    step = kept_ref.shape[1]
    for y in range(NY):
        kept_ref[y] = out[pl.ds(pl.multiple_of((y * NC + mine) * step, step), step), :]
        given_ref[y] = out[pl.ds(pl.multiple_of((y * NC + 1 - mine) * step, step), step), :]


def weight_call(core, xs, rs, tile=512):
    depth = xs[0].shape[1]
    width = rs[0].shape[1]
    rows = sum(x.shape[0] for x in xs)
    step = depth // (NY * NC)
    half = pl.BlockSpec((NY, step, tile), lambda i: (0, 0, i))
    return pl.pallas_call(
        functools.partial(weight_kernel, count=len(xs)),
        grid=(width // tile,),
        in_specs=[pl.BlockSpec(memory_space=pltpu.SMEM)]
        + [pl.BlockSpec(x.shape, lambda i: (0, 0)) for x in xs]
        + [pl.BlockSpec((r.shape[0], tile), lambda i: (0, i)) for r in rs],
        out_specs=[half, half],
        out_shape=[pltpu.HBM((NY, step, width), BF)] * 2,
        scratch_shapes=[
            pltpu.VMEM((rows, depth), BF),
            pltpu.VMEM((rows, tile), BF),
            pltpu.VMEM((depth, tile), BF),
        ],
        cost_estimate=pl.CostEstimate(
            flops=2 * rows * width * depth,
            bytes_accessed=2 * (rows * (depth + width) + width * depth),
            transcendentals=0,
        ),
        compiler_params=pltpu.CompilerParams(vmem_limit_bytes=60 << 20),
        name="weights",
    )(core, *xs, *rs)


def bin_prior(bins, prior_mean):
    levels = jnp.arange(prior_mean.shape[0], dtype=jnp.int32)
    onehot = (bins[:, None] == levels[None, :]).astype(F32)
    return jnp.sum(onehot * prior_mean[None, :], axis=1)


def shift(v, axis, n, d):
    return lax.ppermute(v, axis, ring(n, d))


def exchange(v, axis):
    return lax.all_to_all(v, axis, split_axis=0, concat_axis=0, tiled=True)


def body(
    embeddings, class_weight, class_bias, propensity, label_ids, label_count, label_bins, prior_mean
):
    width, depth = class_weight.shape
    part = embeddings.shape[0]
    block = part * NZ
    x_at, core, y = (lax.axis_index(a) for a in ("x", "core", "y"))
    offset = (x_at * NZ + lax.axis_index("z")) * width
    bias, prop = class_bias[None, :], propensity[None, :]

    own = exchange(jnp.tile(embeddings, (NZ, 1)), "z")
    at = jnp.stack([offset, x_at * block])
    words, obs = words_call(at, label_ids.T, label_count[None, :], width)
    prior = bin_prior(label_bins, prior_mean)

    def brought(d):
        return shift(own, "x", NX, -d)

    front, back, far = brought(1), brought(3), brought(2)
    (res0,), post0 = score_call((own,), (0,), words, class_weight, bias, prop)
    (res1, res3), post1 = score_call(
        (front, back), (block, 3 * block), words, class_weight, bias, prop
    )
    far, post1 = lax.optimization_barrier((far, post1))
    (res2,), post2 = score_call((far,), (2 * block,), words, class_weight, bias, prop)
    post = (post0 + post1) + post2
    both = jnp.concatenate([obs, post], axis=0)[None]
    sums = jnp.sum(exchange(jnp.tile(both, (NY * NC, 1, 1)), ("y", "core")), axis=0)
    updated = ((sums[0:1] + 8.0 * prior[None, :]) / (sums[1:2] + 8.0)).reshape(width)

    kept_rows, given = weight_call(core[None], (own, front, far, back), (res0, res1, res2, res3))
    pair = kept_rows.astype(F32) + shift(given, "core", NC, 1).astype(F32)
    pair = pair.astype(BF)
    pairs = [lax.dynamic_index_in_dim(pair, (y + d) % NY, 0, keepdims=False) for d in range(NY)]

    scaled_weight = (class_weight.astype(F32) / updated[:, None]).astype(BF)

    def term(r):
        return mm(r, scaled_weight, ((1,), (0,)))

    moved = []
    for d, r in ((2, res2), (1, res1), (3, res3)):
        moved.append(shift(term(r).astype(BF), "x", NX, d).astype(F32))
    kept = term(res0)
    kept, pairs = lax.optimization_barrier((kept, pairs))
    weight_sum = pairs[0].astype(F32)
    for d in (1, 2, 3):
        weight_sum = weight_sum + shift(pairs[d], "y", NY, d).astype(F32)
    weight_grad = (weight_sum / updated[None, :]).astype(BF).T

    parts = exchange((kept + moved[0] + moved[1] + moved[2]).astype(BF), "z")
    embed_grad = jnp.sum(parts.reshape(NZ, part, depth).astype(F32), axis=0).astype(BF)
    return updated, weight_grad, embed_grad


def solution(mesh):
    fine = Mesh(mesh.devices.reshape(NY, NC, NX, NZ), ("y", "core", "x", "z"))
    rows, labels = ("y", "core"), ("x", "z")
    both = rows + labels
    return jax.shard_map(
        body,
        mesh=fine,
        in_specs=(
            P(both, None),
            P(labels, None),
            P(labels),
            P(labels),
            P(rows, None),
            P(rows),
            P(labels),
            P(),
        ),
        out_specs=(P(labels), P(labels, rows), P(both, None)),
        check_vma=False,
    )
```

profile of v0, /device:TPU:16, one launch (start us, length us, event | category | flops | bytes accessed | tf_op | source)
XLA Modules:
  0.0 109.2 jit_solution(927137158170693248)
XLA Ops:
  0.6 1.6 %tile.4 = bf16[8,32,768]{2,1,0:T(8,128)(2,1)} broadcast(bf16[32,768]{1,0:T(8,128)(2,1)} %param.8), dimensions={1,2} | broadcast | bytes 442368 | tf_op jit(solution)/shard_map/tile | solution.py:207
  2.2 8.5 %all-to-all-start = ((bf16[8,32,768]{2,1,0:T(8,128)(2,1)}), bf16[8,32,768]{2,1,0:T(8,128)(2,1)S(1)}, u32[]{:S(2)}, u32[]{:S(2)}) async-start(bf16[8,32,768]{2,1,0:T(8,128)(2,1)} %tile.4), calls=%async_computation | async-start | bytes 786432 | tf_op jit(solution)/shard_map/all_to_all | solution.py:194
  12.4 6.2 %words.1 = (s32[1024,128]{1,0:T(8,128)S(1)}, f32[1,2048]{1,0:T(1,128)S(1)}) custom-call(s32[2]{0:T(128)S(1)} %pad_add_fusion.at_ref, s32[32,1024]{1,0:T(8,128)S(1)} %bitcast.34, s32[1,1024]{1,0:T(1,128)S(1)} %bitcast.41), custom_call_target="tpu_custom_call" | custom-call | flops 26214400 | bytes 1048576 | tf_op jit(solution)/shard_map/words/pallas_call | solution.py:53
  18.6 6.8 %all-to-all-done = bf16[8,32,768]{2,1,0:T(8,128)(2,1)S(1)} async-done(((bf16[8,32,768]{2,1,0:T(8,128)(2,1)}), bf16[8,32,768]{2,1,0:T(8,128)(2,1)S(1)}, u32[]{:S(2)}, u32[]{:S(2)}) %all-to-all-start) | async-done | bytes 393248 | tf_op jit(solution)/shard_map/all_to_all | solution.py:194
  25.4 1.5 %collective-permute-start.2 = (bf16[256,768]{1,0:T(8,128)(2,1)S(1)}, bf16[256,768]{1,0:T(8,128)(2,1)S(1)}, u32[]{:S(2)}, u32[]{:S(2)}) collective-permute-start(bf16[256,768]{1,0:T(8,128)(2,1)S(1)} %bitcast.29), channel_id=1, source_target_pairs={{0,8},{8,16},{16,24},{24,0},{1,9},{9,17},{17,25},{25,1},{2,10},{10... | collective-permute-start | bytes 1179656 | tf_op jit(solution)/shard_map/ppermute | solution.py:190
  26.9 1.7 %collective-permute-start.1 = (bf16[256,768]{1,0:T(8,128)(2,1)S(1)}, bf16[256,768]{1,0:T(8,128)(2,1)S(1)}, u32[]{:S(2)}, u32[]{:S(2)}) collective-permute-start(bf16[256,768]{1,0:T(8,128)(2,1)S(1)} %bitcast.30), channel_id=1, source_target_pairs={{0,24},{8,0},{16,8},{24,16},{1,25},{9,1},{17,9},{25,17},{2,26},{10... | collective-permute-start | bytes 1179656 | tf_op jit(solution)/shard_map/ppermute | solution.py:190
  29.4 2.1 %collective-permute-start = (bf16[256,768]{1,0:T(8,128)(2,1)S(1)}, bf16[256,768]{1,0:T(8,128)(2,1)S(1)}, u32[]{:S(2)}, u32[]{:S(2)}) collective-permute-start(bf16[256,768]{1,0:T(8,128)(2,1)S(1)} %bitcast.31), channel_id=1, source_target_pairs={{0,16},{8,24},{16,0},{24,8},{1,17},{9,25},{17,1},{25,9},{2,18},{10... | collective-permute-start | bytes 1179656 | tf_op jit(solution)/shard_map/ppermute | solution.py:190
  32.1 1.9 %copy-done = bf16[2048,768]{1,0:T(8,128)(2,1)S(1)} copy-done((bf16[2048,768]{1,0:T(8,128)(2,1)S(1)}, bf16[2048,768]{1,0:T(8,128)(2,1)}, u32[]{:S(2)}) %copy-start) | copy-done | bytes 3145752
  35.4 2.3 %scores.3 = (bf16[256,2048]{1,0:T(8,128)(2,1)}, f32[1,2048]{1,0:T(1,128)S(1)}) custom-call(bf16[256,768]{1,0:T(8,128)(2,1)S(1)} %bitcast.32, s32[1024,128]{1,0:T(8,128)S(1)} %get-tuple-element.22.refs_1_.refs_2_, bf16[2048,768]{1,0:T(8,128)(2,1)S(1)} %copy-done, f32[1,2048]{1,0:T(1,128)S(1)} %bitcast.35, f32[1,2048]{1,0:T(1,128)S(1)} %bitcast.38), custom_call_target="tpu_custom_call" | custom-call | flops 805306368 | bytes 4587520 | tf_op jit(solution)/shard_map/scores/pallas_call | solution.py:112
  38.5 5.9 %collective-permute-done.1.refs_0_.refs_1_ = bf16[256,768]{1,0:T(8,128)(2,1)S(1)} collective-permute-done((bf16[256,768]{1,0:T(8,128)(2,1)S(1)}, bf16[256,768]{1,0:T(8,128)(2,1)S(1)}, u32[]{:S(2)}, u32[]{:S(2)}) %collective-permute-start.1) | collective-permute-done | bytes 393248 | tf_op jit(solution)/shard_map/ppermute | solution.py:190
  44.5 1.0 copy-done.3
  45.5 3.6 %scores.4 = (bf16[256,2048]{1,0:T(8,128)(2,1)}, bf16[256,2048]{1,0:T(8,128)(2,1)}, f32[1,2048]{1,0:T(1,128)S(1)}) custom-call(bf16[256,768]{1,0:T(8,128)(2,1)S(1)} %collective-permute-done.1.refs_0_.refs_1_, bf16[256,768]{1,0:T(8,128)(2,1)S(1)} %collective-permute-done.2.refs_1_.refs_3_, s32[1024,128]{1,0:T(8,128)S(1)} %copy-done.3, ...), custom_call_target="tpu_custom_call" | custom-call | flops 1610612736 | bytes 6029312 | tf_op jit(solution)/shard_map/scores/pallas_call | solution.py:112
  49.2 2.3 %scores.5 = (bf16[256,2048]{1,0:T(8,128)(2,1)}, f32[1,2048]{1,0:T(1,128)S(1)}) custom-call(bf16[256,768]{1,0:T(8,128)(2,1)S(1)} %collective-permute-done.refs_0_.refs_2_, s32[1024,128]{1,0:T(8,128)S(1)} %copy-done.3, bf16[2048,768]{1,0:T(8,128)(2,1)S(1)} %copy-done.1, f32[1,2048]{1,0:T(1,128)S(1)} %bitcast.37, f32[1,2048]{1,0:T(1,128)S(1)} %bitcast.40), custom_call_target="tpu_custom_call" | custom-call | flops 805306368 | bytes 4587520 | tf_op jit(solution)/shard_map/scores/pallas_call | solution.py:112
  52.2 4.8 %all-to-all-start.1 = ((f32[8,2,2048]{2,1,0:T(2,128)}), f32[8,2,2048]{2,1,0:T(2,128)S(1)}, u32[]{:S(2)}, u32[]{:S(2)}) async-start(f32[8,2,2048]{2,1,0:T(2,128)} %tile.5), calls=%async_computation.1 | async-start | bytes 262144 | tf_op jit(solution)/shard_map/all_to_all | solution.py:194
  57.0 7.6 %weights.1 = (bf16[4,96,2048]{2,1,0:T(8,128)(2,1)}, bf16[4,96,2048]{2,1,0:T(8,128)(2,1)}) custom-call(s32[1]{0:T(128)} %bitcast.9.core_ref, bf16[256,768]{1,0:T(8,128)(2,1)} %bitcast.33, bf16[256,768]{1,0:T(8,128)(2,1)} %copy-done.12, bf16[256,768]{1,0:T(8,128)(2,1)} %copy-done.5, bf16[256,768]{1,0:T(8,128)(2,1)} %copy-done.11, ...), custom_call_target="tpu_custom_call" | custom-call | flops 3221225472 | bytes 8912896 | tf_op jit(solution)/shard_map/weights/pallas_call | solution.py:160
  68.3 4.5 %collective-permute-start.8 = (bf16[256,768]{1,0:T(8,128)(2,1)S(1)}, bf16[256,768]{1,0:T(8,128)(2,1)S(1)}, u32[]{:S(2)}, u32[]{:S(2)}) collective-permute-start(bf16[256,768]{1,0:T(8,128)(2,1)S(1)} %convolution_convert_fusion.1), channel_id=1, source_target_pairs={{0,8},{8,16},{16,24},{24,0},{1,9},{9,17},{17,25},{25,1},{2,10},{10... | collective-permute-start | bytes 1179656 | tf_op jit(solution)/shard_map/ppermute | solution.py:190
  75.1 1.9 %add_convert_fusion = bf16[4,96,2048]{2,1,0:T(8,128)(2,1)S(1)} fusion(bf16[4,96,2048]{2,1,0:T(8,128)(2,1)} %collective-permute-done.3, bf16[4,96,2048]{2,1,0:T(8,128)(2,1)S(1)} %copy-done.13), kind=kLoop, calls=%fused_computation.1 | loop fusion | flops 3145728 | bytes 4718592 | tf_op jit(solution)/shard_map/convert_element_type | solution.py:229
  77.1 1.2 %collective-permute-start.4 = (bf16[96,2048]{1,0:T(8,128)(2,1)S(1)}, bf16[96,2048]{1,0:T(8,128)(2,1)S(1)}, u32[]{:S(2)}, u32[]{:S(2)}) collective-permute-start(bf16[96,2048]{1,0:T(8,128)(2,1)S(1)} %get-tuple-element.35), channel_id=1, source_target_pairs={{0,64},{64,128},{128,192},{192,0},{1,65},{65,129},{129,193},{193,1... | collective-permute-start | bytes 1179656 | tf_op jit(solution)/shard_map/ppermute | solution.py:190
  79.3 1.4 %collective-permute-done.7 = bf16[256,768]{1,0:T(8,128)(2,1)S(1)} collective-permute-done((bf16[256,768]{1,0:T(8,128)(2,1)S(1)}, bf16[256,768]{1,0:T(8,128)(2,1)S(1)}, u32[]{:S(2)}, u32[]{:S(2)}) %collective-permute-start.7) | collective-permute-done | bytes 393248 | tf_op jit(solution)/shard_map/ppermute | solution.py:190
  81.2 7.2 %collective-permute-done.8 = bf16[256,768]{1,0:T(8,128)(2,1)S(1)} collective-permute-done((bf16[256,768]{1,0:T(8,128)(2,1)S(1)}, bf16[256,768]{1,0:T(8,128)(2,1)S(1)}, u32[]{:S(2)}, u32[]{:S(2)}) %collective-permute-start.8) | collective-permute-done | bytes 393248 | tf_op jit(solution)/shard_map/ppermute | solution.py:190
  90.5 3.5 %all-to-all-start.2 = ((bf16[8,32,768]{2,1,0:T(8,128)(2,1)}), bf16[8,32,768]{2,1,0:T(8,128)(2,1)S(1)}, u32[]{:S(2)}, u32[]{:S(2)}) async-start(bf16[8,32,768]{2,1,0:T(8,128)(2,1)} %bitcast.15), calls=%async_computation.2 | async-start | bytes 786432 | tf_op jit(solution)/shard_map/all_to_all | solution.py:194
  93.9 2.6 %collective-permute-done.5 = bf16[96,2048]{1,0:T(8,128)(2,1)S(1)} collective-permute-done((bf16[96,2048]{1,0:T(8,128)(2,1)S(1)}, bf16[96,2048]{1,0:T(8,128)(2,1)S(1)}, u32[]{:S(2)}, u32[]{:S(2)}) %collective-permute-start.5) | collective-permute-done | bytes 393248 | tf_op jit(solution)/shard_map/ppermute | solution.py:190
  96.5 1.8 %collective-permute-done.6 = bf16[96,2048]{1,0:T(8,128)(2,1)S(1)} collective-permute-done((bf16[96,2048]{1,0:T(8,128)(2,1)S(1)}, bf16[96,2048]{1,0:T(8,128)(2,1)S(1)}, u32[]{:S(2)}, u32[]{:S(2)}) %collective-permute-start.6) | collective-permute-done | bytes 393248 | tf_op jit(solution)/shard_map/ppermute | solution.py:190
  99.3 9.2 %all-to-all-done.2 = bf16[8,32,768]{2,1,0:T(8,128)(2,1)S(1)} async-done(((bf16[8,32,768]{2,1,0:T(8,128)(2,1)}), bf16[8,32,768]{2,1,0:T(8,128)(2,1)S(1)}, u32[]{:S(2)}, u32[]{:S(2)}) %all-to-all-start.2) | async-done | bytes 393248 | tf_op jit(solution)/shard_map/all_to_all | solution.py:194
  (66 shorter events, 17.1 us)
Async XLA Ops:
  0.6 43.8 %copy-start.9 = (f32[2048]{0:T(1024)S(1)}, f32[2048]{0:T(1024)}, u32[]{:S(2)}) copy-start(f32[2048]{0:T(1024)} %param.11) | copy-start | bytes 24580
  2.2 23.2 %all-to-all-start = ((bf16[8,32,768]{2,1,0:T(8,128)(2,1)}), bf16[8,32,768]{2,1,0:T(8,128)(2,1)S(1)}, u32[]{:S(2)}, u32[]{:S(2)}) async-start(bf16[8,32,768]{2,1,0:T(8,128)(2,1)} %tile.4), calls=%async_computation | async-start | bytes 786432 | tf_op jit(solution)/shard_map/all_to_all | solution.py:194
  25.4 23.7 %copy-start.4 = (bf16[8,32,768]{2,1,0:T(8,128)(2,1)}, bf16[8,32,768]{2,1,0:T(8,128)(2,1)S(1)}, u32[]{:S(2)}) copy-start(bf16[8,32,768]{2,1,0:T(8,128)(2,1)S(1)} %all-to-all-done) | copy-start | bytes 1179652
  25.4 13.1 %collective-permute-start.2 = (bf16[256,768]{1,0:T(8,128)(2,1)S(1)}, bf16[256,768]{1,0:T(8,128)(2,1)S(1)}, u32[]{:S(2)}, u32[]{:S(2)}) collective-permute-start(bf16[256,768]{1,0:T(8,128)(2,1)S(1)} %bitcast.29), channel_id=1, source_target_pairs={{0,8},{8,16},{16,24},{24,0},{1,9},{9,17},{17,25},{25,1},{2,10},{10... | collective-permute-start | bytes 1179656 | tf_op jit(solution)/shard_map/ppermute | solution.py:190
  26.9 17.6 %collective-permute-start.1 = (bf16[256,768]{1,0:T(8,128)(2,1)S(1)}, bf16[256,768]{1,0:T(8,128)(2,1)S(1)}, u32[]{:S(2)}, u32[]{:S(2)}) collective-permute-start(bf16[256,768]{1,0:T(8,128)(2,1)S(1)} %bitcast.30), channel_id=1, source_target_pairs={{0,24},{8,0},{16,8},{24,16},{1,25},{9,1},{17,9},{25,17},{2,26},{10... | collective-permute-start | bytes 1179656 | tf_op jit(solution)/shard_map/ppermute | solution.py:190
  29.4 19.7 %collective-permute-start = (bf16[256,768]{1,0:T(8,128)(2,1)S(1)}, bf16[256,768]{1,0:T(8,128)(2,1)S(1)}, u32[]{:S(2)}, u32[]{:S(2)}) collective-permute-start(bf16[256,768]{1,0:T(8,128)(2,1)S(1)} %bitcast.31), channel_id=1, source_target_pairs={{0,16},{8,24},{16,0},{24,8},{1,17},{9,25},{17,1},{25,9},{2,18},{10... | collective-permute-start | bytes 1179656 | tf_op jit(solution)/shard_map/ppermute | solution.py:190
  32.1 1.9 %copy-start = (bf16[2048,768]{1,0:T(8,128)(2,1)S(1)}, bf16[2048,768]{1,0:T(8,128)(2,1)}, u32[]{:S(2)}) copy-start(bf16[2048,768]{1,0:T(8,128)(2,1)} %refs_2_.3) | copy-start | bytes 9437188
  38.5 10.6 %copy-start.1 = (bf16[2048,768]{1,0:T(8,128)(2,1)S(1)}, bf16[2048,768]{1,0:T(8,128)(2,1)}, u32[]{:S(2)}) copy-start(bf16[2048,768]{1,0:T(8,128)(2,1)} %refs_2_.3) | copy-start | bytes 9437188
  38.5 12.9 %copy-start.11 = (bf16[256,768]{1,0:T(8,128)(2,1)}, bf16[256,768]{1,0:T(8,128)(2,1)S(1)}, u32[]{:S(2)}) copy-start(bf16[256,768]{1,0:T(8,128)(2,1)S(1)} %collective-permute-done.2.refs_1_.refs_3_) | copy-start | bytes 1179652
  45.5 6.0 %copy-start.12 = (bf16[256,768]{1,0:T(8,128)(2,1)}, bf16[256,768]{1,0:T(8,128)(2,1)S(1)}, u32[]{:S(2)}) copy-start(bf16[256,768]{1,0:T(8,128)(2,1)S(1)} %collective-permute-done.1.refs_0_.refs_1_) | copy-start | bytes 1179652
  49.1 2.4 %copy-start.5 = (bf16[256,768]{1,0:T(8,128)(2,1)}, bf16[256,768]{1,0:T(8,128)(2,1)S(1)}, u32[]{:S(2)}) copy-start(bf16[256,768]{1,0:T(8,128)(2,1)S(1)} %collective-permute-done.refs_0_.refs_2_) | copy-start | bytes 1179652
  52.2 12.5 %all-to-all-start.1 = ((f32[8,2,2048]{2,1,0:T(2,128)}), f32[8,2,2048]{2,1,0:T(2,128)S(1)}, u32[]{:S(2)}, u32[]{:S(2)}) async-start(f32[8,2,2048]{2,1,0:T(2,128)} %tile.5), calls=%async_computation.1 | async-start | bytes 262144 | tf_op jit(solution)/shard_map/all_to_all | solution.py:194
  57.0 7.7 %copy-start.15 = (f32[2048]{0:T(1024)S(1)}, f32[2048]{0:T(1024)}, u32[]{:S(2)}) copy-start(f32[2048]{0:T(1024)} %broadcast_multiply_fusion) | copy-start | bytes 24580
  64.6 10.5 %collective-permute-start.3 = (bf16[4,96,2048]{2,1,0:T(8,128)(2,1)}, bf16[4,96,2048]{2,1,0:T(8,128)(2,1)}, u32[]{:S(2)}, u32[]{:S(2)}) collective-permute-start(bf16[4,96,2048]{2,1,0:T(8,128)(2,1)} %get-tuple-element.33), channel_id=1, source_target_pairs={{0,32},{32,0},{1,33},{33,1},{2,34},{34,2},{3,35},{35,3},{4,36},{36... | collective-permute-start | bytes 4718600 | tf_op jit(solution)/shard_map/ppermute | solution.py:190
  64.8 33.5 %copy-start.14 = (f32[1,2048]{1,0:T(1,128)}, f32[1,2048]{1,0:T(1,128)S(1)}, u32[]{:S(2)}) copy-start(f32[1,2048]{1,0:T(1,128)S(1)} %fusion.1) | copy-start | bytes 24580
  67.0 5.7 %copy-start.18 = (bf16[256,2048]{1,0:T(8,128)(2,1)S(1)}, bf16[256,2048]{1,0:T(8,128)(2,1)}, u32[]{:S(2)}) copy-start(bf16[256,2048]{1,0:T(8,128)(2,1)} %get-tuple-element.31.refs_7_) | copy-start | bytes 3145732
  67.0 13.6 %collective-permute-start.7 = (bf16[256,768]{1,0:T(8,128)(2,1)S(1)}, bf16[256,768]{1,0:T(8,128)(2,1)S(1)}, u32[]{:S(2)}, u32[]{:S(2)}) collective-permute-start(bf16[256,768]{1,0:T(8,128)(2,1)S(1)} %convolution_convert_fusion.2), channel_id=1, source_target_pairs={{0,16},{8,24},{16,0},{24,8},{1,17},{9,25},{17,1},{25,9},{2,18},{10... | collective-permute-start | bytes 1179656 | tf_op jit(solution)/shard_map/ppermute | solution.py:190
  68.3 5.8 %copy-start.16 = (bf16[256,2048]{1,0:T(8,128)(2,1)S(1)}, bf16[256,2048]{1,0:T(8,128)(2,1)}, u32[]{:S(2)}) copy-start(bf16[256,2048]{1,0:T(8,128)(2,1)} %get-tuple-element.28.refs_4_) | copy-start | bytes 3145732
  68.3 20.2 %collective-permute-start.8 = (bf16[256,768]{1,0:T(8,128)(2,1)S(1)}, bf16[256,768]{1,0:T(8,128)(2,1)S(1)}, u32[]{:S(2)}, u32[]{:S(2)}) collective-permute-start(bf16[256,768]{1,0:T(8,128)(2,1)S(1)} %convolution_convert_fusion.1), channel_id=1, source_target_pairs={{0,8},{8,16},{16,24},{24,0},{1,9},{9,17},{17,25},{25,1},{2,10},{10... | collective-permute-start | bytes 1179656 | tf_op jit(solution)/shard_map/ppermute | solution.py:190
  73.7 15.8 %collective-permute-start.9 = (bf16[256,768]{1,0:T(8,128)(2,1)S(1)}, bf16[256,768]{1,0:T(8,128)(2,1)S(1)}, u32[]{:S(2)}, u32[]{:S(2)}) collective-permute-start(bf16[256,768]{1,0:T(8,128)(2,1)S(1)} %convolution_convert_fusion), channel_id=1, source_target_pairs={{0,24},{8,0},{16,8},{24,16},{1,25},{9,1},{17,9},{25,17},{2,26},{10... | collective-permute-start | bytes 1179656 | tf_op jit(solution)/shard_map/ppermute | solution.py:190
  77.1 16.8 %collective-permute-start.4 = (bf16[96,2048]{1,0:T(8,128)(2,1)S(1)}, bf16[96,2048]{1,0:T(8,128)(2,1)S(1)}, u32[]{:S(2)}, u32[]{:S(2)}) collective-permute-start(bf16[96,2048]{1,0:T(8,128)(2,1)S(1)} %get-tuple-element.35), channel_id=1, source_target_pairs={{0,64},{64,128},{128,192},{192,0},{1,65},{65,129},{129,193},{193,1... | collective-permute-start | bytes 1179656 | tf_op jit(solution)/shard_map/ppermute | solution.py:190
  78.4 18.1 %collective-permute-start.5 = (bf16[96,2048]{1,0:T(8,128)(2,1)S(1)}, bf16[96,2048]{1,0:T(8,128)(2,1)S(1)}, u32[]{:S(2)}, u32[]{:S(2)}) collective-permute-start(bf16[96,2048]{1,0:T(8,128)(2,1)S(1)} %get-tuple-element.36), channel_id=1, source_target_pairs={{0,128},{64,192},{128,0},{192,64},{1,129},{65,193},{129,1},{193,65... | collective-permute-start | bytes 1179656 | tf_op jit(solution)/shard_map/ppermute | solution.py:190
  80.7 17.7 %collective-permute-start.6 = (bf16[96,2048]{1,0:T(8,128)(2,1)S(1)}, bf16[96,2048]{1,0:T(8,128)(2,1)S(1)}, u32[]{:S(2)}, u32[]{:S(2)}) collective-permute-start(bf16[96,2048]{1,0:T(8,128)(2,1)S(1)} %get-tuple-element.37), channel_id=1, source_target_pairs={{0,192},{64,0},{128,64},{192,128},{1,193},{65,1},{129,65},{193,129... | collective-permute-start | bytes 1179656 | tf_op jit(solution)/shard_map/ppermute | solution.py:190
  90.5 18.0 %all-to-all-start.2 = ((bf16[8,32,768]{2,1,0:T(8,128)(2,1)}), bf16[8,32,768]{2,1,0:T(8,128)(2,1)S(1)}, u32[]{:S(2)}, u32[]{:S(2)}) async-start(bf16[8,32,768]{2,1,0:T(8,128)(2,1)} %bitcast.15), calls=%async_computation.2 | async-start | bytes 786432 | tf_op jit(solution)/shard_map/all_to_all | solution.py:194
  (9 other events, 8.7 us)
where the time goes:
time: 111 us; the launch traced here: 109 us
  waiting for transfers between devices  36 us (32%)
  starting transfers between devices  29.7 us (27%)
  Pallas kernels  22 us (20%)
  local copies, waits for them, and re-layouts  9.88 us (9%)
  other arithmetic  6.75 us (6%)
  matrix products  3.92 us (4%)
    ppermute x10, waiting for transfers between devices, shift(): return lax.ppermute(v, axis, ring(n, d))  20.1 us
    all_to_all x3, starting transfers between devices, exchange(): return lax.all_to_all(v, axis, split_axis=0, concat_axis=0, tiled=True)  16.7 us
    all_to_all x3, waiting for transfers between devices, exchange(): return lax.all_to_all(v, axis, split_axis=0, concat_axis=0, tiled=True)  16 us
    ppermute x10, starting transfers between devices, shift(): return lax.ppermute(v, axis, ring(n, d))  13 us
    pallas_call x3, Pallas kernels, score_call(): pl.pallas_call(functools.partial(score_kernel, at=at, chunk=chunk, tile=t...  8.21 us
    pallas_call x1, Pallas kernels, weight_call(): pl.pallas_call(functools.partial(weight_kernel, count=len(xs)), grid=(wid...  7.56 us
    unnamed x40, local copies, waits for them, and re-layouts  7.5 us
    pallas_call x1, Pallas kernels, words_call(): pl.pallas_call(functools.partial(words_kernel, width=width), in_specs=[pl...  6.19 us
  transfers between devices with their start and end apart: 13, of which 8 were waited for; matrix products, arithmetic and copies ran while one was open for 9% of the time, Pallas kernels for 18%

commit v1 on v0

--- a/solution.py
+++ b/solution.py
@@ -66,12 +66,14 @@
     )(at, ids, count)
 
 
-def score_kernel(*refs, at, chunk, tile):
+def score_kernel(*refs, at, parts, tile):
     count = len(at)
-    x_refs, words_ref = refs[:count], refs[count]
-    w_ref, bias_ref, prop_ref = refs[count + 1 : count + 4]
-    res_refs, post_ref = refs[count + 4 : 2 * count + 4], refs[2 * count + 4]
-    slots, sems = refs[2 * count + 5 : 3 * count + 5], refs[3 * count + 5]
+    x_refs, refs = refs[: sum(parts)], refs[sum(parts) :]
+    words_ref, w_ref, bias_ref, prop_ref = refs[:4]
+    res_refs, post_ref = refs[4 : count + 4], refs[count + 4]
+    slots, sems = refs[count + 5 : 2 * count + 5], refs[2 * count + 5]
+    starts = [sum(parts[:k]) for k in range(count)]
+    blocks = [x_refs[s : s + p] for s, p in zip(starts, parts)]
     copies = []
     for t in range(w_ref.shape[0] // tile):
         cols = slice(t * tile, (t + 1) * tile)
@@ -80,19 +82,18 @@
         rest = 1.0 - prop
         total = jnp.zeros((8, tile), F32)
         for k in range(count):
-            size = min(chunk, x_refs[k].shape[0])
-            for start in range(0, x_refs[k].shape[0], size):
-                rows = slice(start, start + size)
-                scores = mm(x_refs[k][rows, :], w_ref[cols, :], ((1,), (1,)))
-                grown = 1.0 + jnp.exp2(scores * -LOG2E + bias)
-                prob = 1.0 / grown
-                unseen = rest / (grown - prop)
-                words = words_ref[at[k] + start : at[k] + start + size, :]
-                bits = range(t * tile // LANES, (t + 1) * tile // LANES)
-                seen = jnp.concatenate([words & (1 << b) for b in bits], axis=1)
-                posterior = jnp.where(seen != 0, 1.0, unseen)
-                slots[k][t, rows, :] = (prob - posterior).astype(BF)
-                total = total + jnp.sum(posterior.reshape(size // 8, 8, tile), axis=0)
+            x = jnp.concatenate([x_ref[...] for x_ref in blocks[k]], axis=0)
+            size = x.shape[0]
+            scores = mm(x, w_ref[cols, :], ((1,), (1,)))
+            grown = 1.0 + jnp.exp2(scores * -LOG2E + bias)
+            prob = 1.0 / grown
+            unseen = rest / (grown - prop)
+            words = words_ref[at[k] : at[k] + size, :]
+            bits = range(t * tile // LANES, (t + 1) * tile // LANES)
+            seen = jnp.concatenate([words & (1 << b) for b in bits], axis=1)
+            posterior = jnp.where(seen != 0, 1.0, unseen)
+            slots[k][t] = (prob - posterior).astype(BF)
+            total = total + jnp.sum(posterior.reshape(size // 8, 8, tile), axis=0)
             copy = pltpu.make_async_copy(slots[k].at[t], res_refs[k].at[:, cols], sems.at[k, t])
             copy.start()
             copies.append(copy)
@@ -105,18 +106,21 @@
     return [pl.BlockSpec(memory_space=pltpu.VMEM)] * count
 
 
-def score_call(xs, at, words, w, bias, prop, chunk=256, tile=512):
+def score_call(groups, at, words, w, bias, prop, tile=512):
     width, depth = w.shape
-    rows = sum(x.shape[0] for x in xs)
+    xs = [x for group in groups for x in group]
+    sizes = [sum(x.shape[0] for x in group) for group in groups]
+    rows = sum(sizes)
     tiles = width // tile
+    parts = tuple(len(group) for group in groups)
     *res, post = pl.pallas_call(
-        functools.partial(score_kernel, at=at, chunk=chunk, tile=tile),
+        functools.partial(score_kernel, at=at, parts=parts, tile=tile),
         in_specs=in_vmem(len(xs) + 4),
-        out_specs=[pl.BlockSpec(memory_space=pltpu.HBM)] * len(xs) + in_vmem(1),
-        out_shape=[pltpu.HBM((x.shape[0], width), BF) for x in xs]
+        out_specs=[pl.BlockSpec(memory_space=pltpu.HBM)] * len(sizes) + in_vmem(1),
+        out_shape=[pltpu.HBM((size, width), BF) for size in sizes]
         + [jax.ShapeDtypeStruct((1, width), F32)],
-        scratch_shapes=[pltpu.VMEM((tiles, x.shape[0], tile), BF) for x in xs]
-        + [pltpu.SemaphoreType.DMA((len(xs), tiles))],
+        scratch_shapes=[pltpu.VMEM((tiles, size, tile), BF) for size in sizes]
+        + [pltpu.SemaphoreType.DMA((len(sizes), tiles))],
         cost_estimate=pl.CostEstimate(
             flops=2 * rows * width * depth,
             bytes_accessed=2 * (rows * depth + width * depth + rows * width),
@@ -129,8 +133,8 @@
 
 
 def weight_kernel(core_ref, *refs, count):
-    x_refs, r_refs = refs[:count], refs[count : 2 * count]
-    kept_ref, given_ref, x_all, r_all, out = refs[2 * count :]
+    x_refs, r_refs = refs[:count], refs[count:-5]
+    kept_ref, given_ref, x_all, r_all, out = refs[-5:]
     mine = core_ref[0]
 
     @pl.when(pl.program_id(0) == 0)
@@ -209,13 +213,12 @@
     words, obs = words_call(at, label_ids.T, label_count[None, :], width)
     prior = bin_prior(label_bins, prior_mean)
 
-    def brought(d):
-        return shift(own, "x", NX, -d)
-
-    front, back, far = brought(1), brought(3), brought(2)
-    (res0,), post0 = score_call((own,), (0,), words, class_weight, bias, prop)
+    half = block // 2
+    front, back = shift(own, "x", NX, -1), shift(own, "x", NX, 1)
+    far = (shift(front[:half], "x", NX, -1), shift(back[half:], "x", NX, 1))
+    (res0,), post0 = score_call(((own,),), (0,), words, class_weight, bias, prop)
     (res1, res3), post1 = score_call(
-        (front, back), (block, 3 * block), words, class_weight, bias, prop
+        ((front,), (back,)), (block, 3 * block), words, class_weight, bias, prop
     )
     far, post1 = lax.optimization_barrier((far, post1))
     (res2,), post2 = score_call((far,), (2 * block,), words, class_weight, bias, prop)
@@ -224,7 +227,7 @@
     sums = jnp.sum(exchange(jnp.tile(both, (NY * NC, 1, 1)), ("y", "core")), axis=0)
     updated = ((sums[0:1] + 8.0 * prior[None, :]) / (sums[1:2] + 8.0)).reshape(width)
 
-    kept_rows, given = weight_call(core[None], (own, front, far, back), (res0, res1, res2, res3))
+    kept_rows, given = weight_call(core[None], (own, front, *far, back), (res0, res1, res2, res3))
     pair = kept_rows.astype(F32) + shift(given, "core", NC, 1).astype(F32)
     pair = pair.astype(BF)
     pairs = [lax.dynamic_index_in_dim(pair, (y + d) % NY, 0, keepdims=False) for d in range(NY)]
@@ -234,17 +237,22 @@
     def term(r):
         return mm(r, scaled_weight, ((1,), (0,)))
 
-    moved = []
-    for d, r in ((2, res2), (1, res1), (3, res3)):
-        moved.append(shift(term(r).astype(BF), "x", NX, d).astype(F32))
+    send = lambda v, d: shift(v.astype(BF), "x", NX, d).astype(F32)
+    term2 = term(res2).astype(BF)
+    low2, high2 = send(term2[:half], 1), send(term2[half:], -1)
+    term1 = lax.optimization_barrier(term(res1))
+    term3 = lax.optimization_barrier(term(res3))
+    high1, low3 = send(term1[half:], 1), send(term3[:half], -1)
     kept = term(res0)
+    low1, high3 = send(term1[:half] + low2, 1), send(term3[half:] + high2, -1)
     kept, pairs = lax.optimization_barrier((kept, pairs))
     weight_sum = pairs[0].astype(F32)
     for d in (1, 2, 3):
         weight_sum = weight_sum + shift(pairs[d], "y", NY, d).astype(F32)
     weight_grad = (weight_sum / updated[None, :]).astype(BF).T
 
-    parts = exchange((kept + moved[0] + moved[1] + moved[2]).astype(BF), "z")
+    low, high = kept[:half] + low1 + low3, kept[half:] + high1 + high3
+    parts = exchange(jnp.concatenate([low, high], axis=0).astype(BF), "z")
     embed_grad = jnp.sum(parts.reshape(NZ, part, depth).astype(F32), axis=0).astype(BF)
     return updated, weight_grad, embed_grad
 

time: 111 us -> 113 us (1.018)
  starting transfers between devices: 29.7 us -> 36.4 us
  waiting for transfers between devices: 36 us -> 31.3 us
    ppermute x10 -> x14, starting transfers between devices: 13 us -> 19.7 us  [shift(): return lax.ppermute(v, axis, ring(n, d))]
    ppermute x10 -> x14, waiting for transfers between devices: 20.1 us -> 16.6 us  [shift(): return lax.ppermute(v, axis, ring(n, d))]
    all_to_all x3, waiting for transfers between devices: 16 us -> 14.7 us  [exchange(): return lax.all_to_all(v, axis, split_axis=0, concat_axis=0, tiled=True)]
    unnamed x40 -> x38, local copies, waits for them, and re-layouts: 7.5 us -> 7.44 us
  transfers between devices with their start and end apart: 13 -> 17, of which waited for: 8 -> 5; matrix products, arithmetic and copies ran while one was open for 9% -> 9% of each run, Pallas kernels for 18% -> 18%
where the time goes in v1:
time: 113 us; the launch traced here: 111 us
  starting transfers between devices  36.4 us (32%)
  waiting for transfers between devices  31.3 us (28%)
  Pallas kernels  22 us (19%)
  local copies, waits for them, and re-layouts  9.92 us (9%)
  other arithmetic  6.32 us (6%)
  matrix products  3.91 us (3%)
    ppermute x14, starting transfers between devices, shift(): return lax.ppermute(v, axis, ring(n, d))  19.7 us
    all_to_all x3, starting transfers between devices, exchange(): return lax.all_to_all(v, axis, split_axis=0, concat_axis=0, tiled=True)  16.7 us
    ppermute x14, waiting for transfers between devices, shift(): return lax.ppermute(v, axis, ring(n, d))  16.6 us
    all_to_all x3, waiting for transfers between devices, exchange(): return lax.all_to_all(v, axis, split_axis=0, concat_axis=0, tiled=True)  14.7 us
    pallas_call x3, Pallas kernels, score_call(): pl.pallas_call(functools.partial(score_kernel, at=at, parts=parts, tile=t...  8.22 us
    pallas_call x1, Pallas kernels, weight_call(): pl.pallas_call(functools.partial(weight_kernel, count=len(xs)), grid=(wid...  7.56 us
    unnamed x38, local copies, waits for them, and re-layouts  7.44 us
    pallas_call x1, Pallas kernels, words_call(): pl.pallas_call(functools.partial(words_kernel, width=width), in_specs=[pl...  6.19 us
  transfers between devices with their start and end apart: 17, of which 5 were waited for; matrix products, arithmetic and copies ran while one was open for 9% of the time, Pallas kernels for 18%

profile of v1, /device:TPU:16, one launch (start us, length us, event | category | flops | bytes accessed | tf_op | source)
XLA Modules:
  0.0 110.9 jit_solution(14509545247295680817)
XLA Ops:
  0.6 1.6 %tile.4 = bf16[8,32,768]{2,1,0:T(8,128)(2,1)} broadcast(bf16[32,768]{1,0:T(8,128)(2,1)} %param.8), dimensions={1,2} | broadcast | bytes 442368 | tf_op jit(solution)/shard_map/tile | solution.py:211
  2.2 8.5 %all-to-all-start = ((bf16[8,32,768]{2,1,0:T(8,128)(2,1)}), bf16[8,32,768]{2,1,0:T(8,128)(2,1)S(1)}, u32[]{:S(2)}, u32[]{:S(2)}) async-start(bf16[8,32,768]{2,1,0:T(8,128)(2,1)} %tile.4), calls=%async_computation | async-start | bytes 786432 | tf_op jit(solution)/shard_map/all_to_all | solution.py:198
  10.7 14.7 %all-to-all-done = bf16[8,32,768]{2,1,0:T(8,128)(2,1)S(1)} async-done(((bf16[8,32,768]{2,1,0:T(8,128)(2,1)}), bf16[8,32,768]{2,1,0:T(8,128)(2,1)S(1)}, u32[]{:S(2)}, u32[]{:S(2)}) %all-to-all-start) | async-done | bytes 393248 | tf_op jit(solution)/shard_map/all_to_all | solution.py:198
  25.4 1.5 %collective-permute-start.2 = (bf16[256,768]{1,0:T(8,128)(2,1)S(1)}, bf16[256,768]{1,0:T(8,128)(2,1)S(1)}, u32[]{:S(2)}, u32[]{:S(2)}) collective-permute-start(bf16[256,768]{1,0:T(8,128)(2,1)S(1)} %bitcast.29), channel_id=1, source_target_pairs={{0,8},{8,16},{16,24},{24,0},{1,9},{9,17},{17,25},{25,1},{2,10},{10... | collective-permute-start | bytes 1179656 | tf_op jit(solution)/shard_map/ppermute | solution.py:194
  26.8 1.7 %collective-permute-start = (bf16[256,768]{1,0:T(8,128)(2,1)S(1)}, bf16[256,768]{1,0:T(8,128)(2,1)S(1)}, u32[]{:S(2)}, u32[]{:S(2)}) collective-permute-start(bf16[256,768]{1,0:T(8,128)(2,1)S(1)} %bitcast.30), channel_id=1, source_target_pairs={{0,24},{8,0},{16,8},{24,16},{1,25},{9,1},{17,9},{25,17},{2,26},{10... | collective-permute-start | bytes 1179656 | tf_op jit(solution)/shard_map/ppermute | solution.py:194
  30.3 6.2 %words.1 = (s32[1024,128]{1,0:T(8,128)S(1)}, f32[1,2048]{1,0:T(1,128)S(1)}) custom-call(s32[2]{0:T(128)S(1)} %pad_add_fusion.at_ref, s32[32,1024]{1,0:T(8,128)S(1)} %bitcast.33, s32[1,1024]{1,0:T(1,128)S(1)} %bitcast.40), custom_call_target="tpu_custom_call" | custom-call | flops 26214400 | bytes 1048576 | tf_op jit(solution)/shard_map/words/pallas_call | solution.py:53
  38.5 3.0 %collective-permute-start.1 = (bf16[128,768]{1,0:T(8,128)(2,1)S(1)}, bf16[128,768]{1,0:T(8,128)(2,1)S(1)}, u32[]{:S(2)}, u32[]{:S(2)}) collective-permute-start(bf16[128,768]{1,0:T(8,128)(2,1)S(1)} %slice.50), channel_id=1, source_target_pairs={{0,24},{8,0},{16,8},{24,16},{1,25},{9,1},{17,9},{25,17},{2,26},{10... | collective-permute-start | bytes 589832 | tf_op jit(solution)/shard_map/ppermute | solution.py:194
  41.4 1.9 %copy-done = bf16[2048,768]{1,0:T(8,128)(2,1)S(1)} copy-done((bf16[2048,768]{1,0:T(8,128)(2,1)S(1)}, bf16[2048,768]{1,0:T(8,128)(2,1)}, u32[]{:S(2)}) %copy-start) | copy-done | bytes 3145752
  44.7 2.3 %scores.3 = (bf16[256,2048]{1,0:T(8,128)(2,1)}, f32[1,2048]{1,0:T(1,128)S(1)}) custom-call(bf16[256,768]{1,0:T(8,128)(2,1)S(1)} %bitcast.31, s32[1024,128]{1,0:T(8,128)S(1)} %get-tuple-element.23.refs_1_.refs_2_, bf16[2048,768]{1,0:T(8,128)(2,1)S(1)} %copy-done, f32[1,2048]{1,0:T(1,128)S(1)} %bitcast.34, f32[1,2048]{1,0:T(1,128)S(1)} %bitcast.37), custom_call_target="tpu_custom_call" | custom-call | flops 805306368 | bytes 4587520 | tf_op jit(solution)/shard_map/scores/pallas_call | solution.py:116
  48.0 3.6 %scores.4 = (bf16[256,2048]{1,0:T(8,128)(2,1)}, bf16[256,2048]{1,0:T(8,128)(2,1)}, f32[1,2048]{1,0:T(1,128)S(1)}) custom-call(bf16[256,768]{1,0:T(8,128)(2,1)S(1)} %copy-done.9, bf16[256,768]{1,0:T(8,128)(2,1)S(1)} %copy-done.7, s32[1024,128]{1,0:T(8,128)S(1)} %get-tuple-element.23.refs_1_.refs_2_, bf16[2048,768]{1,0:T(8,128)(2,1)S(1)} %copy-done, ...), custom_call_target="tpu_custom_call" | custom-call | flops 1610612736 | bytes 6029312 | tf_op jit(solution)/shard_map/scores/pallas_call | solution.py:116
  51.7 2.3 %scores.5 = (bf16[256,2048]{1,0:T(8,128)(2,1)}, f32[1,2048]{1,0:T(1,128)S(1)}) custom-call(bf16[128,768]{1,0:T(8,128)(2,1)S(1)} %collective-permute-done.1.refs_0_.refs_2_, bf16[128,768]{1,0:T(8,128)(2,1)S(1)} %collective-permute-done.3.refs_1_.refs_3_, s32[1024,128]{1,0:T(8,128)S(1)} %get-tuple-element.23.refs_1_.refs_2_, bf16[2048,768]{1,0:T(8,128)(2,1)S(1)} %copy-done.1, ...), custom_call_target="tpu_custom_call" | custom-call | flops 805306368 | bytes 4587520 | tf_op jit(solution)/shard_map/scores/pallas_call | solution.py:116
  54.8 4.8 %all-to-all-start.1 = ((f32[8,2,2048]{2,1,0:T(2,128)}), f32[8,2,2048]{2,1,0:T(2,128)S(1)}, u32[]{:S(2)}, u32[]{:S(2)}) async-start(f32[8,2,2048]{2,1,0:T(2,128)} %tile.5), calls=%async_computation.1 | async-start | bytes 262144 | tf_op jit(solution)/shard_map/all_to_all | solution.py:198
  59.6 7.6 %weights.1 = (bf16[4,96,2048]{2,1,0:T(8,128)(2,1)}, bf16[4,96,2048]{2,1,0:T(8,128)(2,1)}) custom-call(s32[1]{0:T(128)} %bitcast.9.core_ref, bf16[256,768]{1,0:T(8,128)(2,1)} %bitcast.32, bf16[256,768]{1,0:T(8,128)(2,1)} %copy-done.8, bf16[128,768]{1,0:T(8,128)(2,1)} %copy-done.4, bf16[128,768]{1,0:T(8,128)(2,1)} %copy-done.3, bf16[256,768]{1,0:T(8,128)(2,1)} %copy-done.6, ...), custom_call_target="tpu_custom_call" | custom-call | flops 3221225472 | bytes 8912896 | tf_op jit(solution)/shard_map/weights/pallas_call | solution.py:164
  71.0 3.2 %collective-permute-start.10 = (bf16[128,768]{1,0:T(8,128)(2,1)S(1)}, bf16[128,768]{1,0:T(8,128)(2,1)S(1)}, u32[]{:S(2)}, u32[]{:S(2)}) collective-permute-start(bf16[128,768]{1,0:T(8,128)(2,1)S(1)} %slice.77), channel_id=1, source_target_pairs={{0,24},{8,0},{16,8},{24,16},{1,25},{9,1},{17,9},{25,17},{2,26},{10... | collective-permute-start | bytes 589832 | tf_op jit(solution)/shard_map/ppermute | solution.py:194
  75.5 3.2 %collective-permute-start.12 = (bf16[128,768]{1,0:T(8,128)(2,1)S(1)}, bf16[128,768]{1,0:T(8,128)(2,1)S(1)}, u32[]{:S(2)}, u32[]{:S(2)}) collective-permute-start(bf16[128,768]{1,0:T(8,128)(2,1)S(1)} %get-tuple-element.48), channel_id=1, source_target_pairs={{0,24},{8,0},{16,8},{24,16},{1,25},{9,1},{17,9},{25,17},{2,26},{10... | collective-permute-start | bytes 589832 | tf_op jit(solution)/shard_map/ppermute | solution.py:194
  79.7 3.8 %collective-permute-done.8 = bf16[128,768]{1,0:T(8,128)(2,1)S(1)} collective-permute-done((bf16[128,768]{1,0:T(8,128)(2,1)S(1)}, bf16[128,768]{1,0:T(8,128)(2,1)S(1)}, u32[]{:S(2)}, u32[]{:S(2)}) %collective-permute-start.8) | collective-permute-done | bytes 196640 | tf_op jit(solution)/shard_map/ppermute | solution.py:194
  83.8 3.3 %collective-permute-start.13 = (bf16[128,768]{1,0:T(8,128)(2,1)S(1)}, bf16[128,768]{1,0:T(8,128)(2,1)S(1)}, u32[]{:S(2)}, u32[]{:S(2)}) collective-permute-start(bf16[128,768]{1,0:T(8,128)(2,1)S(1)} %fusion), channel_id=1, source_target_pairs={{0,24},{8,0},{16,8},{24,16},{1,25},{9,1},{17,9},{25,17},{2,26},{10... | collective-permute-start | bytes 589832 | tf_op jit(solution)/shard_map/ppermute | solution.py:194
  87.1 2.0 %add_convert_fusion = bf16[4,96,2048]{2,1,0:T(8,128)(2,1)S(1)} fusion(bf16[4,96,2048]{2,1,0:T(8,128)(2,1)} %collective-permute-done.4, bf16[4,96,2048]{2,1,0:T(8,128)(2,1)S(1)} %copy-done.13), kind=kLoop, calls=%fused_computation.1 | loop fusion | flops 3145728 | bytes 4718592 | tf_op jit(solution)/shard_map/convert_element_type | solution.py:232
  89.2 1.3 %collective-permute-start.5 = (bf16[96,2048]{1,0:T(8,128)(2,1)S(1)}, bf16[96,2048]{1,0:T(8,128)(2,1)S(1)}, u32[]{:S(2)}, u32[]{:S(2)}) collective-permute-start(bf16[96,2048]{1,0:T(8,128)(2,1)S(1)} %get-tuple-element.37), channel_id=1, source_target_pairs={{0,64},{64,128},{128,192},{192,0},{1,65},{65,129},{129,193},{193,1... | collective-permute-start | bytes 1179656 | tf_op jit(solution)/shard_map/ppermute | solution.py:194
  93.0 3.5 %all-to-all-start.2 = ((bf16[8,32,768]{2,1,0:T(8,128)(2,1)}), bf16[8,32,768]{2,1,0:T(8,128)(2,1)S(1)}, u32[]{:S(2)}, u32[]{:S(2)}) async-start(bf16[8,32,768]{2,1,0:T(8,128)(2,1)} %bitcast.15), calls=%async_computation.2 | async-start | bytes 786432 | tf_op jit(solution)/shard_map/all_to_all | solution.py:198
  96.4 4.9 %collective-permute-done.5 = bf16[96,2048]{1,0:T(8,128)(2,1)S(1)} collective-permute-done((bf16[96,2048]{1,0:T(8,128)(2,1)S(1)}, bf16[96,2048]{1,0:T(8,128)(2,1)S(1)}, u32[]{:S(2)}, u32[]{:S(2)}) %collective-permute-start.5) | collective-permute-done | bytes 393248 | tf_op jit(solution)/shard_map/ppermute | solution.py:194
  101.3 6.1 %collective-permute-done.6 = bf16[96,2048]{1,0:T(8,128)(2,1)S(1)} collective-permute-done((bf16[96,2048]{1,0:T(8,128)(2,1)S(1)}, bf16[96,2048]{1,0:T(8,128)(2,1)S(1)}, u32[]{:S(2)}, u32[]{:S(2)}) %collective-permute-start.6) | collective-permute-done | bytes 393248 | tf_op jit(solution)/shard_map/ppermute | solution.py:194
  107.3 1.8 %collective-permute-done.7 = bf16[96,2048]{1,0:T(8,128)(2,1)S(1)} collective-permute-done((bf16[96,2048]{1,0:T(8,128)(2,1)S(1)}, bf16[96,2048]{1,0:T(8,128)(2,1)S(1)}, u32[]{:S(2)}, u32[]{:S(2)}) %collective-permute-start.7) | collective-permute-done | bytes 393248 | tf_op jit(solution)/shard_map/ppermute | solution.py:194
  109.2 1.0 fusion.2
  (80 shorter events, 16.2 us)
Async XLA Ops:
  2.2 23.2 %all-to-all-start = ((bf16[8,32,768]{2,1,0:T(8,128)(2,1)}), bf16[8,32,768]{2,1,0:T(8,128)(2,1)S(1)}, u32[]{:S(2)}, u32[]{:S(2)}) async-start(bf16[8,32,768]{2,1,0:T(8,128)(2,1)} %tile.4), calls=%async_computation | async-start | bytes 786432 | tf_op jit(solution)/shard_map/all_to_all | solution.py:198
  25.4 26.3 %copy-start.2 = (bf16[8,32,768]{2,1,0:T(8,128)(2,1)}, bf16[8,32,768]{2,1,0:T(8,128)(2,1)S(1)}, u32[]{:S(2)}) copy-start(bf16[8,32,768]{2,1,0:T(8,128)(2,1)S(1)} %all-to-all-done) | copy-start | bytes 1179652
  25.4 11.9 %collective-permute-start.2 = (bf16[256,768]{1,0:T(8,128)(2,1)S(1)}, bf16[256,768]{1,0:T(8,128)(2,1)S(1)}, u32[]{:S(2)}, u32[]{:S(2)}) collective-permute-start(bf16[256,768]{1,0:T(8,128)(2,1)S(1)} %bitcast.29), channel_id=1, source_target_pairs={{0,8},{8,16},{16,24},{24,0},{1,9},{9,17},{17,25},{25,1},{2,10},{10... | collective-permute-start | bytes 1179656 | tf_op jit(solution)/shard_map/ppermute | solution.py:194
  26.8 10.8 %collective-permute-start = (bf16[256,768]{1,0:T(8,128)(2,1)S(1)}, bf16[256,768]{1,0:T(8,128)(2,1)S(1)}, u32[]{:S(2)}, u32[]{:S(2)}) collective-permute-start(bf16[256,768]{1,0:T(8,128)(2,1)S(1)} %bitcast.30), channel_id=1, source_target_pairs={{0,24},{8,0},{16,8},{24,16},{1,25},{9,1},{17,9},{25,17},{2,26},{10... | collective-permute-start | bytes 1179656 | tf_op jit(solution)/shard_map/ppermute | solution.py:194
  37.3 4.1 %copy-start.6 = (bf16[256,768]{1,0:T(8,128)(2,1)}, bf16[256,768]{1,0:T(8,128)(2,1)S(1)}, u32[]{:S(2)}) copy-start(bf16[256,768]{1,0:T(8,128)(2,1)S(1)} %collective-permute-done.2.refs_1_.refs_4_) | copy-start | bytes 1179652
  37.3 14.3 %collective-permute-start.3 = (bf16[128,768]{1,0:T(8,128)(2,1)S(1)}, bf16[128,768]{1,0:T(8,128)(2,1)S(1)}, u32[]{:S(2)}, u32[]{:S(2)}) collective-permute-start(bf16[128,768]{1,0:T(8,128)(2,1)S(1)} %slice.51), channel_id=1, source_target_pairs={{0,8},{8,16},{16,24},{24,0},{1,9},{9,17},{17,25},{25,1},{2,10},{10... | collective-permute-start | bytes 589832 | tf_op jit(solution)/shard_map/ppermute | solution.py:194
  38.5 13.2 %collective-permute-start.1 = (bf16[128,768]{1,0:T(8,128)(2,1)S(1)}, bf16[128,768]{1,0:T(8,128)(2,1)S(1)}, u32[]{:S(2)}, u32[]{:S(2)}) collective-permute-start(bf16[128,768]{1,0:T(8,128)(2,1)S(1)} %slice.50), channel_id=1, source_target_pairs={{0,24},{8,0},{16,8},{24,16},{1,25},{9,1},{17,9},{25,17},{2,26},{10... | collective-permute-start | bytes 589832 | tf_op jit(solution)/shard_map/ppermute | solution.py:194
  48.0 3.7 %copy-start.1 = (bf16[2048,768]{1,0:T(8,128)(2,1)S(1)}, bf16[2048,768]{1,0:T(8,128)(2,1)}, u32[]{:S(2)}) copy-start(bf16[2048,768]{1,0:T(8,128)(2,1)} %refs_3_.3) | copy-start | bytes 9437188
  54.8 12.5 %all-to-all-start.1 = ((f32[8,2,2048]{2,1,0:T(2,128)}), f32[8,2,2048]{2,1,0:T(2,128)S(1)}, u32[]{:S(2)}, u32[]{:S(2)}) async-start(f32[8,2,2048]{2,1,0:T(2,128)} %tile.5), calls=%async_computation.1 | async-start | bytes 262144 | tf_op jit(solution)/shard_map/all_to_all | solution.py:198
  67.1 19.9 %collective-permute-start.4 = (bf16[4,96,2048]{2,1,0:T(8,128)(2,1)}, bf16[4,96,2048]{2,1,0:T(8,128)(2,1)}, u32[]{:S(2)}, u32[]{:S(2)}) collective-permute-start(bf16[4,96,2048]{2,1,0:T(8,128)(2,1)} %get-tuple-element.35), channel_id=1, source_target_pairs={{0,32},{32,0},{1,33},{33,1},{2,34},{34,2},{3,35},{35,3},{4,36},{36... | collective-permute-start | bytes 4718600 | tf_op jit(solution)/shard_map/ppermute | solution.py:194
  67.3 41.8 %copy-start.14 = (f32[1,2048]{1,0:T(1,128)}, f32[1,2048]{1,0:T(1,128)S(1)}, u32[]{:S(2)}) copy-start(f32[1,2048]{1,0:T(1,128)S(1)} %fusion.3) | copy-start | bytes 24580
  69.8 4.4 %copy-start.16 = (bf16[256,2048]{1,0:T(8,128)(2,1)S(1)}, bf16[256,2048]{1,0:T(8,128)(2,1)}, u32[]{:S(2)}) copy-start(bf16[256,2048]{1,0:T(8,128)(2,1)} %get-tuple-element.32.refs_7_) | copy-start | bytes 3145732
  70.9 7.9 %copy-start.15 = (bf16[256,2048]{1,0:T(8,128)(2,1)S(1)}, bf16[256,2048]{1,0:T(8,128)(2,1)}, u32[]{:S(2)}) copy-start(bf16[256,2048]{1,0:T(8,128)(2,1)} %get-tuple-element.30.refs_5_) | copy-start | bytes 3145732
  70.9 19.6 %collective-permute-start.11 = (bf16[128,768]{1,0:T(8,128)(2,1)S(1)}, bf16[128,768]{1,0:T(8,128)(2,1)S(1)}, u32[]{:S(2)}, u32[]{:S(2)}) collective-permute-start(bf16[128,768]{1,0:T(8,128)(2,1)S(1)} %slice.76), channel_id=1, source_target_pairs={{0,8},{8,16},{16,24},{24,0},{1,9},{9,17},{17,25},{25,1},{2,10},{10... | collective-permute-start | bytes 589832 | tf_op jit(solution)/shard_map/ppermute | solution.py:194
  71.0 20.3 %collective-permute-start.10 = (bf16[128,768]{1,0:T(8,128)(2,1)S(1)}, bf16[128,768]{1,0:T(8,128)(2,1)S(1)}, u32[]{:S(2)}, u32[]{:S(2)}) collective-permute-start(bf16[128,768]{1,0:T(8,128)(2,1)S(1)} %slice.77), channel_id=1, source_target_pairs={{0,24},{8,0},{16,8},{24,16},{1,25},{9,1},{17,9},{25,17},{2,26},{10... | collective-permute-start | bytes 589832 | tf_op jit(solution)/shard_map/ppermute | solution.py:194
  75.2 8.4 %collective-permute-start.8 = (bf16[128,768]{1,0:T(8,128)(2,1)S(1)}, bf16[128,768]{1,0:T(8,128)(2,1)S(1)}, u32[]{:S(2)}, u32[]{:S(2)}) collective-permute-start(bf16[128,768]{1,0:T(8,128)(2,1)S(1)} %get-tuple-element.47), channel_id=1, source_target_pairs={{0,8},{8,16},{16,24},{24,0},{1,9},{9,17},{17,25},{25,1},{2,10},{10... | collective-permute-start | bytes 589832 | tf_op jit(solution)/shard_map/ppermute | solution.py:194
  75.5 11.5 %copy-start.13 = (bf16[4,96,2048]{2,1,0:T(8,128)(2,1)S(1)}, bf16[4,96,2048]{2,1,0:T(8,128)(2,1)}, u32[]{:S(2)}) copy-start(bf16[4,96,2048]{2,1,0:T(8,128)(2,1)} %get-tuple-element.34) | copy-start | bytes 4718596
  75.5 8.2 %collective-permute-start.12 = (bf16[128,768]{1,0:T(8,128)(2,1)S(1)}, bf16[128,768]{1,0:T(8,128)(2,1)S(1)}, u32[]{:S(2)}, u32[]{:S(2)}) collective-permute-start(bf16[128,768]{1,0:T(8,128)(2,1)S(1)} %get-tuple-element.48), channel_id=1, source_target_pairs={{0,24},{8,0},{16,8},{24,16},{1,25},{9,1},{17,9},{25,17},{2,26},{10... | collective-permute-start | bytes 589832 | tf_op jit(solution)/shard_map/ppermute | solution.py:194
  83.6 8.4 %collective-permute-start.9 = (bf16[128,768]{1,0:T(8,128)(2,1)S(1)}, bf16[128,768]{1,0:T(8,128)(2,1)S(1)}, u32[]{:S(2)}, u32[]{:S(2)}) collective-permute-start(bf16[128,768]{1,0:T(8,128)(2,1)S(1)} %fusion.1), channel_id=1, source_target_pairs={{0,8},{8,16},{16,24},{24,0},{1,9},{9,17},{17,25},{25,1},{2,10},{10... | collective-permute-start | bytes 589832 | tf_op jit(solution)/shard_map/ppermute | solution.py:194
  83.8 8.3 %collective-permute-start.13 = (bf16[128,768]{1,0:T(8,128)(2,1)S(1)}, bf16[128,768]{1,0:T(8,128)(2,1)S(1)}, u32[]{:S(2)}, u32[]{:S(2)}) collective-permute-start(bf16[128,768]{1,0:T(8,128)(2,1)S(1)} %fusion), channel_id=1, source_target_pairs={{0,24},{8,0},{16,8},{24,16},{1,25},{9,1},{17,9},{25,17},{2,26},{10... | collective-permute-start | bytes 589832 | tf_op jit(solution)/shard_map/ppermute | solution.py:194
  89.2 12.1 %collective-permute-start.5 = (bf16[96,2048]{1,0:T(8,128)(2,1)S(1)}, bf16[96,2048]{1,0:T(8,128)(2,1)S(1)}, u32[]{:S(2)}, u32[]{:S(2)}) collective-permute-start(bf16[96,2048]{1,0:T(8,128)(2,1)S(1)} %get-tuple-element.37), channel_id=1, source_target_pairs={{0,64},{64,128},{128,192},{192,0},{1,65},{65,129},{129,193},{193,1... | collective-permute-start | bytes 1179656 | tf_op jit(solution)/shard_map/ppermute | solution.py:194
  90.5 16.9 %collective-permute-start.6 = (bf16[96,2048]{1,0:T(8,128)(2,1)S(1)}, bf16[96,2048]{1,0:T(8,128)(2,1)S(1)}, u32[]{:S(2)}, u32[]{:S(2)}) collective-permute-start(bf16[96,2048]{1,0:T(8,128)(2,1)S(1)} %get-tuple-element.38), channel_id=1, source_target_pairs={{0,128},{64,192},{128,0},{192,64},{1,129},{65,193},{129,1},{193,65... | collective-permute-start | bytes 1179656 | tf_op jit(solution)/shard_map/ppermute | solution.py:194
  91.3 17.9 %collective-permute-start.7 = (bf16[96,2048]{1,0:T(8,128)(2,1)S(1)}, bf16[96,2048]{1,0:T(8,128)(2,1)S(1)}, u32[]{:S(2)}, u32[]{:S(2)}) collective-permute-start(bf16[96,2048]{1,0:T(8,128)(2,1)S(1)} %get-tuple-element.39), channel_id=1, source_target_pairs={{0,192},{64,0},{128,64},{192,128},{1,193},{65,1},{129,65},{193,129... | collective-permute-start | bytes 1179656 | tf_op jit(solution)/shard_map/ppermute | solution.py:194
  93.0 17.2 %all-to-all-start.2 = ((bf16[8,32,768]{2,1,0:T(8,128)(2,1)}), bf16[8,32,768]{2,1,0:T(8,128)(2,1)S(1)}, u32[]{:S(2)}, u32[]{:S(2)}) async-start(bf16[8,32,768]{2,1,0:T(8,128)(2,1)} %bitcast.15), calls=%async_computation.2 | async-start | bytes 786432 | tf_op jit(solution)/shard_map/all_to_all | solution.py:198
  (12 other events, 16.1 us)

commit v2 on v1

--- a/solution.py
+++ b/solution.py
@@ -22,8 +22,18 @@
     return lax.dot_general(a, b, (dims, ((), ())), preferred_element_type=F32)
 
 
-def words_kernel(at_ref, ids_ref, count_ref, words_ref, obs_ref, *, width):
+def words_kernel(
+    at_ref, mean_ref, ids_ref, count_ref, bias_ref, prop_ref, bins_ref, words_ref, obs_ref, label_ref
+):
     slots, rows = ids_ref.shape
+    width = bias_ref.shape[1]
+    label_ref[0:1, :] = bias_ref[...] * -LOG2E
+    label_ref[1:2, :] = prop_ref[...]
+    bins = bins_ref[...]
+    prior = jnp.zeros((1, width), F32)
+    for b in range(mean_ref.shape[0]):
+        prior = prior + jnp.where(bins == b, mean_ref[b], 0.0)
+    label_ref[2:3, :] = 8.0 * prior
     lanes = lax.broadcasted_iota(jnp.int32, (LANES, LANES), 1)
     slot = lax.broadcasted_iota(jnp.int32, (slots, LANES), 0)
     counts = [jnp.zeros((8, LANES), jnp.int32) for _ in range(width // LANES)]
@@ -48,57 +58,81 @@
         )
 
 
-def words_call(at, ids, count, width):
-    rows = ids.shape[1]
+def words_call(at, mean, ids, count, bias, prop, bins):
+    rows, width = ids.shape[1], bias.shape[1]
     return pl.pallas_call(
-        functools.partial(words_kernel, width=width),
-        in_specs=[pl.BlockSpec(memory_space=pltpu.SMEM)] + in_vmem(2),
-        out_specs=in_vmem(2),
+        words_kernel,
+        in_specs=[pl.BlockSpec(memory_space=pltpu.SMEM)] * 2 + in_vmem(5),
+        out_specs=in_vmem(3),
         out_shape=[
             jax.ShapeDtypeStruct((rows, LANES), jnp.int32),
             jax.ShapeDtypeStruct((1, width), F32),
+            jax.ShapeDtypeStruct((3, width), F32),
         ],
         cost_estimate=pl.CostEstimate(
             flops=200 * rows * LANES, bytes_accessed=8 * rows * LANES, transcendentals=0
         ),
         compiler_params=pltpu.CompilerParams(vmem_limit_bytes=16 << 20),
         name="words",
-    )(at, ids, count)
-
-
-def score_kernel(*refs, at, parts, tile):
+    )(at, mean, ids, count, bias, prop, bins)
+
+
+def score_kernel(*refs, at, parts, sizes, tile):
     count = len(at)
     x_refs, refs = refs[: sum(parts)], refs[sum(parts) :]
-    words_ref, w_ref, bias_ref, prop_ref = refs[:4]
-    res_refs, post_ref = refs[4 : count + 4], refs[count + 4]
-    slots, sems = refs[count + 5 : 2 * count + 5], refs[2 * count + 5]
-    starts = [sum(parts[:k]) for k in range(count)]
-    blocks = [x_refs[s : s + p] for s, p in zip(starts, parts)]
-    copies = []
-    for t in range(w_ref.shape[0] // tile):
+    words_ref, w_ref, label_ref = refs[:3]
+    res_refs, post_ref, refs = refs[3 : count + 3], refs[count + 3], refs[count + 4 :]
+    x_in, words_in, slots = refs[:count], refs[count : 2 * count], refs[2 * count : 3 * count]
+    w_in, label_in, x_sems, words_sems, w_sems, label_sem, out_sems = refs[3 * count :]
+    tiles = w_ref.shape[0] // tile
+
+    first = []
+    n = 0
+    for k in range(count):
+        low = 0
+        for _ in range(parts[k]):
+            size = x_refs[n].shape[0]
+            target = x_in[k].at[low : low + size, :]
+            first.append(pltpu.make_async_copy(x_refs[n], target, x_sems.at[n]))
+            low, n = low + size, n + 1
+        source = words_ref.at[at[k] : at[k] + sizes[k], :]
+        first.append(pltpu.make_async_copy(source, words_in[k], words_sems.at[k]))
+    first.append(pltpu.make_async_copy(label_ref, label_in, label_sem))
+    weights = [
+        pltpu.make_async_copy(w_ref.at[t * tile : (t + 1) * tile, :], w_in.at[t], w_sems.at[t])
+        for t in range(tiles)
+    ]
+    for copy in first + weights:
+        copy.start()
+    for copy in first:
+        copy.wait()
+
+    outs = []
+    for t in range(tiles):
+        weights[t].wait()
         cols = slice(t * tile, (t + 1) * tile)
-        bias = bias_ref[:, cols] * -LOG2E
-        prop = prop_ref[:, cols]
+        bias, prop = label_in[0:1, cols], label_in[1:2, cols]
         rest = 1.0 - prop
         total = jnp.zeros((8, tile), F32)
         for k in range(count):
-            x = jnp.concatenate([x_ref[...] for x_ref in blocks[k]], axis=0)
-            size = x.shape[0]
-            scores = mm(x, w_ref[cols, :], ((1,), (1,)))
+            size = sizes[k]
+            scores = mm(x_in[k][...], w_in[t], ((1,), (1,)))
             grown = 1.0 + jnp.exp2(scores * -LOG2E + bias)
             prob = 1.0 / grown
             unseen = rest / (grown - prop)
-            words = words_ref[at[k] : at[k] + size, :]
+            words = words_in[k][...]
             bits = range(t * tile // LANES, (t + 1) * tile // LANES)
             seen = jnp.concatenate([words & (1 << b) for b in bits], axis=1)
             posterior = jnp.where(seen != 0, 1.0, unseen)
             slots[k][t] = (prob - posterior).astype(BF)
             total = total + jnp.sum(posterior.reshape(size // 8, 8, tile), axis=0)
-            copy = pltpu.make_async_copy(slots[k].at[t], res_refs[k].at[:, cols], sems.at[k, t])
+            copy = pltpu.make_async_copy(
+                slots[k].at[t], res_refs[k].at[:, cols], out_sems.at[k, t]
+            )
             copy.start()
-            copies.append(copy)
+            outs.append(copy)
         post_ref[:, cols] = jnp.sum(total, axis=0, keepdims=True)
-    for copy in copies:
+    for copy in outs:
         copy.wait()
 
 
@@ -106,29 +140,33 @@
     return [pl.BlockSpec(memory_space=pltpu.VMEM)] * count
 
 
-def score_call(groups, at, words, w, bias, prop, tile=512):
+def score_call(groups, at, words, w, label, tile=512):
     width, depth = w.shape
     xs = [x for group in groups for x in group]
-    sizes = [sum(x.shape[0] for x in group) for group in groups]
+    sizes = tuple(sum(x.shape[0] for x in group) for group in groups)
     rows = sum(sizes)
-    tiles = width // tile
+    tiles, count = width // tile, len(sizes)
     parts = tuple(len(group) for group in groups)
+    dma = pltpu.SemaphoreType.DMA
     *res, post = pl.pallas_call(
-        functools.partial(score_kernel, at=at, parts=parts, tile=tile),
-        in_specs=in_vmem(len(xs) + 4),
-        out_specs=[pl.BlockSpec(memory_space=pltpu.HBM)] * len(sizes) + in_vmem(1),
+        functools.partial(score_kernel, at=at, parts=parts, sizes=sizes, tile=tile),
+        in_specs=[pl.BlockSpec(memory_space=pl.ANY)] * (len(xs) + 3),
+        out_specs=[pl.BlockSpec(memory_space=pltpu.HBM)] * count + in_vmem(1),
         out_shape=[pltpu.HBM((size, width), BF) for size in sizes]
         + [jax.ShapeDtypeStruct((1, width), F32)],
-        scratch_shapes=[pltpu.VMEM((tiles, size, tile), BF) for size in sizes]
-        + [pltpu.SemaphoreType.DMA((len(sizes), tiles))],
+        scratch_shapes=[pltpu.VMEM((size, depth), BF) for size in sizes]
+        + [pltpu.VMEM((size, LANES), jnp.int32) for size in sizes]
+        + [pltpu.VMEM((tiles, size, tile), BF) for size in sizes]
+        + [pltpu.VMEM((tiles, tile, depth), BF), pltpu.VMEM(label.shape, F32)]
+        + [dma((len(xs),)), dma((count,)), dma((tiles,)), dma(()), dma((count, tiles))],
         cost_estimate=pl.CostEstimate(
             flops=2 * rows * width * depth,
             bytes_accessed=2 * (rows * depth + width * depth + rows * width),
             transcendentals=3 * rows * width,
         ),
-        compiler_params=pltpu.CompilerParams(vmem_limit_bytes=24 << 20),
+        compiler_params=pltpu.CompilerParams(vmem_limit_bytes=60 << 20),
         name="scores",
-    )(*xs, words, w, bias, prop)
+    )(*xs, words, w, label)
     return res, post
 
 
@@ -184,12 +222,6 @@
     )(core, *xs, *rs)
 
 
-def bin_prior(bins, prior_mean):
-    levels = jnp.arange(prior_mean.shape[0], dtype=jnp.int32)
-    onehot = (bins[:, None] == levels[None, :]).astype(F32)
-    return jnp.sum(onehot * prior_mean[None, :], axis=1)
-
-
 def shift(v, axis, n, d):
     return lax.ppermute(v, axis, ring(n, d))
 
@@ -206,28 +238,33 @@
     block = part * NZ
     x_at, core, y = (lax.axis_index(a) for a in ("x", "core", "y"))
     offset = (x_at * NZ + lax.axis_index("z")) * width
-    bias, prop = class_bias[None, :], propensity[None, :]
-
     own = exchange(jnp.tile(embeddings, (NZ, 1)), "z")
-    at = jnp.stack([offset, x_at * block])
-    words, obs = words_call(at, label_ids.T, label_count[None, :], width)
-    prior = bin_prior(label_bins, prior_mean)
+    words, obs, label = words_call(
+        jnp.stack([offset, x_at * block]),
+        prior_mean,
+        label_ids.T,
+        label_count[None, :],
+        class_bias[None, :],
+        propensity[None, :],
+        label_bins[None, :],
+    )
 
     half = block // 2
-    front, back = shift(own, "x", NX, -1), shift(own, "x", NX, 1)
-    far = (shift(front[:half], "x", NX, -1), shift(back[half:], "x", NX, 1))
-    (res0,), post0 = score_call(((own,),), (0,), words, class_weight, bias, prop)
-    (res1, res3), post1 = score_call(
-        ((front,), (back,)), (block, 3 * block), words, class_weight, bias, prop
-    )
+    low, high = own[:half], own[half:]
+    front_low, back_high = shift(low, "x", NX, -1), shift(high, "x", NX, 1)
+    front_high, back_low = shift(high, "x", NX, -1), shift(low, "x", NX, 1)
+    far = (shift(front_low, "x", NX, -1), shift(back_high, "x", NX, 1))
+    front, back = (front_low, front_high), (back_low, back_high)
+    (res0,), post0 = score_call(((own,),), (0,), words, class_weight, label)
+    (res1, res3), post1 = score_call((front, back), (block, 3 * block), words, class_weight, label)
     far, post1 = lax.optimization_barrier((far, post1))
-    (res2,), post2 = score_call((far,), (2 * block,), words, class_weight, bias, prop)
+    (res2,), post2 = score_call((far,), (2 * block,), words, class_weight, label)
     post = (post0 + post1) + post2
     both = jnp.concatenate([obs, post], axis=0)[None]
     sums = jnp.sum(exchange(jnp.tile(both, (NY * NC, 1, 1)), ("y", "core")), axis=0)
-    updated = ((sums[0:1] + 8.0 * prior[None, :]) / (sums[1:2] + 8.0)).reshape(width)
-
-    kept_rows, given = weight_call(core[None], (own, front, *far, back), (res0, res1, res2, res3))
+    updated = ((sums[0:1] + label[2:3]) / (sums[1:2] + 8.0)).reshape(width)
+
+    kept_rows, given = weight_call(core[None], (own, *front, *far, *back), (res0, res1, res2, res3))
     pair = kept_rows.astype(F32) + shift(given, "core", NC, 1).astype(F32)
     pair = pair.astype(BF)
     pairs = [lax.dynamic_index_in_dim(pair, (y + d) % NY, 0, keepdims=False) for d in range(NY)]

time: 113 us -> 126 us (1.12)
  blocking collectives: 0 us -> 22.9 us
  waiting for transfers between devices: 31.3 us -> 17.3 us
  Pallas kernels: 22 us -> 32.1 us
  starting transfers between devices: 36.4 us -> 29.5 us
    all_to_all x0 -> x1, blocking collectives: none -> 22.9 us  [exchange(): return lax.all_to_all(v, axis, split_axis=0, concat_axis=0, tiled=True)]
    all_to_all x3 -> x2, waiting for transfers between devices: 14.7 us -> 0.01 us  [exchange(): return lax.all_to_all(v, axis, split_axis=0, concat_axis=0, tiled=True)]
    pallas_call x4, Pallas kernels: 14.4 us -> 24.4 us  [the longest x3 18.2 us: score_call(): pl.pallas_call(functools.partial(score_kernel, at=at, parts=parts, sizes=...]
    all_to_all x3 -> x2, starting transfers between devices: 16.7 us -> 8.25 us  [exchange(): return lax.all_to_all(v, axis, split_axis=0, concat_axis=0, tiled=True)]
    ppermute x14 -> x16, starting transfers between devices: 19.7 us -> 21.3 us  [shift(): return lax.ppermute(v, axis, ring(n, d))]
    unnamed x38 -> x48, local copies, waits for them, and re-layouts: 7.44 us -> 8.62 us
    ppermute x14 -> x16, waiting for transfers between devices: 16.6 us -> 17.2 us  [shift(): return lax.ppermute(v, axis, ring(n, d))]
  transfers between devices with their start and end apart: 17 -> 18, of which waited for: 5 -> 4; matrix products, arithmetic and copies ran while one was open for 9% -> 8% of each run, Pallas kernels for 18% -> 21%
where the time goes in v2:
time: 126 us; the launch traced here: 124 us
  Pallas kernels  32.1 us (25%)
  starting transfers between devices  29.5 us (23%)
  blocking collectives  22.9 us (18%)
  waiting for transfers between devices  17.3 us (14%)
  local copies, waits for them, and re-layouts  10.3 us (8%)
  other arithmetic  6.95 us (6%)
  matrix products  3.92 us (3%)
    all_to_all x1, blocking collectives, exchange(): return lax.all_to_all(v, axis, split_axis=0, concat_axis=0, tiled=True)  22.9 us
    ppermute x16, starting transfers between devices, shift(): return lax.ppermute(v, axis, ring(n, d))  21.3 us
    pallas_call x3, Pallas kernels, score_call(): pl.pallas_call(functools.partial(score_kernel, at=at, parts=parts, sizes=...  18.2 us
    ppermute x16, waiting for transfers between devices, shift(): return lax.ppermute(v, axis, ring(n, d))  17.2 us
    unnamed x48, local copies, waits for them, and re-layouts  8.62 us
    all_to_all x2, starting transfers between devices, exchange(): return lax.all_to_all(v, axis, split_axis=0, concat_axis=0, tiled=True)  8.25 us
    pallas_call x1, Pallas kernels, weight_call(): pl.pallas_call(functools.partial(weight_kernel, count=len(xs)), grid=(wid...  7.75 us
    pallas_call x1, Pallas kernels, words_call(): pl.pallas_call(words_kernel, in_specs=[pl.BlockSpec(memory_space=pltpu.SM...  6.21 us
  transfers between devices with their start and end apart: 18, of which 4 were waited for; matrix products, arithmetic and copies ran while one was open for 8% of the time, Pallas kernels for 21%

profile of v2, /device:TPU:16, one launch (start us, length us, event | category | flops | bytes accessed | tf_op | source)
XLA Modules:
  0.0 124.0 jit_solution(12156257991025199204)
XLA Ops:
  1.5 22.9 %all_to_all.19 = bf16[8,32,768]{2,1,0:T(8,128)(2,1)S(1)} all-to-all(bf16[8,32,768]{2,1,0:T(8,128)(2,1)S(1)} %tile.4), channel_id=1, replica_groups=mesh['y'=4,'core'=2,'x'=4,'z'=8] {'z'}, dimensions={0} | all-to-all | bytes 786432 | tf_op jit(solution)/shard_map/all_to_all | solution.py:230
  24.4 2.8 %collective-permute-start = (bf16[128,768]{1,0:T(8,128)(2,1)S(1)}, bf16[128,768]{1,0:T(8,128)(2,1)S(1)}, u32[]{:S(2)}, u32[]{:S(2)}) collective-permute-start(bf16[128,768]{1,0:T(8,128)(2,1)S(1)} %bitcast.40), channel_id=1, source_target_pairs={{0,24},{8,0},{16,8},{24,16},{1,25},{9,1},{17,9},{25,17},{2,26},{10... | collective-permute-start | bytes 589832 | tf_op jit(solution)/shard_map/ppermute | solution.py:226
  28.0 2.5 %collective-permute-start.4 = (bf16[128,768]{1,0:T(8,128)(2,1)S(1)}, bf16[128,768]{1,0:T(8,128)(2,1)S(1)}, u32[]{:S(2)}, u32[]{:S(2)}) collective-permute-start(bf16[128,768]{1,0:T(8,128)(2,1)S(1)} %bitcast.39), channel_id=1, source_target_pairs={{0,24},{8,0},{16,8},{24,16},{1,25},{9,1},{17,9},{25,17},{2,26},{10... | collective-permute-start | bytes 589832 | tf_op jit(solution)/shard_map/ppermute | solution.py:226
  35.0 6.2 %words.1 = (s32[1024,128]{1,0:T(8,128)S(1)}, f32[1,2048]{1,0:T(1,128)S(1)}, f32[3,2048]{1,0:T(4,128)S(1)}) custom-call(s32[2]{0:T(128)S(1)} %pad_add_fusion.at_ref, f32[16]{0:T(128)S(1)} %copy-done.7, s32[32,1024]{1,0:T(8,128)S(1)} %bitcast.31, s32[1,1024]{1,0:T(1,128)S(1)} %bitcast.35, f32[1,2048]{1,0:T(1,128)S(1)} %bitcast.32, f32[1,2048]{1,0:T(1,128)S(1)} %bitcast.33, ...), custom_call_target="tpu_custom_call" | custom-call | flops 26214400 | bytes 1048576 | tf_op jit(solution)/shard_map/words/pallas_call | solution.py:63
  42.6 2.0 %collective-permute-start.1 = (bf16[128,768]{1,0:T(8,128)(2,1)S(1)}, bf16[128,768]{1,0:T(8,128)(2,1)S(1)}, u32[]{:S(2)}, u32[]{:S(2)}) collective-permute-start(bf16[128,768]{1,0:T(8,128)(2,1)S(1)} %collective-permute-done.refs_0_.refs_1_), channel_id=1, source_target_pairs={{0,24},{8,0},{16,8},{24,16},{1,25},{9,1},{17,9},{25,17},{2,26},{10... | collective-permute-start | bytes 589832 | tf_op jit(solution)/shard_map/ppermute | solution.py:226
  44.6 5.6 %scores.3 = (bf16[256,2048]{1,0:T(8,128)(2,1)}, f32[1,2048]{1,0:T(1,128)}) custom-call(bf16[256,768]{1,0:T(8,128)(2,1)} %bitcast.36, s32[1024,128]{1,0:T(8,128)} %copy-done, bf16[2048,768]{1,0:T(8,128)(2,1)} %refs_3_.1, f32[3,2048]{1,0:T(4,128)} %copy-done.1), custom_call_target="tpu_custom_call" | custom-call | flops 805306368 | bytes 4587520 | tf_op jit(solution)/shard_map/scores/pallas_call | solution.py:151
  51.6 7.0 %scores.4 = (bf16[256,2048]{1,0:T(8,128)(2,1)}, bf16[256,2048]{1,0:T(8,128)(2,1)}, f32[1,2048]{1,0:T(1,128)}) custom-call(bf16[128,768]{1,0:T(8,128)(2,1)} %copy-done.18, bf16[128,768]{1,0:T(8,128)(2,1)} %copy-done.21, bf16[128,768]{1,0:T(8,128)(2,1)} %copy-done.20, bf16[128,768]{1,0:T(8,128)(2,1)} %copy-done.19, s32[1024,128]{1,0:T(8,128)} %copy-done, ...), custom_call_target="tpu_custom_call" | custom-call | flops 1610612736 | bytes 6029312 | tf_op jit(solution)/shard_map/scores/pallas_call | solution.py:151
  59.4 5.5 %scores.5 = (bf16[256,2048]{1,0:T(8,128)(2,1)}, f32[1,2048]{1,0:T(1,128)}) custom-call(bf16[128,768]{1,0:T(8,128)(2,1)} %copy-done.11, bf16[128,768]{1,0:T(8,128)(2,1)} %copy-done.12, s32[1024,128]{1,0:T(8,128)} %copy-done, bf16[2048,768]{1,0:T(8,128)(2,1)} %refs_3_.1, f32[3,2048]{1,0:T(4,128)} %copy-done.1), custom_call_target="tpu_custom_call" | custom-call | flops 805306368 | bytes 4587520 | tf_op jit(solution)/shard_map/scores/pallas_call | solution.py:151
  66.4 4.8 %all-to-all-start.1 = ((f32[8,2,2048]{2,1,0:T(2,128)}), f32[8,2,2048]{2,1,0:T(2,128)S(1)}, u32[]{:S(2)}, u32[]{:S(2)}) async-start(f32[8,2,2048]{2,1,0:T(2,128)} %tile.5), calls=%async_computation.1 | async-start | bytes 262144 | tf_op jit(solution)/shard_map/all_to_all | solution.py:230
  71.2 7.7 %weights.1 = (bf16[4,96,2048]{2,1,0:T(8,128)(2,1)}, bf16[4,96,2048]{2,1,0:T(8,128)(2,1)}) custom-call(s32[1]{0:T(128)} %bitcast.11.core_ref, bf16[256,768]{1,0:T(8,128)(2,1)} %bitcast.37, bf16[128,768]{1,0:T(8,128)(2,1)} %copy-done.18, bf16[128,768]{1,0:T(8,128)(2,1)} %copy-done.21, bf16[128,768]{1,0:T(8,128)(2,1)} %copy-done.11, ...), custom_call_target="tpu_custom_call" | custom-call | flops 3221225472 | bytes 8912896 | tf_op jit(solution)/shard_map/weights/pallas_call | solution.py:202
  81.2 1.0 fusion.8
  82.4 1.0 fusion.7
  83.6 3.4 %collective-permute-start.12 = (bf16[128,768]{1,0:T(8,128)(2,1)S(1)}, bf16[128,768]{1,0:T(8,128)(2,1)S(1)}, u32[]{:S(2)}, u32[]{:S(2)}) collective-permute-start(bf16[128,768]{1,0:T(8,128)(2,1)S(1)} %slice.90), channel_id=1, source_target_pairs={{0,24},{8,0},{16,8},{24,16},{1,25},{9,1},{17,9},{25,17},{2,26},{10... | collective-permute-start | bytes 589832 | tf_op jit(solution)/shard_map/ppermute | solution.py:226
  87.0 1.0 convolution_convert_fusion
  88.1 3.2 %collective-permute-start.14 = (bf16[128,768]{1,0:T(8,128)(2,1)S(1)}, bf16[128,768]{1,0:T(8,128)(2,1)S(1)}, u32[]{:S(2)}, u32[]{:S(2)}) collective-permute-start(bf16[128,768]{1,0:T(8,128)(2,1)S(1)} %get-tuple-element.50), channel_id=1, source_target_pairs={{0,24},{8,0},{16,8},{24,16},{1,25},{9,1},{17,9},{25,17},{2,26},{10... | collective-permute-start | bytes 589832 | tf_op jit(solution)/shard_map/ppermute | solution.py:226
  92.3 4.0 %collective-permute-done.10 = bf16[128,768]{1,0:T(8,128)(2,1)S(1)} collective-permute-done((bf16[128,768]{1,0:T(8,128)(2,1)S(1)}, bf16[128,768]{1,0:T(8,128)(2,1)S(1)}, u32[]{:S(2)}, u32[]{:S(2)}) %collective-permute-start.10) | collective-permute-done | bytes 196640 | tf_op jit(solution)/shard_map/ppermute | solution.py:226
  96.6 3.3 %collective-permute-start.15 = (bf16[128,768]{1,0:T(8,128)(2,1)S(1)}, bf16[128,768]{1,0:T(8,128)(2,1)S(1)}, u32[]{:S(2)}, u32[]{:S(2)}) collective-permute-start(bf16[128,768]{1,0:T(8,128)(2,1)S(1)} %fusion), channel_id=1, source_target_pairs={{0,24},{8,0},{16,8},{24,16},{1,25},{9,1},{17,9},{25,17},{2,26},{10... | collective-permute-start | bytes 589832 | tf_op jit(solution)/shard_map/ppermute | solution.py:226
  99.8 2.0 %add_convert_fusion = bf16[4,96,2048]{2,1,0:T(8,128)(2,1)S(1)} fusion(bf16[4,96,2048]{2,1,0:T(8,128)(2,1)} %collective-permute-done.6, bf16[4,96,2048]{2,1,0:T(8,128)(2,1)S(1)} %copy-done.10), kind=kLoop, calls=%fused_computation.1 | loop fusion | flops 3145728 | bytes 4718592 | tf_op jit(solution)/shard_map/convert_element_type | solution.py:269
  102.0 1.3 %collective-permute-start.7 = (bf16[96,2048]{1,0:T(8,128)(2,1)S(1)}, bf16[96,2048]{1,0:T(8,128)(2,1)S(1)}, u32[]{:S(2)}, u32[]{:S(2)}) collective-permute-start(bf16[96,2048]{1,0:T(8,128)(2,1)S(1)} %get-tuple-element.39), channel_id=1, source_target_pairs={{0,64},{64,128},{128,192},{192,0},{1,65},{65,129},{129,193},{193,1... | collective-permute-start | bytes 1179656 | tf_op jit(solution)/shard_map/ppermute | solution.py:226
  105.7 3.5 %all-to-all-start.2 = ((bf16[8,32,768]{2,1,0:T(8,128)(2,1)}), bf16[8,32,768]{2,1,0:T(8,128)(2,1)S(1)}, u32[]{:S(2)}, u32[]{:S(2)}) async-start(bf16[8,32,768]{2,1,0:T(8,128)(2,1)} %bitcast.17), calls=%async_computation.2 | async-start | bytes 786432 | tf_op jit(solution)/shard_map/all_to_all | solution.py:230
  109.2 4.9 %collective-permute-done.7 = bf16[96,2048]{1,0:T(8,128)(2,1)S(1)} collective-permute-done((bf16[96,2048]{1,0:T(8,128)(2,1)S(1)}, bf16[96,2048]{1,0:T(8,128)(2,1)S(1)}, u32[]{:S(2)}, u32[]{:S(2)}) %collective-permute-start.7) | collective-permute-done | bytes 393248 | tf_op jit(solution)/shard_map/ppermute | solution.py:226
  114.1 6.5 %collective-permute-done.8 = bf16[96,2048]{1,0:T(8,128)(2,1)S(1)} collective-permute-done((bf16[96,2048]{1,0:T(8,128)(2,1)S(1)}, bf16[96,2048]{1,0:T(8,128)(2,1)S(1)}, u32[]{:S(2)}, u32[]{:S(2)}) %collective-permute-start.8) | collective-permute-done | bytes 393248 | tf_op jit(solution)/shard_map/ppermute | solution.py:226
  120.5 1.8 %collective-permute-done.9 = bf16[96,2048]{1,0:T(8,128)(2,1)S(1)} collective-permute-done((bf16[96,2048]{1,0:T(8,128)(2,1)S(1)}, bf16[96,2048]{1,0:T(8,128)(2,1)S(1)}, u32[]{:S(2)}, u32[]{:S(2)}) %collective-permute-start.9) | collective-permute-done | bytes 393248 | tf_op jit(solution)/shard_map/ppermute | solution.py:226
  122.4 1.0 fusion.2
  (90 shorter events, 18.0 us)
Async XLA Ops:
  24.4 20.2 %copy-start.9 = (bf16[8,32,768]{2,1,0:T(8,128)(2,1)}, bf16[8,32,768]{2,1,0:T(8,128)(2,1)S(1)}, u32[]{:S(2)}) copy-start(bf16[8,32,768]{2,1,0:T(8,128)(2,1)S(1)} %all_to_all.19) | copy-start | bytes 1179652
  24.4 18.2 %collective-permute-start = (bf16[128,768]{1,0:T(8,128)(2,1)S(1)}, bf16[128,768]{1,0:T(8,128)(2,1)S(1)}, u32[]{:S(2)}, u32[]{:S(2)}) collective-permute-start(bf16[128,768]{1,0:T(8,128)(2,1)S(1)} %bitcast.40), channel_id=1, source_target_pairs={{0,24},{8,0},{16,8},{24,16},{1,25},{9,1},{17,9},{25,17},{2,26},{10... | collective-permute-start | bytes 589832 | tf_op jit(solution)/shard_map/ppermute | solution.py:226
  27.3 17.3 %collective-permute-start.2 = (bf16[128,768]{1,0:T(8,128)(2,1)S(1)}, bf16[128,768]{1,0:T(8,128)(2,1)S(1)}, u32[]{:S(2)}, u32[]{:S(2)}) collective-permute-start(bf16[128,768]{1,0:T(8,128)(2,1)S(1)} %bitcast.38), channel_id=1, source_target_pairs={{0,8},{8,16},{16,24},{24,0},{1,9},{9,17},{17,25},{25,1},{2,10},{10... | collective-permute-start | bytes 589832 | tf_op jit(solution)/shard_map/ppermute | solution.py:226
  27.3 23.0 %collective-permute-start.5 = (bf16[128,768]{1,0:T(8,128)(2,1)S(1)}, bf16[128,768]{1,0:T(8,128)(2,1)S(1)}, u32[]{:S(2)}, u32[]{:S(2)}) collective-permute-start(bf16[128,768]{1,0:T(8,128)(2,1)S(1)} %bitcast.41), channel_id=1, source_target_pairs={{0,8},{8,16},{16,24},{24,0},{1,9},{9,17},{17,25},{25,1},{2,10},{10... | collective-permute-start | bytes 589832 | tf_op jit(solution)/shard_map/ppermute | solution.py:226
  28.0 22.2 %collective-permute-start.4 = (bf16[128,768]{1,0:T(8,128)(2,1)S(1)}, bf16[128,768]{1,0:T(8,128)(2,1)S(1)}, u32[]{:S(2)}, u32[]{:S(2)}) collective-permute-start(bf16[128,768]{1,0:T(8,128)(2,1)S(1)} %bitcast.39), channel_id=1, source_target_pairs={{0,24},{8,0},{16,8},{24,16},{1,25},{9,1},{17,9},{25,17},{2,26},{10... | collective-permute-start | bytes 589832 | tf_op jit(solution)/shard_map/ppermute | solution.py:226
  42.6 7.7 %copy-start.18 = (bf16[128,768]{1,0:T(8,128)(2,1)}, bf16[128,768]{1,0:T(8,128)(2,1)S(1)}, u32[]{:S(2)}) copy-start(bf16[128,768]{1,0:T(8,128)(2,1)S(1)} %collective-permute-done.refs_0_.refs_1_) | copy-start | bytes 589828
  42.6 16.1 %collective-permute-start.1 = (bf16[128,768]{1,0:T(8,128)(2,1)S(1)}, bf16[128,768]{1,0:T(8,128)(2,1)S(1)}, u32[]{:S(2)}, u32[]{:S(2)}) collective-permute-start(bf16[128,768]{1,0:T(8,128)(2,1)S(1)} %collective-permute-done.refs_0_.refs_1_), channel_id=1, source_target_pairs={{0,24},{8,0},{16,8},{24,16},{1,25},{9,1},{17,9},{25,17},{2,26},{10... | collective-permute-start | bytes 589832 | tf_op jit(solution)/shard_map/ppermute | solution.py:226
  44.6 14.1 %collective-permute-start.3 = (bf16[128,768]{1,0:T(8,128)(2,1)S(1)}, bf16[128,768]{1,0:T(8,128)(2,1)S(1)}, u32[]{:S(2)}, u32[]{:S(2)}) collective-permute-start(bf16[128,768]{1,0:T(8,128)(2,1)S(1)} %collective-permute-done.2.refs_3_.refs_6_), channel_id=1, source_target_pairs={{0,8},{8,16},{16,24},{24,0},{1,9},{9,17},{17,25},{25,1},{2,10},{10... | collective-permute-start | bytes 589832 | tf_op jit(solution)/shard_map/ppermute | solution.py:226
  66.4 12.7 %all-to-all-start.1 = ((f32[8,2,2048]{2,1,0:T(2,128)}), f32[8,2,2048]{2,1,0:T(2,128)S(1)}, u32[]{:S(2)}, u32[]{:S(2)}) async-start(f32[8,2,2048]{2,1,0:T(2,128)} %tile.5), calls=%async_computation.1 | async-start | bytes 262144 | tf_op jit(solution)/shard_map/all_to_all | solution.py:230
  71.2 8.7 %copy-start.8 = (bf16[2048,768]{1,0:T(8,128)(2,1)S(1)}, bf16[2048,768]{1,0:T(8,128)(2,1)}, u32[]{:S(2)}) copy-start(bf16[2048,768]{1,0:T(8,128)(2,1)} %refs_3_.1) | copy-start | bytes 9437188
  79.0 20.9 %collective-permute-start.6 = (bf16[4,96,2048]{2,1,0:T(8,128)(2,1)}, bf16[4,96,2048]{2,1,0:T(8,128)(2,1)}, u32[]{:S(2)}, u32[]{:S(2)}) collective-permute-start(bf16[4,96,2048]{2,1,0:T(8,128)(2,1)} %get-tuple-element.37), channel_id=1, source_target_pairs={{0,32},{32,0},{1,33},{33,1},{2,34},{34,2},{3,35},{35,3},{4,36},{36... | collective-permute-start | bytes 4718600 | tf_op jit(solution)/shard_map/ppermute | solution.py:226
  79.9 42.5 %copy-start.13 = (f32[1,2048]{1,0:T(1,128)}, f32[1,2048]{1,0:T(1,128)S(1)}, u32[]{:S(2)}) copy-start(f32[1,2048]{1,0:T(1,128)S(1)} %fusion.3) | copy-start | bytes 24580
  83.5 7.9 %copy-start.16 = (bf16[256,2048]{1,0:T(8,128)(2,1)S(1)}, bf16[256,2048]{1,0:T(8,128)(2,1)}, u32[]{:S(2)}) copy-start(bf16[256,2048]{1,0:T(8,128)(2,1)} %get-tuple-element.32.refs_7_) | copy-start | bytes 3145732
  83.5 19.8 %collective-permute-start.13 = (bf16[128,768]{1,0:T(8,128)(2,1)S(1)}, bf16[128,768]{1,0:T(8,128)(2,1)S(1)}, u32[]{:S(2)}, u32[]{:S(2)}) collective-permute-start(bf16[128,768]{1,0:T(8,128)(2,1)S(1)} %slice.89), channel_id=1, source_target_pairs={{0,8},{8,16},{16,24},{24,0},{1,9},{9,17},{17,25},{25,1},{2,10},{10... | collective-permute-start | bytes 589832 | tf_op jit(solution)/shard_map/ppermute | solution.py:226
  83.6 20.5 %collective-permute-start.12 = (bf16[128,768]{1,0:T(8,128)(2,1)S(1)}, bf16[128,768]{1,0:T(8,128)(2,1)S(1)}, u32[]{:S(2)}, u32[]{:S(2)}) collective-permute-start(bf16[128,768]{1,0:T(8,128)(2,1)S(1)} %slice.90), channel_id=1, source_target_pairs={{0,24},{8,0},{16,8},{24,16},{1,25},{9,1},{17,9},{25,17},{2,26},{10... | collective-permute-start | bytes 589832 | tf_op jit(solution)/shard_map/ppermute | solution.py:226
  88.0 8.3 %collective-permute-start.10 = (bf16[128,768]{1,0:T(8,128)(2,1)S(1)}, bf16[128,768]{1,0:T(8,128)(2,1)S(1)}, u32[]{:S(2)}, u32[]{:S(2)}) collective-permute-start(bf16[128,768]{1,0:T(8,128)(2,1)S(1)} %get-tuple-element.49), channel_id=1, source_target_pairs={{0,8},{8,16},{16,24},{24,0},{1,9},{9,17},{17,25},{25,1},{2,10},{10... | collective-permute-start | bytes 589832 | tf_op jit(solution)/shard_map/ppermute | solution.py:226
  88.1 11.7 %copy-start.10 = (bf16[4,96,2048]{2,1,0:T(8,128)(2,1)S(1)}, bf16[4,96,2048]{2,1,0:T(8,128)(2,1)}, u32[]{:S(2)}) copy-start(bf16[4,96,2048]{2,1,0:T(8,128)(2,1)} %get-tuple-element.36) | copy-start | bytes 4718596
  88.1 8.4 %collective-permute-start.14 = (bf16[128,768]{1,0:T(8,128)(2,1)S(1)}, bf16[128,768]{1,0:T(8,128)(2,1)S(1)}, u32[]{:S(2)}, u32[]{:S(2)}) collective-permute-start(bf16[128,768]{1,0:T(8,128)(2,1)S(1)} %get-tuple-element.50), channel_id=1, source_target_pairs={{0,24},{8,0},{16,8},{24,16},{1,25},{9,1},{17,9},{25,17},{2,26},{10... | collective-permute-start | bytes 589832 | tf_op jit(solution)/shard_map/ppermute | solution.py:226
  96.4 8.4 %collective-permute-start.11 = (bf16[128,768]{1,0:T(8,128)(2,1)S(1)}, bf16[128,768]{1,0:T(8,128)(2,1)S(1)}, u32[]{:S(2)}, u32[]{:S(2)}) collective-permute-start(bf16[128,768]{1,0:T(8,128)(2,1)S(1)} %fusion.1), channel_id=1, source_target_pairs={{0,8},{8,16},{16,24},{24,0},{1,9},{9,17},{17,25},{25,1},{2,10},{10... | collective-permute-start | bytes 589832 | tf_op jit(solution)/shard_map/ppermute | solution.py:226
  96.6 8.3 %collective-permute-start.15 = (bf16[128,768]{1,0:T(8,128)(2,1)S(1)}, bf16[128,768]{1,0:T(8,128)(2,1)S(1)}, u32[]{:S(2)}, u32[]{:S(2)}) collective-permute-start(bf16[128,768]{1,0:T(8,128)(2,1)S(1)} %fusion), channel_id=1, source_target_pairs={{0,24},{8,0},{16,8},{24,16},{1,25},{9,1},{17,9},{25,17},{2,26},{10... | collective-permute-start | bytes 589832 | tf_op jit(solution)/shard_map/ppermute | solution.py:226
  102.0 12.1 %collective-permute-start.7 = (bf16[96,2048]{1,0:T(8,128)(2,1)S(1)}, bf16[96,2048]{1,0:T(8,128)(2,1)S(1)}, u32[]{:S(2)}, u32[]{:S(2)}) collective-permute-start(bf16[96,2048]{1,0:T(8,128)(2,1)S(1)} %get-tuple-element.39), channel_id=1, source_target_pairs={{0,64},{64,128},{128,192},{192,0},{1,65},{65,129},{129,193},{193,1... | collective-permute-start | bytes 1179656 | tf_op jit(solution)/shard_map/ppermute | solution.py:226
  103.2 17.3 %collective-permute-start.8 = (bf16[96,2048]{1,0:T(8,128)(2,1)S(1)}, bf16[96,2048]{1,0:T(8,128)(2,1)S(1)}, u32[]{:S(2)}, u32[]{:S(2)}) collective-permute-start(bf16[96,2048]{1,0:T(8,128)(2,1)S(1)} %get-tuple-element.40), channel_id=1, source_target_pairs={{0,128},{64,192},{128,0},{192,64},{1,129},{65,193},{129,1},{193,65... | collective-permute-start | bytes 1179656 | tf_op jit(solution)/shard_map/ppermute | solution.py:226
  104.1 18.3 %collective-permute-start.9 = (bf16[96,2048]{1,0:T(8,128)(2,1)S(1)}, bf16[96,2048]{1,0:T(8,128)(2,1)S(1)}, u32[]{:S(2)}, u32[]{:S(2)}) collective-permute-start(bf16[96,2048]{1,0:T(8,128)(2,1)S(1)} %get-tuple-element.41), channel_id=1, source_target_pairs={{0,192},{64,0},{128,64},{192,128},{1,193},{65,1},{129,65},{193,129... | collective-permute-start | bytes 1179656 | tf_op jit(solution)/shard_map/ppermute | solution.py:226
  105.7 17.6 %all-to-all-start.2 = ((bf16[8,32,768]{2,1,0:T(8,128)(2,1)}), bf16[8,32,768]{2,1,0:T(8,128)(2,1)S(1)}, u32[]{:S(2)}, u32[]{:S(2)}) async-start(bf16[8,32,768]{2,1,0:T(8,128)(2,1)} %bitcast.17), calls=%async_computation.2 | async-start | bytes 786432 | tf_op jit(solution)/shard_map/all_to_all | solution.py:230
  (18 other events, 33.9 us)

commit v3 on v2

--- a/solution.py
+++ b/solution.py
@@ -80,10 +80,10 @@
 def score_kernel(*refs, at, parts, sizes, tile):
     count = len(at)
     x_refs, refs = refs[: sum(parts)], refs[sum(parts) :]
-    words_ref, w_ref, label_ref = refs[:3]
+    words_ref, label_ref, w_ref = refs[:3]
     res_refs, post_ref, refs = refs[3 : count + 3], refs[count + 3], refs[count + 4 :]
     x_in, words_in, slots = refs[:count], refs[count : 2 * count], refs[2 * count : 3 * count]
-    w_in, label_in, x_sems, words_sems, w_sems, label_sem, out_sems = refs[3 * count :]
+    label_in, x_sems, words_sems, label_sem, out_sems = refs[3 * count :]
     tiles = w_ref.shape[0] // tile
 
     first = []
@@ -98,25 +98,20 @@
         source = words_ref.at[at[k] : at[k] + sizes[k], :]
         first.append(pltpu.make_async_copy(source, words_in[k], words_sems.at[k]))
     first.append(pltpu.make_async_copy(label_ref, label_in, label_sem))
-    weights = [
-        pltpu.make_async_copy(w_ref.at[t * tile : (t + 1) * tile, :], w_in.at[t], w_sems.at[t])
-        for t in range(tiles)
-    ]
-    for copy in first + weights:
+    for copy in first:
         copy.start()
     for copy in first:
         copy.wait()
 
     outs = []
     for t in range(tiles):
-        weights[t].wait()
         cols = slice(t * tile, (t + 1) * tile)
         bias, prop = label_in[0:1, cols], label_in[1:2, cols]
         rest = 1.0 - prop
         total = jnp.zeros((8, tile), F32)
         for k in range(count):
             size = sizes[k]
-            scores = mm(x_in[k][...], w_in[t], ((1,), (1,)))
+            scores = mm(x_in[k][...], w_ref[cols, :], ((1,), (1,)))
             grown = 1.0 + jnp.exp2(scores * -LOG2E + bias)
             prob = 1.0 / grown
             unseen = rest / (grown - prop)
@@ -150,23 +145,23 @@
     dma = pltpu.SemaphoreType.DMA
     *res, post = pl.pallas_call(
         functools.partial(score_kernel, at=at, parts=parts, sizes=sizes, tile=tile),
-        in_specs=[pl.BlockSpec(memory_space=pl.ANY)] * (len(xs) + 3),
+        in_specs=[pl.BlockSpec(memory_space=pltpu.HBM)] * (len(xs) + 2) + in_vmem(1),
         out_specs=[pl.BlockSpec(memory_space=pltpu.HBM)] * count + in_vmem(1),
         out_shape=[pltpu.HBM((size, width), BF) for size in sizes]
         + [jax.ShapeDtypeStruct((1, width), F32)],
         scratch_shapes=[pltpu.VMEM((size, depth), BF) for size in sizes]
         + [pltpu.VMEM((size, LANES), jnp.int32) for size in sizes]
         + [pltpu.VMEM((tiles, size, tile), BF) for size in sizes]
-        + [pltpu.VMEM((tiles, tile, depth), BF), pltpu.VMEM(label.shape, F32)]
-        + [dma((len(xs),)), dma((count,)), dma((tiles,)), dma(()), dma((count, tiles))],
+        + [pltpu.VMEM(label.shape, F32)]
+        + [dma((len(xs),)), dma((count,)), dma(()), dma((count, tiles))],
         cost_estimate=pl.CostEstimate(
             flops=2 * rows * width * depth,
             bytes_accessed=2 * (rows * depth + width * depth + rows * width),
             transcendentals=3 * rows * width,
         ),
-        compiler_params=pltpu.CompilerParams(vmem_limit_bytes=60 << 20),
+        compiler_params=pltpu.CompilerParams(vmem_limit_bytes=24 << 20),
         name="scores",
-    )(*xs, words, w, label)
+    )(*xs, words, label, w)
     return res, post
 
 

time: 126 us -> 117 us (0.929)
  Pallas kernels: 32.1 us -> 24.7 us
    pallas_call x3, Pallas kernels: 18.2 us -> 10.8 us  [score_call(): pl.pallas_call(functools.partial(score_kernel, at=at, parts=parts, sizes=...]
    unnamed x48 -> x36, local copies, waits for them, and re-layouts: 8.62 us -> 7.06 us
  transfers between devices with their start and end apart: 18 -> 18, of which waited for: 4 -> 4; matrix products, arithmetic and copies ran while one was open for 8% -> 8% of each run, Pallas kernels for 21% -> 19%
where the time goes in v3:
time: 117 us; the launch traced here: 115 us
  starting transfers between devices  29.6 us (25%)
  Pallas kernels  24.7 us (21%)
  blocking collectives  22.9 us (20%)
  waiting for transfers between devices  17 us (15%)
  local copies, waits for them, and re-layouts  9.59 us (8%)
  other arithmetic  6.27 us (5%)
  matrix products  3.9 us (3%)
    all_to_all x1, blocking collectives, exchange(): return lax.all_to_all(v, axis, split_axis=0, concat_axis=0, tiled=True)  22.9 us
    ppermute x16, starting transfers between devices, shift(): return lax.ppermute(v, axis, ring(n, d))  21.3 us
    ppermute x16, waiting for transfers between devices, shift(): return lax.ppermute(v, axis, ring(n, d))  17 us
    pallas_call x3, Pallas kernels, score_call(): pl.pallas_call(functools.partial(score_kernel, at=at, parts=parts, sizes=...  10.8 us
    all_to_all x2, starting transfers between devices, exchange(): return lax.all_to_all(v, axis, split_axis=0, concat_axis=0, tiled=True)  8.25 us
    pallas_call x1, Pallas kernels, weight_call(): pl.pallas_call(functools.partial(weight_kernel, count=len(xs)), grid=(wid...  7.6 us
    unnamed x36, local copies, waits for them, and re-layouts  7.06 us
    pallas_call x1, Pallas kernels, words_call(): pl.pallas_call(words_kernel, in_specs=[pl.BlockSpec(memory_space=pltpu.SM...  6.21 us
  transfers between devices with their start and end apart: 18, of which 4 were waited for; matrix products, arithmetic and copies ran while one was open for 8% of the time, Pallas kernels for 19%

profile of v3, /device:TPU:16, one launch (start us, length us, event | category | flops | bytes accessed | tf_op | source)
XLA Modules:
  0.0 115.0 jit_solution(11616584381777448131)
XLA Ops:
  1.5 22.9 %all_to_all.19 = bf16[8,32,768]{2,1,0:T(8,128)(2,1)S(1)} all-to-all(bf16[8,32,768]{2,1,0:T(8,128)(2,1)S(1)} %tile.4), channel_id=1, replica_groups=mesh['y'=4,'core'=2,'x'=4,'z'=8] {'z'}, dimensions={0} | all-to-all | bytes 786432 | tf_op jit(solution)/shard_map/all_to_all | solution.py:225
  25.2 2.8 %collective-permute-start = (bf16[128,768]{1,0:T(8,128)(2,1)}, bf16[128,768]{1,0:T(8,128)(2,1)}, u32[]{:S(2)}, u32[]{:S(2)}) collective-permute-start(bf16[128,768]{1,0:T(8,128)(2,1)} %bitcast.8), channel_id=1, source_target_pairs={{0,24},{8,0},{16,8},{24,16},{1,25},{9,1},{17,9},{25,17},{2,26},{10... | collective-permute-start | bytes 589832 | tf_op jit(solution)/shard_map/ppermute | solution.py:221
  28.8 2.5 %collective-permute-start.4 = (bf16[128,768]{1,0:T(8,128)(2,1)}, bf16[128,768]{1,0:T(8,128)(2,1)}, u32[]{:S(2)}, u32[]{:S(2)}) collective-permute-start(bf16[128,768]{1,0:T(8,128)(2,1)} %bitcast.9), channel_id=1, source_target_pairs={{0,24},{8,0},{16,8},{24,16},{1,25},{9,1},{17,9},{25,17},{2,26},{10... | collective-permute-start | bytes 589832 | tf_op jit(solution)/shard_map/ppermute | solution.py:221
  35.7 6.2 %words.1 = (s32[1024,128]{1,0:T(8,128)S(1)}, f32[1,2048]{1,0:T(1,128)S(1)}, f32[3,2048]{1,0:T(4,128)S(1)}) custom-call(s32[2]{0:T(128)S(1)} %pad_add_fusion.at_ref, f32[16]{0:T(128)S(1)} %copy-done.11, s32[32,1024]{1,0:T(8,128)S(1)} %bitcast.33, s32[1,1024]{1,0:T(1,128)S(1)} %bitcast.37, f32[1,2048]{1,0:T(1,128)S(1)} %bitcast.34, f32[1,2048]{1,0:T(1,128)S(1)} %bitcast.35, ...), custom_call_target="tpu_custom_call" | custom-call | flops 26214400 | bytes 1048576 | tf_op jit(solution)/shard_map/words/pallas_call | solution.py:63
  41.9 2.1 %collective-permute-start.1 = (bf16[128,768]{1,0:T(8,128)(2,1)}, bf16[128,768]{1,0:T(8,128)(2,1)S(1)}, u32[]{:S(2)}, u32[]{:S(2)}) collective-permute-start(bf16[128,768]{1,0:T(8,128)(2,1)} %collective-permute-done.refs_0_.refs_1_), channel_id=1, source_target_pairs={{0,24},{8,0},{16,8},{24,16},{1,25},{9,1},{17,9},{25,17},{2,26},{10... | collective-permute-start | bytes 589832 | tf_op jit(solution)/shard_map/ppermute | solution.py:221
  44.0 1.9 %copy-done = bf16[2048,768]{1,0:T(8,128)(2,1)S(1)} copy-done((bf16[2048,768]{1,0:T(8,128)(2,1)S(1)}, bf16[2048,768]{1,0:T(8,128)(2,1)}, u32[]{:S(2)}) %copy-start) | copy-done | bytes 3145752
  45.9 2.8 %scores.3 = (bf16[256,2048]{1,0:T(8,128)(2,1)}, f32[1,2048]{1,0:T(1,128)S(1)}) custom-call(bf16[256,768]{1,0:T(8,128)(2,1)S(1)} %bitcast.31, s32[1024,128]{1,0:T(8,128)S(1)} %get-tuple-element.24.refs_1_.refs_4_.refs_2_, f32[3,2048]{1,0:T(4,128)S(1)} %get-tuple-element.25.refs_2_.refs_5_.refs_3_, bf16[2048,768]{1,0:T(8,128)(2,1)S(1)} %copy-done), custom_call_target="tpu_custom_call" | custom-call | flops 805306368 | bytes 4587520 | tf_op jit(solution)/shard_map/scores/pallas_call | solution.py:146
  48.7 5.1 %scores.4 = (bf16[256,2048]{1,0:T(8,128)(2,1)}, bf16[256,2048]{1,0:T(8,128)(2,1)}, f32[1,2048]{1,0:T(1,128)S(1)}) custom-call(bf16[128,768]{1,0:T(8,128)(2,1)} %collective-permute-done.refs_0_.refs_1_, bf16[128,768]{1,0:T(8,128)(2,1)} %collective-permute-done.4.refs_1_.refs_2_, bf16[128,768]{1,0:T(8,128)(2,1)} %collective-permute-done.5.refs_2_.refs_5_, ...), custom_call_target="tpu_custom_call" | custom-call | flops 1610612736 | bytes 6029312 | tf_op jit(solution)/shard_map/scores/pallas_call | solution.py:146
  53.8 3.0 %scores.5 = (bf16[256,2048]{1,0:T(8,128)(2,1)}, f32[1,2048]{1,0:T(1,128)S(1)}) custom-call(bf16[128,768]{1,0:T(8,128)(2,1)S(1)} %collective-permute-done.1.refs_0_.refs_3_, bf16[128,768]{1,0:T(8,128)(2,1)S(1)} %collective-permute-done.3.refs_1_.refs_4_, s32[1024,128]{1,0:T(8,128)S(1)} %get-tuple-element.24.refs_1_.refs_4_.refs_2_, ...), custom_call_target="tpu_custom_call" | custom-call | flops 805306368 | bytes 4587520 | tf_op jit(solution)/shard_map/scores/pallas_call | solution.py:146
  57.6 4.8 %all-to-all-start.1 = ((f32[8,2,2048]{2,1,0:T(2,128)}), f32[8,2,2048]{2,1,0:T(2,128)S(1)}, u32[]{:S(2)}, u32[]{:S(2)}) async-start(f32[8,2,2048]{2,1,0:T(2,128)} %tile.5), calls=%async_computation.1 | async-start | bytes 262144 | tf_op jit(solution)/shard_map/all_to_all | solution.py:225
  62.5 7.6 %weights.1 = (bf16[4,96,2048]{2,1,0:T(8,128)(2,1)}, bf16[4,96,2048]{2,1,0:T(8,128)(2,1)}) custom-call(s32[1]{0:T(128)} %bitcast.11.core_ref, bf16[256,768]{1,0:T(8,128)(2,1)} %bitcast.32, bf16[128,768]{1,0:T(8,128)(2,1)} %collective-permute-done.refs_0_.refs_1_, bf16[128,768]{1,0:T(8,128)(2,1)} %collective-permute-done.4.refs_1_.refs_2_, ...), custom_call_target="tpu_custom_call" | custom-call | flops 3221225472 | bytes 8912896 | tf_op jit(solution)/shard_map/weights/pallas_call | solution.py:197
  72.3 1.0 fusion.8
  74.6 3.3 %collective-permute-start.12 = (bf16[128,768]{1,0:T(8,128)(2,1)S(1)}, bf16[128,768]{1,0:T(8,128)(2,1)S(1)}, u32[]{:S(2)}, u32[]{:S(2)}) collective-permute-start(bf16[128,768]{1,0:T(8,128)(2,1)S(1)} %slice.90), channel_id=1, source_target_pairs={{0,24},{8,0},{16,8},{24,16},{1,25},{9,1},{17,9},{25,17},{2,26},{10... | collective-permute-start | bytes 589832 | tf_op jit(solution)/shard_map/ppermute | solution.py:221
  77.9 1.0 convolution_convert_fusion
  79.3 3.2 %collective-permute-start.14 = (bf16[128,768]{1,0:T(8,128)(2,1)S(1)}, bf16[128,768]{1,0:T(8,128)(2,1)S(1)}, u32[]{:S(2)}, u32[]{:S(2)}) collective-permute-start(bf16[128,768]{1,0:T(8,128)(2,1)S(1)} %get-tuple-element.50), channel_id=1, source_target_pairs={{0,24},{8,0},{16,8},{24,16},{1,25},{9,1},{17,9},{25,17},{2,26},{10... | collective-permute-start | bytes 589832 | tf_op jit(solution)/shard_map/ppermute | solution.py:221
  83.5 4.0 %collective-permute-done.10 = bf16[128,768]{1,0:T(8,128)(2,1)S(1)} collective-permute-done((bf16[128,768]{1,0:T(8,128)(2,1)S(1)}, bf16[128,768]{1,0:T(8,128)(2,1)S(1)}, u32[]{:S(2)}, u32[]{:S(2)}) %collective-permute-start.10) | collective-permute-done | bytes 196640 | tf_op jit(solution)/shard_map/ppermute | solution.py:221
  87.7 3.3 %collective-permute-start.15 = (bf16[128,768]{1,0:T(8,128)(2,1)S(1)}, bf16[128,768]{1,0:T(8,128)(2,1)S(1)}, u32[]{:S(2)}, u32[]{:S(2)}) collective-permute-start(bf16[128,768]{1,0:T(8,128)(2,1)S(1)} %fusion), channel_id=1, source_target_pairs={{0,24},{8,0},{16,8},{24,16},{1,25},{9,1},{17,9},{25,17},{2,26},{10... | collective-permute-start | bytes 589832 | tf_op jit(solution)/shard_map/ppermute | solution.py:221
  91.0 2.0 %add_convert_fusion = bf16[4,96,2048]{2,1,0:T(8,128)(2,1)S(1)} fusion(bf16[4,96,2048]{2,1,0:T(8,128)(2,1)} %collective-permute-done.6, bf16[4,96,2048]{2,1,0:T(8,128)(2,1)S(1)} %copy-done.12), kind=kLoop, calls=%fused_computation.1 | loop fusion | flops 3145728 | bytes 4718592 | tf_op jit(solution)/shard_map/convert_element_type | solution.py:264
  93.1 1.3 %collective-permute-start.7 = (bf16[96,2048]{1,0:T(8,128)(2,1)S(1)}, bf16[96,2048]{1,0:T(8,128)(2,1)S(1)}, u32[]{:S(2)}, u32[]{:S(2)}) collective-permute-start(bf16[96,2048]{1,0:T(8,128)(2,1)S(1)} %get-tuple-element.39), channel_id=1, source_target_pairs={{0,64},{64,128},{128,192},{192,0},{1,65},{65,129},{129,193},{193,1... | collective-permute-start | bytes 1179656 | tf_op jit(solution)/shard_map/ppermute | solution.py:221
  96.9 3.5 %all-to-all-start.2 = ((bf16[8,32,768]{2,1,0:T(8,128)(2,1)}), bf16[8,32,768]{2,1,0:T(8,128)(2,1)S(1)}, u32[]{:S(2)}, u32[]{:S(2)}) async-start(bf16[8,32,768]{2,1,0:T(8,128)(2,1)} %bitcast.17), calls=%async_computation.2 | async-start | bytes 786432 | tf_op jit(solution)/shard_map/all_to_all | solution.py:225
  100.3 4.9 %collective-permute-done.7 = bf16[96,2048]{1,0:T(8,128)(2,1)S(1)} collective-permute-done((bf16[96,2048]{1,0:T(8,128)(2,1)S(1)}, bf16[96,2048]{1,0:T(8,128)(2,1)S(1)}, u32[]{:S(2)}, u32[]{:S(2)}) %collective-permute-start.7) | collective-permute-done | bytes 393248 | tf_op jit(solution)/shard_map/ppermute | solution.py:221
  105.2 6.3 %collective-permute-done.8 = bf16[96,2048]{1,0:T(8,128)(2,1)S(1)} collective-permute-done((bf16[96,2048]{1,0:T(8,128)(2,1)S(1)}, bf16[96,2048]{1,0:T(8,128)(2,1)S(1)}, u32[]{:S(2)}, u32[]{:S(2)}) %collective-permute-start.8) | collective-permute-done | bytes 393248 | tf_op jit(solution)/shard_map/ppermute | solution.py:221
  111.5 1.8 %collective-permute-done.9 = bf16[96,2048]{1,0:T(8,128)(2,1)S(1)} collective-permute-done((bf16[96,2048]{1,0:T(8,128)(2,1)S(1)}, bf16[96,2048]{1,0:T(8,128)(2,1)S(1)}, u32[]{:S(2)}, u32[]{:S(2)}) %collective-permute-start.9) | collective-permute-done | bytes 393248 | tf_op jit(solution)/shard_map/ppermute | solution.py:221
  113.3 1.0 fusion.2
  (78 shorter events, 15.9 us)
Async XLA Ops:
  24.4 29.4 %copy-start.2 = (bf16[8,32,768]{2,1,0:T(8,128)(2,1)}, bf16[8,32,768]{2,1,0:T(8,128)(2,1)S(1)}, u32[]{:S(2)}) copy-start(bf16[8,32,768]{2,1,0:T(8,128)(2,1)S(1)} %all_to_all.19) | copy-start | bytes 1179652
  25.2 16.7 %collective-permute-start = (bf16[128,768]{1,0:T(8,128)(2,1)}, bf16[128,768]{1,0:T(8,128)(2,1)}, u32[]{:S(2)}, u32[]{:S(2)}) collective-permute-start(bf16[128,768]{1,0:T(8,128)(2,1)} %bitcast.8), channel_id=1, source_target_pairs={{0,24},{8,0},{16,8},{24,16},{1,25},{9,1},{17,9},{25,17},{2,26},{10... | collective-permute-start | bytes 589832 | tf_op jit(solution)/shard_map/ppermute | solution.py:221
  28.0 16.0 %collective-permute-start.2 = (bf16[128,768]{1,0:T(8,128)(2,1)}, bf16[128,768]{1,0:T(8,128)(2,1)}, u32[]{:S(2)}, u32[]{:S(2)}) collective-permute-start(bf16[128,768]{1,0:T(8,128)(2,1)} %bitcast.9), channel_id=1, source_target_pairs={{0,8},{8,16},{16,24},{24,0},{1,9},{9,17},{17,25},{25,1},{2,10},{10... | collective-permute-start | bytes 589832 | tf_op jit(solution)/shard_map/ppermute | solution.py:221
  28.0 20.7 %collective-permute-start.5 = (bf16[128,768]{1,0:T(8,128)(2,1)}, bf16[128,768]{1,0:T(8,128)(2,1)}, u32[]{:S(2)}, u32[]{:S(2)}) collective-permute-start(bf16[128,768]{1,0:T(8,128)(2,1)} %bitcast.8), channel_id=1, source_target_pairs={{0,8},{8,16},{16,24},{24,0},{1,9},{9,17},{17,25},{25,1},{2,10},{10... | collective-permute-start | bytes 589832 | tf_op jit(solution)/shard_map/ppermute | solution.py:221
  28.8 19.9 %collective-permute-start.4 = (bf16[128,768]{1,0:T(8,128)(2,1)}, bf16[128,768]{1,0:T(8,128)(2,1)}, u32[]{:S(2)}, u32[]{:S(2)}) collective-permute-start(bf16[128,768]{1,0:T(8,128)(2,1)} %bitcast.9), channel_id=1, source_target_pairs={{0,24},{8,0},{16,8},{24,16},{1,25},{9,1},{17,9},{25,17},{2,26},{10... | collective-permute-start | bytes 589832 | tf_op jit(solution)/shard_map/ppermute | solution.py:221
  41.9 11.9 %copy-start.5 = (f32[3,2048]{1,0:T(4,128)}, f32[3,2048]{1,0:T(4,128)S(1)}, u32[]{:S(2)}) copy-start(f32[3,2048]{1,0:T(4,128)S(1)} %get-tuple-element.25.refs_2_.refs_5_.refs_3_) | copy-start | bytes 73732
  41.9 11.9 %collective-permute-start.1 = (bf16[128,768]{1,0:T(8,128)(2,1)}, bf16[128,768]{1,0:T(8,128)(2,1)S(1)}, u32[]{:S(2)}, u32[]{:S(2)}) collective-permute-start(bf16[128,768]{1,0:T(8,128)(2,1)} %collective-permute-done.refs_0_.refs_1_), channel_id=1, source_target_pairs={{0,24},{8,0},{16,8},{24,16},{1,25},{9,1},{17,9},{25,17},{2,26},{10... | collective-permute-start | bytes 589832 | tf_op jit(solution)/shard_map/ppermute | solution.py:221
  44.0 9.8 %collective-permute-start.3 = (bf16[128,768]{1,0:T(8,128)(2,1)}, bf16[128,768]{1,0:T(8,128)(2,1)S(1)}, u32[]{:S(2)}, u32[]{:S(2)}) collective-permute-start(bf16[128,768]{1,0:T(8,128)(2,1)} %collective-permute-done.2.refs_3_.refs_6_), channel_id=1, source_target_pairs={{0,8},{8,16},{16,24},{24,0},{1,9},{9,17},{17,25},{25,1},{2,10},{10... | collective-permute-start | bytes 589832 | tf_op jit(solution)/shard_map/ppermute | solution.py:221
  48.7 5.2 %copy-start.1 = (bf16[2048,768]{1,0:T(8,128)(2,1)S(1)}, bf16[2048,768]{1,0:T(8,128)(2,1)}, u32[]{:S(2)}) copy-start(bf16[2048,768]{1,0:T(8,128)(2,1)} %refs_4_.1) | copy-start | bytes 9437188
  57.6 12.5 %all-to-all-start.1 = ((f32[8,2,2048]{2,1,0:T(2,128)}), f32[8,2,2048]{2,1,0:T(2,128)S(1)}, u32[]{:S(2)}, u32[]{:S(2)}) async-start(f32[8,2,2048]{2,1,0:T(2,128)} %tile.5), calls=%async_computation.1 | async-start | bytes 262144 | tf_op jit(solution)/shard_map/all_to_all | solution.py:225
  70.0 20.9 %collective-permute-start.6 = (bf16[4,96,2048]{2,1,0:T(8,128)(2,1)}, bf16[4,96,2048]{2,1,0:T(8,128)(2,1)}, u32[]{:S(2)}, u32[]{:S(2)}) collective-permute-start(bf16[4,96,2048]{2,1,0:T(8,128)(2,1)} %get-tuple-element.37), channel_id=1, source_target_pairs={{0,32},{32,0},{1,33},{33,1},{2,34},{34,2},{3,35},{35,3},{4,36},{36... | collective-permute-start | bytes 4718600 | tf_op jit(solution)/shard_map/ppermute | solution.py:221
  71.0 42.3 %copy-start.13 = (f32[1,2048]{1,0:T(1,128)}, f32[1,2048]{1,0:T(1,128)S(1)}, u32[]{:S(2)}) copy-start(f32[1,2048]{1,0:T(1,128)S(1)} %fusion.3) | copy-start | bytes 24580
  74.5 8.0 %copy-start.14 = (bf16[256,2048]{1,0:T(8,128)(2,1)S(1)}, bf16[256,2048]{1,0:T(8,128)(2,1)}, u32[]{:S(2)}) copy-start(bf16[256,2048]{1,0:T(8,128)(2,1)} %get-tuple-element.32.refs_7_) | copy-start | bytes 3145732
  74.5 19.8 %collective-permute-start.13 = (bf16[128,768]{1,0:T(8,128)(2,1)S(1)}, bf16[128,768]{1,0:T(8,128)(2,1)S(1)}, u32[]{:S(2)}, u32[]{:S(2)}) collective-permute-start(bf16[128,768]{1,0:T(8,128)(2,1)S(1)} %slice.89), channel_id=1, source_target_pairs={{0,8},{8,16},{16,24},{24,0},{1,9},{9,17},{17,25},{25,1},{2,10},{10... | collective-permute-start | bytes 589832 | tf_op jit(solution)/shard_map/ppermute | solution.py:221
  74.6 20.6 %collective-permute-start.12 = (bf16[128,768]{1,0:T(8,128)(2,1)S(1)}, bf16[128,768]{1,0:T(8,128)(2,1)S(1)}, u32[]{:S(2)}, u32[]{:S(2)}) collective-permute-start(bf16[128,768]{1,0:T(8,128)(2,1)S(1)} %slice.90), channel_id=1, source_target_pairs={{0,24},{8,0},{16,8},{24,16},{1,25},{9,1},{17,9},{25,17},{2,26},{10... | collective-permute-start | bytes 589832 | tf_op jit(solution)/shard_map/ppermute | solution.py:221
  78.9 8.6 %collective-permute-start.10 = (bf16[128,768]{1,0:T(8,128)(2,1)S(1)}, bf16[128,768]{1,0:T(8,128)(2,1)S(1)}, u32[]{:S(2)}, u32[]{:S(2)}) collective-permute-start(bf16[128,768]{1,0:T(8,128)(2,1)S(1)} %get-tuple-element.49), channel_id=1, source_target_pairs={{0,8},{8,16},{16,24},{24,0},{1,9},{9,17},{17,25},{25,1},{2,10},{10... | collective-permute-start | bytes 589832 | tf_op jit(solution)/shard_map/ppermute | solution.py:221
  79.2 11.7 %copy-start.12 = (bf16[4,96,2048]{2,1,0:T(8,128)(2,1)S(1)}, bf16[4,96,2048]{2,1,0:T(8,128)(2,1)}, u32[]{:S(2)}) copy-start(bf16[4,96,2048]{2,1,0:T(8,128)(2,1)} %get-tuple-element.36) | copy-start | bytes 4718596
  79.3 8.4 %collective-permute-start.14 = (bf16[128,768]{1,0:T(8,128)(2,1)S(1)}, bf16[128,768]{1,0:T(8,128)(2,1)S(1)}, u32[]{:S(2)}, u32[]{:S(2)}) collective-permute-start(bf16[128,768]{1,0:T(8,128)(2,1)S(1)} %get-tuple-element.50), channel_id=1, source_target_pairs={{0,24},{8,0},{16,8},{24,16},{1,25},{9,1},{17,9},{25,17},{2,26},{10... | collective-permute-start | bytes 589832 | tf_op jit(solution)/shard_map/ppermute | solution.py:221
  87.5 8.4 %collective-permute-start.11 = (bf16[128,768]{1,0:T(8,128)(2,1)S(1)}, bf16[128,768]{1,0:T(8,128)(2,1)S(1)}, u32[]{:S(2)}, u32[]{:S(2)}) collective-permute-start(bf16[128,768]{1,0:T(8,128)(2,1)S(1)} %fusion.1), channel_id=1, source_target_pairs={{0,8},{8,16},{16,24},{24,0},{1,9},{9,17},{17,25},{25,1},{2,10},{10... | collective-permute-start | bytes 589832 | tf_op jit(solution)/shard_map/ppermute | solution.py:221
  87.7 8.3 %collective-permute-start.15 = (bf16[128,768]{1,0:T(8,128)(2,1)S(1)}, bf16[128,768]{1,0:T(8,128)(2,1)S(1)}, u32[]{:S(2)}, u32[]{:S(2)}) collective-permute-start(bf16[128,768]{1,0:T(8,128)(2,1)S(1)} %fusion), channel_id=1, source_target_pairs={{0,24},{8,0},{16,8},{24,16},{1,25},{9,1},{17,9},{25,17},{2,26},{10... | collective-permute-start | bytes 589832 | tf_op jit(solution)/shard_map/ppermute | solution.py:221
  93.1 12.1 %collective-permute-start.7 = (bf16[96,2048]{1,0:T(8,128)(2,1)S(1)}, bf16[96,2048]{1,0:T(8,128)(2,1)S(1)}, u32[]{:S(2)}, u32[]{:S(2)}) collective-permute-start(bf16[96,2048]{1,0:T(8,128)(2,1)S(1)} %get-tuple-element.39), channel_id=1, source_target_pairs={{0,64},{64,128},{128,192},{192,0},{1,65},{65,129},{129,193},{193,1... | collective-permute-start | bytes 1179656 | tf_op jit(solution)/shard_map/ppermute | solution.py:221
  94.4 17.1 %collective-permute-start.8 = (bf16[96,2048]{1,0:T(8,128)(2,1)S(1)}, bf16[96,2048]{1,0:T(8,128)(2,1)S(1)}, u32[]{:S(2)}, u32[]{:S(2)}) collective-permute-start(bf16[96,2048]{1,0:T(8,128)(2,1)S(1)} %get-tuple-element.40), channel_id=1, source_target_pairs={{0,128},{64,192},{128,0},{192,64},{1,129},{65,193},{129,1},{193,65... | collective-permute-start | bytes 1179656 | tf_op jit(solution)/shard_map/ppermute | solution.py:221
  95.2 18.1 %collective-permute-start.9 = (bf16[96,2048]{1,0:T(8,128)(2,1)S(1)}, bf16[96,2048]{1,0:T(8,128)(2,1)S(1)}, u32[]{:S(2)}, u32[]{:S(2)}) collective-permute-start(bf16[96,2048]{1,0:T(8,128)(2,1)S(1)} %get-tuple-element.41), channel_id=1, source_target_pairs={{0,192},{64,0},{128,64},{192,128},{1,193},{65,1},{129,65},{193,129... | collective-permute-start | bytes 1179656 | tf_op jit(solution)/shard_map/ppermute | solution.py:221
  96.9 17.4 %all-to-all-start.2 = ((bf16[8,32,768]{2,1,0:T(8,128)(2,1)}), bf16[8,32,768]{2,1,0:T(8,128)(2,1)S(1)}, u32[]{:S(2)}, u32[]{:S(2)}) async-start(bf16[8,32,768]{2,1,0:T(8,128)(2,1)} %bitcast.17), calls=%async_computation.2 | async-start | bytes 786432 | tf_op jit(solution)/shard_map/all_to_all | solution.py:225
  (12 other events, 19.3 us)

commit v4 on v3

--- a/solution.py
+++ b/solution.py
@@ -77,56 +77,70 @@
     )(at, mean, ids, count, bias, prop, bins)
 
 
-def score_kernel(*refs, at, parts, sizes, tile):
+def score_kernel(*refs, at, parts, sizes, tile, stream):
     count = len(at)
     x_refs, refs = refs[: sum(parts)], refs[sum(parts) :]
     words_ref, label_ref, w_ref = refs[:3]
     res_refs, post_ref, refs = refs[3 : count + 3], refs[count + 3], refs[count + 4 :]
     x_in, words_in, slots = refs[:count], refs[count : 2 * count], refs[2 * count : 3 * count]
-    label_in, x_sems, words_sems, label_sem, out_sems = refs[3 * count :]
+    label_in, total_in, x_sems, words_sems, label_sem, out_sems = refs[3 * count :][:6]
     tiles = w_ref.shape[0] // tile
 
-    first = []
+    label = pltpu.make_async_copy(label_ref, label_in, label_sem)
+    label.start()
+    loads = []
+    if stream:
+        w_in, w_sems = refs[3 * count + 6 :]
+        loads = [
+            pltpu.make_async_copy(w_ref.at[t * tile : (t + 1) * tile, :], w_in.at[t], w_sems.at[t])
+            for t in range(tiles)
+        ]
+    needed = []
     n = 0
     for k in range(count):
+        source = words_ref.at[at[k] : at[k] + sizes[k], :]
+        copies = [pltpu.make_async_copy(source, words_in[k], words_sems.at[k])]
         low = 0
         for _ in range(parts[k]):
             size = x_refs[n].shape[0]
             target = x_in[k].at[low : low + size, :]
-            first.append(pltpu.make_async_copy(x_refs[n], target, x_sems.at[n]))
+            copies.append(pltpu.make_async_copy(x_refs[n], target, x_sems.at[n]))
             low, n = low + size, n + 1
-        source = words_ref.at[at[k] : at[k] + sizes[k], :]
-        first.append(pltpu.make_async_copy(source, words_in[k], words_sems.at[k]))
-    first.append(pltpu.make_async_copy(label_ref, label_in, label_sem))
-    for copy in first:
-        copy.start()
-    for copy in first:
-        copy.wait()
+        for copy in copies:
+            copy.start()
+        needed.append(copies)
+        if k == 0:
+            for load in loads:
+                load.start()
+    label.wait()
 
     outs = []
-    for t in range(tiles):
-        cols = slice(t * tile, (t + 1) * tile)
-        bias, prop = label_in[0:1, cols], label_in[1:2, cols]
-        rest = 1.0 - prop
-        total = jnp.zeros((8, tile), F32)
-        for k in range(count):
-            size = sizes[k]
-            scores = mm(x_in[k][...], w_ref[cols, :], ((1,), (1,)))
+    for k in range(count):
+        for copy in needed[k]:
+            copy.wait()
+        for t in range(tiles):
+            cols = slice(t * tile, (t + 1) * tile)
+            bias, prop = label_in[0:1, cols], label_in[1:2, cols]
+            if stream and k == 0:
+                loads[t].wait()
+            w = w_in[t] if stream else w_ref[cols, :]
+            scores = mm(x_in[k][...], w, ((1,), (1,)))
             grown = 1.0 + jnp.exp2(scores * -LOG2E + bias)
             prob = 1.0 / grown
-            unseen = rest / (grown - prop)
+            unseen = (1.0 - prop) / (grown - prop)
             words = words_in[k][...]
             bits = range(t * tile // LANES, (t + 1) * tile // LANES)
             seen = jnp.concatenate([words & (1 << b) for b in bits], axis=1)
             posterior = jnp.where(seen != 0, 1.0, unseen)
             slots[k][t] = (prob - posterior).astype(BF)
-            total = total + jnp.sum(posterior.reshape(size // 8, 8, tile), axis=0)
+            total = jnp.sum(posterior.reshape(sizes[k] // 8, 8, tile), axis=0)
+            total_in[:, cols] = total if k == 0 else total_in[:, cols] + total
             copy = pltpu.make_async_copy(
                 slots[k].at[t], res_refs[k].at[:, cols], out_sems.at[k, t]
             )
             copy.start()
             outs.append(copy)
-        post_ref[:, cols] = jnp.sum(total, axis=0, keepdims=True)
+    post_ref[...] = jnp.sum(total_in[...], axis=0, keepdims=True)
     for copy in outs:
         copy.wait()
 
@@ -135,7 +149,7 @@
     return [pl.BlockSpec(memory_space=pltpu.VMEM)] * count
 
 
-def score_call(groups, at, words, w, label, tile=512):
+def score_call(groups, at, words, w, label, stream, tile=512):
     width, depth = w.shape
     xs = [x for group in groups for x in group]
     sizes = tuple(sum(x.shape[0] for x in group) for group in groups)
@@ -144,22 +158,26 @@
     parts = tuple(len(group) for group in groups)
     dma = pltpu.SemaphoreType.DMA
     *res, post = pl.pallas_call(
-        functools.partial(score_kernel, at=at, parts=parts, sizes=sizes, tile=tile),
-        in_specs=[pl.BlockSpec(memory_space=pltpu.HBM)] * (len(xs) + 2) + in_vmem(1),
+        functools.partial(
+            score_kernel, at=at, parts=parts, sizes=sizes, tile=tile, stream=stream
+        ),
+        in_specs=[pl.BlockSpec(memory_space=pltpu.HBM)] * (len(xs) + 2)
+        + [pl.BlockSpec(memory_space=pltpu.HBM if stream else pltpu.VMEM)],
         out_specs=[pl.BlockSpec(memory_space=pltpu.HBM)] * count + in_vmem(1),
         out_shape=[pltpu.HBM((size, width), BF) for size in sizes]
         + [jax.ShapeDtypeStruct((1, width), F32)],
         scratch_shapes=[pltpu.VMEM((size, depth), BF) for size in sizes]
         + [pltpu.VMEM((size, LANES), jnp.int32) for size in sizes]
         + [pltpu.VMEM((tiles, size, tile), BF) for size in sizes]
-        + [pltpu.VMEM(label.shape, F32)]
-        + [dma((len(xs),)), dma((count,)), dma(()), dma((count, tiles))],
+        + [pltpu.VMEM(label.shape, F32), pltpu.VMEM((8, width), F32)]
+        + [dma((len(xs),)), dma((count,)), dma(()), dma((count, tiles))]
+        + ([pltpu.VMEM((tiles, tile, depth), BF), dma((tiles,))] if stream else []),
         cost_estimate=pl.CostEstimate(
             flops=2 * rows * width * depth,
             bytes_accessed=2 * (rows * depth + width * depth + rows * width),
             transcendentals=3 * rows * width,
         ),
-        compiler_params=pltpu.CompilerParams(vmem_limit_bytes=24 << 20),
+        compiler_params=pltpu.CompilerParams(vmem_limit_bytes=(60 if stream else 24) << 20),
         name="scores",
     )(*xs, words, label, w)
     return res, post
@@ -174,14 +192,14 @@
     def _():
         at = 0
         for x_ref in x_refs:
-            x_all[at : at + x_ref.shape[0], :] = x_ref[...]
+            x_all[:, at : at + x_ref.shape[0]] = x_ref[...].T
             at += x_ref.shape[0]
 
     at = 0
     for r_ref in r_refs:
         r_all[at : at + r_ref.shape[0], :] = r_ref[...]
         at += r_ref.shape[0]
-    out[...] = mm(x_all[...], r_all[...], ((0,), (0,))).astype(BF)
+    out[...] = mm(x_all[...], r_all[...], ((1,), (0,))).astype(BF)
     step = kept_ref.shape[1]
     for y in range(NY):
         kept_ref[y] = out[pl.ds(pl.multiple_of((y * NC + mine) * step, step), step), :]
@@ -203,7 +221,7 @@
         out_specs=[half, half],
         out_shape=[pltpu.HBM((NY, step, width), BF)] * 2,
         scratch_shapes=[
-            pltpu.VMEM((rows, depth), BF),
+            pltpu.VMEM((depth, rows), BF),
             pltpu.VMEM((rows, tile), BF),
             pltpu.VMEM((depth, tile), BF),
         ],
@@ -250,11 +268,12 @@
     front_high, back_low = shift(high, "x", NX, -1), shift(low, "x", NX, 1)
     far = (shift(front_low, "x", NX, -1), shift(back_high, "x", NX, 1))
     front, back = (front_low, front_high), (back_low, back_high)
-    (res0,), post0 = score_call(((own,),), (0,), words, class_weight, label)
-    (res1, res3), post1 = score_call((front, back), (block, 3 * block), words, class_weight, label)
+    (res0, res1, res3), post1 = score_call(
+        ((own,), front, back), (0, block, 3 * block), words, class_weight, label, True
+    )
     far, post1 = lax.optimization_barrier((far, post1))
-    (res2,), post2 = score_call((far,), (2 * block,), words, class_weight, label)
-    post = (post0 + post1) + post2
+    (res2,), post2 = score_call((far,), (2 * block,), words, class_weight, label, False)
+    post = post1 + post2
     both = jnp.concatenate([obs, post], axis=0)[None]
     sums = jnp.sum(exchange(jnp.tile(both, (NY * NC, 1, 1)), ("y", "core")), axis=0)
     updated = ((sums[0:1] + label[2:3]) / (sums[1:2] + 8.0)).reshape(width)

time: 117 us -> 119 us (1.017)
  Pallas kernels: 24.7 us -> 26.1 us
    pallas_call x3 -> x2, Pallas kernels: 10.8 us -> 12 us  [score_call(): pl.pallas_call(functools.partial(score_kernel, at=at, parts=parts, sizes=...]
    unnamed x36 -> x46, local copies, waits for them, and re-layouts: 7.06 us -> 7.3 us
  transfers between devices with their start and end apart: 18 -> 18, of which waited for: 4 -> 4; matrix products, arithmetic and copies ran while one was open for 8% -> 9% of each run, Pallas kernels for 19% -> 20%
where the time goes in v4:
time: 119 us; the launch traced here: 117 us
  starting transfers between devices  29.6 us (25%)
  Pallas kernels  26.1 us (22%)
  blocking collectives  22.9 us (19%)
  waiting for transfers between devices  17.3 us (15%)
  local copies, waits for them, and re-layouts  9.03 us (8%)
  other arithmetic  7.15 us (6%)
  matrix products  3.93 us (3%)
    all_to_all x1, blocking collectives, exchange(): return lax.all_to_all(v, axis, split_axis=0, concat_axis=0, tiled=True)  22.9 us
    ppermute x16, starting transfers between devices, shift(): return lax.ppermute(v, axis, ring(n, d))  21.3 us
    ppermute x16, waiting for transfers between devices, shift(): return lax.ppermute(v, axis, ring(n, d))  17.3 us
    pallas_call x2, Pallas kernels, score_call(): pl.pallas_call(functools.partial(score_kernel, at=at, parts=parts, sizes=...  12 us
    all_to_all x2, starting transfers between devices, exchange(): return lax.all_to_all(v, axis, split_axis=0, concat_axis=0, tiled=True)  8.25 us
    pallas_call x1, Pallas kernels, weight_call(): pl.pallas_call(functools.partial(weight_kernel, count=len(xs)), grid=(wid...  7.95 us
    unnamed x46, local copies, waits for them, and re-layouts  7.3 us
    pallas_call x1, Pallas kernels, words_call(): pl.pallas_call(words_kernel, in_specs=[pl.BlockSpec(memory_space=pltpu.SM...  6.21 us
  transfers between devices with their start and end apart: 18, of which 4 were waited for; matrix products, arithmetic and copies ran while one was open for 9% of the time, Pallas kernels for 20%

profile of v4, /device:TPU:16, one launch (start us, length us, event | category | flops | bytes accessed | tf_op | source)
XLA Modules:
  0.0 117.0 jit_solution(15800402517329540555)
XLA Ops:
  1.5 22.9 %all_to_all.19 = bf16[8,32,768]{2,1,0:T(8,128)(2,1)S(1)} all-to-all(bf16[8,32,768]{2,1,0:T(8,128)(2,1)S(1)} %tile.4), channel_id=1, replica_groups=mesh['y'=4,'core'=2,'x'=4,'z'=8] {'z'}, dimensions={0} | all-to-all | bytes 786432 | tf_op jit(solution)/shard_map/all_to_all | solution.py:243
  24.4 2.8 %collective-permute-start = (bf16[128,768]{1,0:T(8,128)(2,1)S(1)}, bf16[128,768]{1,0:T(8,128)(2,1)}, u32[]{:S(2)}, u32[]{:S(2)}) collective-permute-start(bf16[128,768]{1,0:T(8,128)(2,1)S(1)} %bitcast.40), channel_id=1, source_target_pairs={{0,24},{8,0},{16,8},{24,16},{1,25},{9,1},{17,9},{25,17},{2,26},{10... | collective-permute-start | bytes 589832 | tf_op jit(solution)/shard_map/ppermute | solution.py:239
  28.0 2.5 %collective-permute-start.4 = (bf16[128,768]{1,0:T(8,128)(2,1)S(1)}, bf16[128,768]{1,0:T(8,128)(2,1)S(1)}, u32[]{:S(2)}, u32[]{:S(2)}) collective-permute-start(bf16[128,768]{1,0:T(8,128)(2,1)S(1)} %bitcast.39), channel_id=1, source_target_pairs={{0,24},{8,0},{16,8},{24,16},{1,25},{9,1},{17,9},{25,17},{2,26},{10... | collective-permute-start | bytes 589832 | tf_op jit(solution)/shard_map/ppermute | solution.py:239
  35.0 6.2 %words.1 = (s32[1024,128]{1,0:T(8,128)S(1)}, f32[1,2048]{1,0:T(1,128)S(1)}, f32[3,2048]{1,0:T(4,128)S(1)}) custom-call(s32[2]{0:T(128)S(1)} %pad_add_fusion.at_ref, f32[16]{0:T(128)S(1)} %copy-done.12, s32[32,1024]{1,0:T(8,128)S(1)} %bitcast.31, s32[1,1024]{1,0:T(1,128)S(1)} %bitcast.35, f32[1,2048]{1,0:T(1,128)S(1)} %bitcast.32, f32[1,2048]{1,0:T(1,128)S(1)} %bitcast.33, ...), custom_call_target="tpu_custom_call" | custom-call | flops 26214400 | bytes 1048576 | tf_op jit(solution)/shard_map/words/pallas_call | solution.py:63
  42.6 2.0 %collective-permute-start.1 = (bf16[128,768]{1,0:T(8,128)(2,1)}, bf16[128,768]{1,0:T(8,128)(2,1)S(1)}, u32[]{:S(2)}, u32[]{:S(2)}) collective-permute-start(bf16[128,768]{1,0:T(8,128)(2,1)} %collective-permute-done.refs_1_), channel_id=1, source_target_pairs={{0,24},{8,0},{16,8},{24,16},{1,25},{9,1},{17,9},{25,17},{2,26},{10... | collective-permute-start | bytes 589832 | tf_op jit(solution)/shard_map/ppermute | solution.py:239
  45.4 8.9 %scores.2 = (bf16[256,2048]{1,0:T(8,128)(2,1)}, bf16[256,2048]{1,0:T(8,128)(2,1)}, bf16[256,2048]{1,0:T(8,128)(2,1)}, f32[1,2048]{1,0:T(1,128)}) custom-call(bf16[256,768]{1,0:T(8,128)(2,1)} %bitcast.36, bf16[128,768]{1,0:T(8,128)(2,1)} %collective-permute-done.refs_1_, bf16[128,768]{1,0:T(8,128)(2,1)} %copy-done.19, bf16[128,768]{1,0:T(8,128)(2,1)} %copy-done.18, ...), custom_call_target="tpu_custom_call" | custom-call | flops 2415919104 | bytes 7471104 | tf_op jit(solution)/shard_map/scores/pallas_call | solution.py:160
  54.4 3.0 %scores.3 = (bf16[256,2048]{1,0:T(8,128)(2,1)}, f32[1,2048]{1,0:T(1,128)S(1)}) custom-call(bf16[128,768]{1,0:T(8,128)(2,1)S(1)} %collective-permute-done.1.refs_0_.refs_3_, bf16[128,768]{1,0:T(8,128)(2,1)S(1)} %collective-permute-done.3.refs_1_.refs_4_, s32[1024,128]{1,0:T(8,128)S(1)} %copy-done.2, f32[3,2048]{1,0:T(4,128)S(1)} %copy-done.7, ...), custom_call_target="tpu_custom_call" | custom-call | flops 805306368 | bytes 4587520 | tf_op jit(solution)/shard_map/scores/pallas_call | solution.py:160
  58.2 4.8 %all-to-all-start.1 = ((f32[8,2,2048]{2,1,0:T(2,128)}), f32[8,2,2048]{2,1,0:T(2,128)}, u32[]{:S(2)}, u32[]{:S(2)}) async-start(f32[8,2,2048]{2,1,0:T(2,128)} %tile.5), calls=%async_computation.1 | async-start | bytes 262144 | tf_op jit(solution)/shard_map/all_to_all | solution.py:243
  63.0 8.0 %weights.1 = (bf16[4,96,2048]{2,1,0:T(8,128)(2,1)}, bf16[4,96,2048]{2,1,0:T(8,128)(2,1)}) custom-call(s32[1]{0:T(128)} %bitcast.11.core_ref, bf16[256,768]{1,0:T(8,128)(2,1)} %bitcast.37, bf16[128,768]{1,0:T(8,128)(2,1)} %collective-permute-done.refs_1_, bf16[128,768]{1,0:T(8,128)(2,1)} %copy-done.19, bf16[128,768]{1,0:T(8,128)(2,1)} %copy-done.3, ...), custom_call_target="tpu_custom_call" | custom-call | flops 3221225472 | bytes 8912896 | tf_op jit(solution)/shard_map/weights/pallas_call | solution.py:215
  74.1 1.0 fusion.8
  75.3 1.0 fusion.7
  76.5 3.5 %collective-permute-start.12 = (bf16[128,768]{1,0:T(8,128)(2,1)S(1)}, bf16[128,768]{1,0:T(8,128)(2,1)S(1)}, u32[]{:S(2)}, u32[]{:S(2)}) collective-permute-start(bf16[128,768]{1,0:T(8,128)(2,1)S(1)} %slice.90), channel_id=1, source_target_pairs={{0,24},{8,0},{16,8},{24,16},{1,25},{9,1},{17,9},{25,17},{2,26},{10... | collective-permute-start | bytes 589832 | tf_op jit(solution)/shard_map/ppermute | solution.py:239
  80.0 1.0 convolution_convert_fusion
  81.1 3.2 %collective-permute-start.14 = (bf16[128,768]{1,0:T(8,128)(2,1)S(1)}, bf16[128,768]{1,0:T(8,128)(2,1)S(1)}, u32[]{:S(2)}, u32[]{:S(2)}) collective-permute-start(bf16[128,768]{1,0:T(8,128)(2,1)S(1)} %get-tuple-element.48), channel_id=1, source_target_pairs={{0,24},{8,0},{16,8},{24,16},{1,25},{9,1},{17,9},{25,17},{2,26},{10... | collective-permute-start | bytes 589832 | tf_op jit(solution)/shard_map/ppermute | solution.py:239
  84.3 1.0 fusion.6
  85.3 4.0 %collective-permute-done.10 = bf16[128,768]{1,0:T(8,128)(2,1)S(1)} collective-permute-done((bf16[128,768]{1,0:T(8,128)(2,1)S(1)}, bf16[128,768]{1,0:T(8,128)(2,1)S(1)}, u32[]{:S(2)}, u32[]{:S(2)}) %collective-permute-start.10) | collective-permute-done | bytes 196640 | tf_op jit(solution)/shard_map/ppermute | solution.py:239
  89.5 3.3 %collective-permute-start.15 = (bf16[128,768]{1,0:T(8,128)(2,1)S(1)}, bf16[128,768]{1,0:T(8,128)(2,1)S(1)}, u32[]{:S(2)}, u32[]{:S(2)}) collective-permute-start(bf16[128,768]{1,0:T(8,128)(2,1)S(1)} %fusion), channel_id=1, source_target_pairs={{0,24},{8,0},{16,8},{24,16},{1,25},{9,1},{17,9},{25,17},{2,26},{10... | collective-permute-start | bytes 589832 | tf_op jit(solution)/shard_map/ppermute | solution.py:239
  92.8 2.0 %add_convert_fusion = bf16[4,96,2048]{2,1,0:T(8,128)(2,1)S(1)} fusion(bf16[4,96,2048]{2,1,0:T(8,128)(2,1)} %collective-permute-done.6, bf16[4,96,2048]{2,1,0:T(8,128)(2,1)S(1)} %copy-done.14), kind=kLoop, calls=%fused_computation.1 | loop fusion | flops 3145728 | bytes 4718592 | tf_op jit(solution)/shard_map/convert_element_type | solution.py:283
  94.9 1.2 %collective-permute-start.7 = (bf16[96,2048]{1,0:T(8,128)(2,1)S(1)}, bf16[96,2048]{1,0:T(8,128)(2,1)S(1)}, u32[]{:S(2)}, u32[]{:S(2)}) collective-permute-start(bf16[96,2048]{1,0:T(8,128)(2,1)S(1)} %get-tuple-element.37), channel_id=1, source_target_pairs={{0,64},{64,128},{128,192},{192,0},{1,65},{65,129},{129,193},{193,1... | collective-permute-start | bytes 1179656 | tf_op jit(solution)/shard_map/ppermute | solution.py:239
  98.7 3.5 %all-to-all-start.2 = ((bf16[8,32,768]{2,1,0:T(8,128)(2,1)}), bf16[8,32,768]{2,1,0:T(8,128)(2,1)S(1)}, u32[]{:S(2)}, u32[]{:S(2)}) async-start(bf16[8,32,768]{2,1,0:T(8,128)(2,1)} %bitcast.17), calls=%async_computation.2 | async-start | bytes 786432 | tf_op jit(solution)/shard_map/all_to_all | solution.py:243
  102.1 4.9 %collective-permute-done.7 = bf16[96,2048]{1,0:T(8,128)(2,1)S(1)} collective-permute-done((bf16[96,2048]{1,0:T(8,128)(2,1)S(1)}, bf16[96,2048]{1,0:T(8,128)(2,1)S(1)}, u32[]{:S(2)}, u32[]{:S(2)}) %collective-permute-start.7) | collective-permute-done | bytes 393248 | tf_op jit(solution)/shard_map/ppermute | solution.py:239
  107.0 6.5 %collective-permute-done.8 = bf16[96,2048]{1,0:T(8,128)(2,1)S(1)} collective-permute-done((bf16[96,2048]{1,0:T(8,128)(2,1)S(1)}, bf16[96,2048]{1,0:T(8,128)(2,1)S(1)}, u32[]{:S(2)}, u32[]{:S(2)}) %collective-permute-start.8) | collective-permute-done | bytes 393248 | tf_op jit(solution)/shard_map/ppermute | solution.py:239
  113.5 1.8 %collective-permute-done.9 = bf16[96,2048]{1,0:T(8,128)(2,1)S(1)} collective-permute-done((bf16[96,2048]{1,0:T(8,128)(2,1)S(1)}, bf16[96,2048]{1,0:T(8,128)(2,1)S(1)}, u32[]{:S(2)}, u32[]{:S(2)}) %collective-permute-start.9) | collective-permute-done | bytes 393248 | tf_op jit(solution)/shard_map/ppermute | solution.py:239
  115.3 1.0 fusion.2
  (87 shorter events, 15.9 us)
Async XLA Ops:
  24.4 20.2 %copy-start.13 = (bf16[8,32,768]{2,1,0:T(8,128)(2,1)}, bf16[8,32,768]{2,1,0:T(8,128)(2,1)S(1)}, u32[]{:S(2)}) copy-start(bf16[8,32,768]{2,1,0:T(8,128)(2,1)S(1)} %all_to_all.19) | copy-start | bytes 1179652
  24.4 18.1 %collective-permute-start = (bf16[128,768]{1,0:T(8,128)(2,1)S(1)}, bf16[128,768]{1,0:T(8,128)(2,1)}, u32[]{:S(2)}, u32[]{:S(2)}) collective-permute-start(bf16[128,768]{1,0:T(8,128)(2,1)S(1)} %bitcast.40), channel_id=1, source_target_pairs={{0,24},{8,0},{16,8},{24,16},{1,25},{9,1},{17,9},{25,17},{2,26},{10... | collective-permute-start | bytes 589832 | tf_op jit(solution)/shard_map/ppermute | solution.py:239
  27.3 17.3 %collective-permute-start.2 = (bf16[128,768]{1,0:T(8,128)(2,1)S(1)}, bf16[128,768]{1,0:T(8,128)(2,1)}, u32[]{:S(2)}, u32[]{:S(2)}) collective-permute-start(bf16[128,768]{1,0:T(8,128)(2,1)S(1)} %bitcast.38), channel_id=1, source_target_pairs={{0,8},{8,16},{16,24},{24,0},{1,9},{9,17},{17,25},{25,1},{2,10},{10... | collective-permute-start | bytes 589832 | tf_op jit(solution)/shard_map/ppermute | solution.py:239
  27.3 17.3 %collective-permute-start.5 = (bf16[128,768]{1,0:T(8,128)(2,1)S(1)}, bf16[128,768]{1,0:T(8,128)(2,1)S(1)}, u32[]{:S(2)}, u32[]{:S(2)}) collective-permute-start(bf16[128,768]{1,0:T(8,128)(2,1)S(1)} %bitcast.41), channel_id=1, source_target_pairs={{0,8},{8,16},{16,24},{24,0},{1,9},{9,17},{17,25},{25,1},{2,10},{10... | collective-permute-start | bytes 589832 | tf_op jit(solution)/shard_map/ppermute | solution.py:239
  28.0 16.6 %collective-permute-start.4 = (bf16[128,768]{1,0:T(8,128)(2,1)S(1)}, bf16[128,768]{1,0:T(8,128)(2,1)S(1)}, u32[]{:S(2)}, u32[]{:S(2)}) collective-permute-start(bf16[128,768]{1,0:T(8,128)(2,1)S(1)} %bitcast.39), channel_id=1, source_target_pairs={{0,24},{8,0},{16,8},{24,16},{1,25},{9,1},{17,9},{25,17},{2,26},{10... | collective-permute-start | bytes 589832 | tf_op jit(solution)/shard_map/ppermute | solution.py:239
  42.6 11.8 %collective-permute-start.1 = (bf16[128,768]{1,0:T(8,128)(2,1)}, bf16[128,768]{1,0:T(8,128)(2,1)S(1)}, u32[]{:S(2)}, u32[]{:S(2)}) collective-permute-start(bf16[128,768]{1,0:T(8,128)(2,1)} %collective-permute-done.refs_1_), channel_id=1, source_target_pairs={{0,24},{8,0},{16,8},{24,16},{1,25},{9,1},{17,9},{25,17},{2,26},{10... | collective-permute-start | bytes 589832 | tf_op jit(solution)/shard_map/ppermute | solution.py:239
  44.6 9.8 %collective-permute-start.3 = (bf16[128,768]{1,0:T(8,128)(2,1)}, bf16[128,768]{1,0:T(8,128)(2,1)S(1)}, u32[]{:S(2)}, u32[]{:S(2)}) collective-permute-start(bf16[128,768]{1,0:T(8,128)(2,1)} %collective-permute-done.2.refs_4_.refs_6_), channel_id=1, source_target_pairs={{0,8},{8,16},{16,24},{24,0},{1,9},{9,17},{17,25},{25,1},{2,10},{10... | collective-permute-start | bytes 589832 | tf_op jit(solution)/shard_map/ppermute | solution.py:239
  45.4 9.0 %copy-start = (bf16[2048,768]{1,0:T(8,128)(2,1)S(1)}, bf16[2048,768]{1,0:T(8,128)(2,1)}, u32[]{:S(2)}) copy-start(bf16[2048,768]{1,0:T(8,128)(2,1)} %refs_4_.1) | copy-start | bytes 9437188
  45.4 9.0 %copy-start.2 = (s32[1024,128]{1,0:T(8,128)S(1)}, s32[1024,128]{1,0:T(8,128)}, u32[]{:S(2)}) copy-start(s32[1024,128]{1,0:T(8,128)} %copy-done.1) | copy-start | bytes 1572868
  45.4 9.0 %copy-start.7 = (f32[3,2048]{1,0:T(4,128)S(1)}, f32[3,2048]{1,0:T(4,128)}, u32[]{:S(2)}) copy-start(f32[3,2048]{1,0:T(4,128)} %copy-done.6) | copy-start | bytes 73732
  58.2 12.9 %all-to-all-start.1 = ((f32[8,2,2048]{2,1,0:T(2,128)}), f32[8,2,2048]{2,1,0:T(2,128)}, u32[]{:S(2)}, u32[]{:S(2)}) async-start(f32[8,2,2048]{2,1,0:T(2,128)} %tile.5), calls=%async_computation.1 | async-start | bytes 262144 | tf_op jit(solution)/shard_map/all_to_all | solution.py:243
  71.0 21.8 %collective-permute-start.6 = (bf16[4,96,2048]{2,1,0:T(8,128)(2,1)}, bf16[4,96,2048]{2,1,0:T(8,128)(2,1)}, u32[]{:S(2)}, u32[]{:S(2)}) collective-permute-start(bf16[4,96,2048]{2,1,0:T(8,128)(2,1)} %get-tuple-element.35), channel_id=1, source_target_pairs={{0,32},{32,0},{1,33},{33,1},{2,34},{34,2},{3,35},{35,3},{4,36},{36... | collective-permute-start | bytes 4718600 | tf_op jit(solution)/shard_map/ppermute | solution.py:239
  72.8 42.5 %copy-start.15 = (f32[1,2048]{1,0:T(1,128)}, f32[1,2048]{1,0:T(1,128)S(1)}, u32[]{:S(2)}) copy-start(f32[1,2048]{1,0:T(1,128)S(1)} %fusion.3) | copy-start | bytes 24580
  76.4 19.8 %collective-permute-start.13 = (bf16[128,768]{1,0:T(8,128)(2,1)S(1)}, bf16[128,768]{1,0:T(8,128)(2,1)S(1)}, u32[]{:S(2)}, u32[]{:S(2)}) collective-permute-start(bf16[128,768]{1,0:T(8,128)(2,1)S(1)} %slice.89), channel_id=1, source_target_pairs={{0,8},{8,16},{16,24},{24,0},{1,9},{9,17},{17,25},{25,1},{2,10},{10... | collective-permute-start | bytes 589832 | tf_op jit(solution)/shard_map/ppermute | solution.py:239
  76.5 20.6 %collective-permute-start.12 = (bf16[128,768]{1,0:T(8,128)(2,1)S(1)}, bf16[128,768]{1,0:T(8,128)(2,1)S(1)}, u32[]{:S(2)}, u32[]{:S(2)}) collective-permute-start(bf16[128,768]{1,0:T(8,128)(2,1)S(1)} %slice.90), channel_id=1, source_target_pairs={{0,24},{8,0},{16,8},{24,16},{1,25},{9,1},{17,9},{25,17},{2,26},{10... | collective-permute-start | bytes 589832 | tf_op jit(solution)/shard_map/ppermute | solution.py:239
  81.0 8.3 %collective-permute-start.10 = (bf16[128,768]{1,0:T(8,128)(2,1)S(1)}, bf16[128,768]{1,0:T(8,128)(2,1)S(1)}, u32[]{:S(2)}, u32[]{:S(2)}) collective-permute-start(bf16[128,768]{1,0:T(8,128)(2,1)S(1)} %get-tuple-element.47), channel_id=1, source_target_pairs={{0,8},{8,16},{16,24},{24,0},{1,9},{9,17},{17,25},{25,1},{2,10},{10... | collective-permute-start | bytes 589832 | tf_op jit(solution)/shard_map/ppermute | solution.py:239
  81.1 11.7 %copy-start.14 = (bf16[4,96,2048]{2,1,0:T(8,128)(2,1)S(1)}, bf16[4,96,2048]{2,1,0:T(8,128)(2,1)}, u32[]{:S(2)}) copy-start(bf16[4,96,2048]{2,1,0:T(8,128)(2,1)} %get-tuple-element.34) | copy-start | bytes 4718596
  81.1 8.4 %collective-permute-start.14 = (bf16[128,768]{1,0:T(8,128)(2,1)S(1)}, bf16[128,768]{1,0:T(8,128)(2,1)S(1)}, u32[]{:S(2)}, u32[]{:S(2)}) collective-permute-start(bf16[128,768]{1,0:T(8,128)(2,1)S(1)} %get-tuple-element.48), channel_id=1, source_target_pairs={{0,24},{8,0},{16,8},{24,16},{1,25},{9,1},{17,9},{25,17},{2,26},{10... | collective-permute-start | bytes 589832 | tf_op jit(solution)/shard_map/ppermute | solution.py:239
  89.4 8.4 %collective-permute-start.11 = (bf16[128,768]{1,0:T(8,128)(2,1)S(1)}, bf16[128,768]{1,0:T(8,128)(2,1)S(1)}, u32[]{:S(2)}, u32[]{:S(2)}) collective-permute-start(bf16[128,768]{1,0:T(8,128)(2,1)S(1)} %fusion.1), channel_id=1, source_target_pairs={{0,8},{8,16},{16,24},{24,0},{1,9},{9,17},{17,25},{25,1},{2,10},{10... | collective-permute-start | bytes 589832 | tf_op jit(solution)/shard_map/ppermute | solution.py:239
  89.5 8.3 %collective-permute-start.15 = (bf16[128,768]{1,0:T(8,128)(2,1)S(1)}, bf16[128,768]{1,0:T(8,128)(2,1)S(1)}, u32[]{:S(2)}, u32[]{:S(2)}) collective-permute-start(bf16[128,768]{1,0:T(8,128)(2,1)S(1)} %fusion), channel_id=1, source_target_pairs={{0,24},{8,0},{16,8},{24,16},{1,25},{9,1},{17,9},{25,17},{2,26},{10... | collective-permute-start | bytes 589832 | tf_op jit(solution)/shard_map/ppermute | solution.py:239
  94.9 12.1 %collective-permute-start.7 = (bf16[96,2048]{1,0:T(8,128)(2,1)S(1)}, bf16[96,2048]{1,0:T(8,128)(2,1)S(1)}, u32[]{:S(2)}, u32[]{:S(2)}) collective-permute-start(bf16[96,2048]{1,0:T(8,128)(2,1)S(1)} %get-tuple-element.37), channel_id=1, source_target_pairs={{0,64},{64,128},{128,192},{192,0},{1,65},{65,129},{129,193},{193,1... | collective-permute-start | bytes 1179656 | tf_op jit(solution)/shard_map/ppermute | solution.py:239
  96.2 17.3 %collective-permute-start.8 = (bf16[96,2048]{1,0:T(8,128)(2,1)S(1)}, bf16[96,2048]{1,0:T(8,128)(2,1)S(1)}, u32[]{:S(2)}, u32[]{:S(2)}) collective-permute-start(bf16[96,2048]{1,0:T(8,128)(2,1)S(1)} %get-tuple-element.38), channel_id=1, source_target_pairs={{0,128},{64,192},{128,0},{192,64},{1,129},{65,193},{129,1},{193,65... | collective-permute-start | bytes 1179656 | tf_op jit(solution)/shard_map/ppermute | solution.py:239
  97.0 18.3 %collective-permute-start.9 = (bf16[96,2048]{1,0:T(8,128)(2,1)S(1)}, bf16[96,2048]{1,0:T(8,128)(2,1)S(1)}, u32[]{:S(2)}, u32[]{:S(2)}) collective-permute-start(bf16[96,2048]{1,0:T(8,128)(2,1)S(1)} %get-tuple-element.39), channel_id=1, source_target_pairs={{0,192},{64,0},{128,64},{192,128},{1,193},{65,1},{129,65},{193,129... | collective-permute-start | bytes 1179656 | tf_op jit(solution)/shard_map/ppermute | solution.py:239
  98.7 17.7 %all-to-all-start.2 = ((bf16[8,32,768]{2,1,0:T(8,128)(2,1)}), bf16[8,32,768]{2,1,0:T(8,128)(2,1)S(1)}, u32[]{:S(2)}, u32[]{:S(2)}) async-start(bf16[8,32,768]{2,1,0:T(8,128)(2,1)} %bitcast.17), calls=%async_computation.2 | async-start | bytes 786432 | tf_op jit(solution)/shard_map/all_to_all | solution.py:243
  (17 other events, 42.7 us)

commit v5 on v1

--- a/solution.py
+++ b/solution.py
@@ -22,8 +22,18 @@
     return lax.dot_general(a, b, (dims, ((), ())), preferred_element_type=F32)
 
 
-def words_kernel(at_ref, ids_ref, count_ref, words_ref, obs_ref, *, width):
+def words_kernel(
+    at_ref, mean_ref, ids_ref, count_ref, bias_ref, prop_ref, bins_ref, words_ref, obs_ref, label_ref
+):
     slots, rows = ids_ref.shape
+    width = bias_ref.shape[1]
+    label_ref[0:1, :] = bias_ref[...] * -LOG2E
+    label_ref[1:2, :] = prop_ref[...]
+    bins = bins_ref[...]
+    prior = jnp.zeros((1, width), F32)
+    for b in range(mean_ref.shape[0]):
+        prior = prior + jnp.where(bins == b, mean_ref[b], 0.0)
+    label_ref[2:3, :] = 8.0 * prior
     lanes = lax.broadcasted_iota(jnp.int32, (LANES, LANES), 1)
     slot = lax.broadcasted_iota(jnp.int32, (slots, LANES), 0)
     counts = [jnp.zeros((8, LANES), jnp.int32) for _ in range(width // LANES)]
@@ -48,37 +58,37 @@
         )
 
 
-def words_call(at, ids, count, width):
-    rows = ids.shape[1]
+def words_call(at, mean, ids, count, bias, prop, bins):
+    rows, width = ids.shape[1], bias.shape[1]
     return pl.pallas_call(
-        functools.partial(words_kernel, width=width),
-        in_specs=[pl.BlockSpec(memory_space=pltpu.SMEM)] + in_vmem(2),
-        out_specs=in_vmem(2),
+        words_kernel,
+        in_specs=[pl.BlockSpec(memory_space=pltpu.SMEM)] * 2 + in_vmem(5),
+        out_specs=in_vmem(3),
         out_shape=[
             jax.ShapeDtypeStruct((rows, LANES), jnp.int32),
             jax.ShapeDtypeStruct((1, width), F32),
+            jax.ShapeDtypeStruct((3, width), F32),
         ],
         cost_estimate=pl.CostEstimate(
             flops=200 * rows * LANES, bytes_accessed=8 * rows * LANES, transcendentals=0
         ),
         compiler_params=pltpu.CompilerParams(vmem_limit_bytes=16 << 20),
         name="words",
-    )(at, ids, count)
+    )(at, mean, ids, count, bias, prop, bins)
 
 
 def score_kernel(*refs, at, parts, tile):
     count = len(at)
     x_refs, refs = refs[: sum(parts)], refs[sum(parts) :]
-    words_ref, w_ref, bias_ref, prop_ref = refs[:4]
-    res_refs, post_ref = refs[4 : count + 4], refs[count + 4]
-    slots, sems = refs[count + 5 : 2 * count + 5], refs[2 * count + 5]
+    words_ref, w_ref, label_ref = refs[:3]
+    res_refs, post_ref = refs[3 : count + 3], refs[count + 3]
+    slots, sems = refs[count + 4 : 2 * count + 4], refs[2 * count + 4]
     starts = [sum(parts[:k]) for k in range(count)]
     blocks = [x_refs[s : s + p] for s, p in zip(starts, parts)]
     copies = []
     for t in range(w_ref.shape[0] // tile):
         cols = slice(t * tile, (t + 1) * tile)
-        bias = bias_ref[:, cols] * -LOG2E
-        prop = prop_ref[:, cols]
+        bias, prop = label_ref[0:1, cols], label_ref[1:2, cols]
         rest = 1.0 - prop
         total = jnp.zeros((8, tile), F32)
         for k in range(count):
@@ -106,7 +116,7 @@
     return [pl.BlockSpec(memory_space=pltpu.VMEM)] * count
 
 
-def score_call(groups, at, words, w, bias, prop, tile=512):
+def score_call(groups, at, words, w, label, tile=512):
     width, depth = w.shape
     xs = [x for group in groups for x in group]
     sizes = [sum(x.shape[0] for x in group) for group in groups]
@@ -115,7 +125,7 @@
     parts = tuple(len(group) for group in groups)
     *res, post = pl.pallas_call(
         functools.partial(score_kernel, at=at, parts=parts, tile=tile),
-        in_specs=in_vmem(len(xs) + 4),
+        in_specs=in_vmem(len(xs) + 3),
         out_specs=[pl.BlockSpec(memory_space=pltpu.HBM)] * len(sizes) + in_vmem(1),
         out_shape=[pltpu.HBM((size, width), BF) for size in sizes]
         + [jax.ShapeDtypeStruct((1, width), F32)],
@@ -128,7 +138,7 @@
         ),
         compiler_params=pltpu.CompilerParams(vmem_limit_bytes=24 << 20),
         name="scores",
-    )(*xs, words, w, bias, prop)
+    )(*xs, words, w, label)
     return res, post
 
 
@@ -184,12 +194,6 @@
     )(core, *xs, *rs)
 
 
-def bin_prior(bins, prior_mean):
-    levels = jnp.arange(prior_mean.shape[0], dtype=jnp.int32)
-    onehot = (bins[:, None] == levels[None, :]).astype(F32)
-    return jnp.sum(onehot * prior_mean[None, :], axis=1)
-
-
 def shift(v, axis, n, d):
     return lax.ppermute(v, axis, ring(n, d))
 
@@ -206,26 +210,31 @@
     block = part * NZ
     x_at, core, y = (lax.axis_index(a) for a in ("x", "core", "y"))
     offset = (x_at * NZ + lax.axis_index("z")) * width
-    bias, prop = class_bias[None, :], propensity[None, :]
 
     own = exchange(jnp.tile(embeddings, (NZ, 1)), "z")
-    at = jnp.stack([offset, x_at * block])
-    words, obs = words_call(at, label_ids.T, label_count[None, :], width)
-    prior = bin_prior(label_bins, prior_mean)
+    words, obs, label = words_call(
+        jnp.stack([offset, x_at * block]),
+        prior_mean,
+        label_ids.T,
+        label_count[None, :],
+        class_bias[None, :],
+        propensity[None, :],
+        label_bins[None, :],
+    )
 
     half = block // 2
     front, back = shift(own, "x", NX, -1), shift(own, "x", NX, 1)
     far = (shift(front[:half], "x", NX, -1), shift(back[half:], "x", NX, 1))
-    (res0,), post0 = score_call(((own,),), (0,), words, class_weight, bias, prop)
+    (res0,), post0 = score_call(((own,),), (0,), words, class_weight, label)
     (res1, res3), post1 = score_call(
-        ((front,), (back,)), (block, 3 * block), words, class_weight, bias, prop
+        ((front,), (back,)), (block, 3 * block), words, class_weight, label
     )
     far, post1 = lax.optimization_barrier((far, post1))
-    (res2,), post2 = score_call((far,), (2 * block,), words, class_weight, bias, prop)
+    (res2,), post2 = score_call((far,), (2 * block,), words, class_weight, label)
     post = (post0 + post1) + post2
     both = jnp.concatenate([obs, post], axis=0)[None]
     sums = jnp.sum(exchange(jnp.tile(both, (NY * NC, 1, 1)), ("y", "core")), axis=0)
-    updated = ((sums[0:1] + 8.0 * prior[None, :]) / (sums[1:2] + 8.0)).reshape(width)
+    updated = ((sums[0:1] + label[2:3]) / (sums[1:2] + 8.0)).reshape(width)
 
     kept_rows, given = weight_call(core[None], (own, front, *far, back), (res0, res1, res2, res3))
     pair = kept_rows.astype(F32) + shift(given, "core", NC, 1).astype(F32)

time: 113 us -> 113 us (level)
  blocking collectives: 0 us -> 22.9 us
  waiting for transfers between devices: 31.3 us -> 16.7 us
  starting transfers between devices: 36.4 us -> 27.9 us
    all_to_all x0 -> x1, blocking collectives: none -> 22.9 us  [exchange(): return lax.all_to_all(v, axis, split_axis=0, concat_axis=0, tiled=True)]
    all_to_all x3 -> x2, waiting for transfers between devices: 14.7 us -> 0.01 us  [exchange(): return lax.all_to_all(v, axis, split_axis=0, concat_axis=0, tiled=True)]
    all_to_all x3 -> x2, starting transfers between devices: 16.7 us -> 8.25 us  [exchange(): return lax.all_to_all(v, axis, split_axis=0, concat_axis=0, tiled=True)]
    unnamed x38 -> x44, local copies, waits for them, and re-layouts: 7.44 us -> 8.79 us
  transfers between devices with their start and end apart: 17 -> 16, of which waited for: 5 -> 4; matrix products, arithmetic and copies ran while one was open for 9% -> 9% of each run, Pallas kernels for 18% -> 18%
where the time goes in v5:
time: 113 us; the launch traced here: 111 us
  starting transfers between devices  27.9 us (25%)
  blocking collectives  22.9 us (20%)
  Pallas kernels  22 us (19%)
  waiting for transfers between devices  16.7 us (15%)
  local copies, waits for them, and re-layouts  10.5 us (9%)
  other arithmetic  6.26 us (6%)
  matrix products  3.9 us (3%)
    all_to_all x1, blocking collectives, exchange(): return lax.all_to_all(v, axis, split_axis=0, concat_axis=0, tiled=True)  22.9 us
    ppermute x14, starting transfers between devices, shift(): return lax.ppermute(v, axis, ring(n, d))  19.7 us
    ppermute x14, waiting for transfers between devices, shift(): return lax.ppermute(v, axis, ring(n, d))  16.7 us
    unnamed x44, local copies, waits for them, and re-layouts  8.79 us
    all_to_all x2, starting transfers between devices, exchange(): return lax.all_to_all(v, axis, split_axis=0, concat_axis=0, tiled=True)  8.25 us
    pallas_call x3, Pallas kernels, score_call(): pl.pallas_call(functools.partial(score_kernel, at=at, parts=parts, tile=t...  8.24 us
    pallas_call x1, Pallas kernels, weight_call(): pl.pallas_call(functools.partial(weight_kernel, count=len(xs)), grid=(wid...  7.56 us
    pallas_call x1, Pallas kernels, words_call(): pl.pallas_call(words_kernel, in_specs=[pl.BlockSpec(memory_space=pltpu.SM...  6.21 us
  transfers between devices with their start and end apart: 16, of which 4 were waited for; matrix products, arithmetic and copies ran while one was open for 9% of the time, Pallas kernels for 18%

profile of v5, /device:TPU:16, one launch (start us, length us, event | category | flops | bytes accessed | tf_op | source)
XLA Modules:
  0.0 111.3 jit_solution(579850291990817216)
XLA Ops:
  1.5 22.9 %all_to_all.19 = bf16[8,32,768]{2,1,0:T(8,128)(2,1)S(1)} all-to-all(bf16[8,32,768]{2,1,0:T(8,128)(2,1)S(1)} %tile.4), channel_id=1, replica_groups=mesh['y'=4,'core'=2,'x'=4,'z'=8] {'z'}, dimensions={0} | all-to-all | bytes 786432 | tf_op jit(solution)/shard_map/all_to_all | solution.py:202
  24.4 1.5 %collective-permute-start.2 = (bf16[256,768]{1,0:T(8,128)(2,1)S(1)}, bf16[256,768]{1,0:T(8,128)(2,1)S(1)}, u32[]{:S(2)}, u32[]{:S(2)}) collective-permute-start(bf16[256,768]{1,0:T(8,128)(2,1)S(1)} %bitcast.29), channel_id=1, source_target_pairs={{0,8},{8,16},{16,24},{24,0},{1,9},{9,17},{17,25},{25,1},{2,10},{10... | collective-permute-start | bytes 1179656 | tf_op jit(solution)/shard_map/ppermute | solution.py:198
  25.9 1.7 %collective-permute-start = (bf16[256,768]{1,0:T(8,128)(2,1)S(1)}, bf16[256,768]{1,0:T(8,128)(2,1)S(1)}, u32[]{:S(2)}, u32[]{:S(2)}) collective-permute-start(bf16[256,768]{1,0:T(8,128)(2,1)S(1)} %bitcast.30), channel_id=1, source_target_pairs={{0,24},{8,0},{16,8},{24,16},{1,25},{9,1},{17,9},{25,17},{2,26},{10... | collective-permute-start | bytes 1179656 | tf_op jit(solution)/shard_map/ppermute | solution.py:198
  32.1 6.2 %words.1 = (s32[1024,128]{1,0:T(8,128)S(1)}, f32[1,2048]{1,0:T(1,128)S(1)}, f32[3,2048]{1,0:T(4,128)S(1)}) custom-call(s32[2]{0:T(128)S(1)} %pad_add_fusion.at_ref, f32[16]{0:T(128)S(1)} %copy-done.15, s32[32,1024]{1,0:T(8,128)S(1)} %bitcast.33, s32[1,1024]{1,0:T(1,128)S(1)} %bitcast.37, f32[1,2048]{1,0:T(1,128)S(1)} %bitcast.34, f32[1,2048]{1,0:T(1,128)S(1)} %bitcast.35, ...), custom_call_target="tpu_custom_call" | custom-call | flops 26214400 | bytes 1048576 | tf_op jit(solution)/shard_map/words/pallas_call | solution.py:63
  39.5 3.0 %collective-permute-start.1 = (bf16[128,768]{1,0:T(8,128)(2,1)S(1)}, bf16[128,768]{1,0:T(8,128)(2,1)S(1)}, u32[]{:S(2)}, u32[]{:S(2)}) collective-permute-start(bf16[128,768]{1,0:T(8,128)(2,1)S(1)} %slice.54), channel_id=1, source_target_pairs={{0,24},{8,0},{16,8},{24,16},{1,25},{9,1},{17,9},{25,17},{2,26},{10... | collective-permute-start | bytes 589832 | tf_op jit(solution)/shard_map/ppermute | solution.py:198
  42.4 1.9 %copy-done = bf16[2048,768]{1,0:T(8,128)(2,1)S(1)} copy-done((bf16[2048,768]{1,0:T(8,128)(2,1)S(1)}, bf16[2048,768]{1,0:T(8,128)(2,1)}, u32[]{:S(2)}) %copy-start) | copy-done | bytes 3145752
  44.3 2.3 %scores.3 = (bf16[256,2048]{1,0:T(8,128)(2,1)}, f32[1,2048]{1,0:T(1,128)S(1)}) custom-call(bf16[256,768]{1,0:T(8,128)(2,1)S(1)} %bitcast.31, s32[1024,128]{1,0:T(8,128)S(1)} %get-tuple-element.24.refs_1_.refs_2_, bf16[2048,768]{1,0:T(8,128)(2,1)S(1)} %copy-done, f32[3,2048]{1,0:T(4,128)S(1)} %get-tuple-element.25.refs_3_.refs_4_), custom_call_target="tpu_custom_call" | custom-call | flops 805306368 | bytes 4587520 | tf_op jit(solution)/shard_map/scores/pallas_call | solution.py:126
  46.6 1.0 copy-done.8
  47.6 3.6 %scores.4 = (bf16[256,2048]{1,0:T(8,128)(2,1)}, bf16[256,2048]{1,0:T(8,128)(2,1)}, f32[1,2048]{1,0:T(1,128)S(1)}) custom-call(bf16[256,768]{1,0:T(8,128)(2,1)S(1)} %copy-done.10, bf16[256,768]{1,0:T(8,128)(2,1)S(1)} %copy-done.8, s32[1024,128]{1,0:T(8,128)S(1)} %get-tuple-element.24.refs_1_.refs_2_, bf16[2048,768]{1,0:T(8,128)(2,1)S(1)} %copy-done, ...), custom_call_target="tpu_custom_call" | custom-call | flops 1610612736 | bytes 6029312 | tf_op jit(solution)/shard_map/scores/pallas_call | solution.py:126
  51.4 2.3 %scores.5 = (bf16[256,2048]{1,0:T(8,128)(2,1)}, f32[1,2048]{1,0:T(1,128)S(1)}) custom-call(bf16[128,768]{1,0:T(8,128)(2,1)S(1)} %collective-permute-done.1.refs_0_.refs_2_, bf16[128,768]{1,0:T(8,128)(2,1)S(1)} %collective-permute-done.3.refs_1_.refs_3_, s32[1024,128]{1,0:T(8,128)S(1)} %get-tuple-element.24.refs_1_.refs_2_, bf16[2048,768]{1,0:T(8,128)(2,1)S(1)} %copy-done.1, ...), custom_call_target="tpu_custom_call" | custom-call | flops 805306368 | bytes 4587520 | tf_op jit(solution)/shard_map/scores/pallas_call | solution.py:126
  54.4 4.8 %all-to-all-start.1 = ((f32[8,2,2048]{2,1,0:T(2,128)}), f32[8,2,2048]{2,1,0:T(2,128)S(1)}, u32[]{:S(2)}, u32[]{:S(2)}) async-start(f32[8,2,2048]{2,1,0:T(2,128)} %tile.5), calls=%async_computation.1 | async-start | bytes 262144 | tf_op jit(solution)/shard_map/all_to_all | solution.py:202
  59.2 7.6 %weights.1 = (bf16[4,96,2048]{2,1,0:T(8,128)(2,1)}, bf16[4,96,2048]{2,1,0:T(8,128)(2,1)}) custom-call(s32[1]{0:T(128)} %bitcast.9.core_ref, bf16[256,768]{1,0:T(8,128)(2,1)} %bitcast.32, bf16[256,768]{1,0:T(8,128)(2,1)} %copy-done.9, bf16[128,768]{1,0:T(8,128)(2,1)} %copy-done.4, bf16[128,768]{1,0:T(8,128)(2,1)} %copy-done.3, bf16[256,768]{1,0:T(8,128)(2,1)} %copy-done.7, ...), custom_call_target="tpu_custom_call" | custom-call | flops 3221225472 | bytes 8912896 | tf_op jit(solution)/shard_map/weights/pallas_call | solution.py:174
  71.3 3.2 %collective-permute-start.10 = (bf16[128,768]{1,0:T(8,128)(2,1)S(1)}, bf16[128,768]{1,0:T(8,128)(2,1)S(1)}, u32[]{:S(2)}, u32[]{:S(2)}) collective-permute-start(bf16[128,768]{1,0:T(8,128)(2,1)S(1)} %slice.82), channel_id=1, source_target_pairs={{0,24},{8,0},{16,8},{24,16},{1,25},{9,1},{17,9},{25,17},{2,26},{10... | collective-permute-start | bytes 589832 | tf_op jit(solution)/shard_map/ppermute | solution.py:198
  74.6 1.0 convolution_convert_fusion
  75.9 3.2 %collective-permute-start.12 = (bf16[128,768]{1,0:T(8,128)(2,1)S(1)}, bf16[128,768]{1,0:T(8,128)(2,1)S(1)}, u32[]{:S(2)}, u32[]{:S(2)}) collective-permute-start(bf16[128,768]{1,0:T(8,128)(2,1)S(1)} %get-tuple-element.50), channel_id=1, source_target_pairs={{0,24},{8,0},{16,8},{24,16},{1,25},{9,1},{17,9},{25,17},{2,26},{10... | collective-permute-start | bytes 589832 | tf_op jit(solution)/shard_map/ppermute | solution.py:198
  80.1 3.8 %collective-permute-done.8 = bf16[128,768]{1,0:T(8,128)(2,1)S(1)} collective-permute-done((bf16[128,768]{1,0:T(8,128)(2,1)S(1)}, bf16[128,768]{1,0:T(8,128)(2,1)S(1)}, u32[]{:S(2)}, u32[]{:S(2)}) %collective-permute-start.8) | collective-permute-done | bytes 196640 | tf_op jit(solution)/shard_map/ppermute | solution.py:198
  84.2 3.3 %collective-permute-start.13 = (bf16[128,768]{1,0:T(8,128)(2,1)S(1)}, bf16[128,768]{1,0:T(8,128)(2,1)S(1)}, u32[]{:S(2)}, u32[]{:S(2)}) collective-permute-start(bf16[128,768]{1,0:T(8,128)(2,1)S(1)} %fusion), channel_id=1, source_target_pairs={{0,24},{8,0},{16,8},{24,16},{1,25},{9,1},{17,9},{25,17},{2,26},{10... | collective-permute-start | bytes 589832 | tf_op jit(solution)/shard_map/ppermute | solution.py:198
  87.5 2.0 %add_convert_fusion = bf16[4,96,2048]{2,1,0:T(8,128)(2,1)S(1)} fusion(bf16[4,96,2048]{2,1,0:T(8,128)(2,1)} %collective-permute-done.4, bf16[4,96,2048]{2,1,0:T(8,128)(2,1)S(1)} %copy-done.16), kind=kLoop, calls=%fused_computation.1 | loop fusion | flops 3145728 | bytes 4718592 | tf_op jit(solution)/shard_map/convert_element_type | solution.py:241
  89.6 1.2 %collective-permute-start.5 = (bf16[96,2048]{1,0:T(8,128)(2,1)S(1)}, bf16[96,2048]{1,0:T(8,128)(2,1)S(1)}, u32[]{:S(2)}, u32[]{:S(2)}) collective-permute-start(bf16[96,2048]{1,0:T(8,128)(2,1)S(1)} %get-tuple-element.39), channel_id=1, source_target_pairs={{0,64},{64,128},{128,192},{192,0},{1,65},{65,129},{129,193},{193,1... | collective-permute-start | bytes 1179656 | tf_op jit(solution)/shard_map/ppermute | solution.py:198
  93.3 3.5 %all-to-all-start.2 = ((bf16[8,32,768]{2,1,0:T(8,128)(2,1)}), bf16[8,32,768]{2,1,0:T(8,128)(2,1)S(1)}, u32[]{:S(2)}, u32[]{:S(2)}) async-start(bf16[8,32,768]{2,1,0:T(8,128)(2,1)} %bitcast.15), calls=%async_computation.2 | async-start | bytes 786432 | tf_op jit(solution)/shard_map/all_to_all | solution.py:202
  96.8 4.9 %collective-permute-done.5 = bf16[96,2048]{1,0:T(8,128)(2,1)S(1)} collective-permute-done((bf16[96,2048]{1,0:T(8,128)(2,1)S(1)}, bf16[96,2048]{1,0:T(8,128)(2,1)S(1)}, u32[]{:S(2)}, u32[]{:S(2)}) %collective-permute-start.5) | collective-permute-done | bytes 393248 | tf_op jit(solution)/shard_map/ppermute | solution.py:198
  101.7 6.1 %collective-permute-done.6 = bf16[96,2048]{1,0:T(8,128)(2,1)S(1)} collective-permute-done((bf16[96,2048]{1,0:T(8,128)(2,1)S(1)}, bf16[96,2048]{1,0:T(8,128)(2,1)S(1)}, u32[]{:S(2)}, u32[]{:S(2)}) %collective-permute-start.6) | collective-permute-done | bytes 393248 | tf_op jit(solution)/shard_map/ppermute | solution.py:198
  107.7 1.8 %collective-permute-done.7 = bf16[96,2048]{1,0:T(8,128)(2,1)S(1)} collective-permute-done((bf16[96,2048]{1,0:T(8,128)(2,1)S(1)}, bf16[96,2048]{1,0:T(8,128)(2,1)S(1)}, u32[]{:S(2)}, u32[]{:S(2)}) %collective-permute-start.7) | collective-permute-done | bytes 393248 | tf_op jit(solution)/shard_map/ppermute | solution.py:198
  109.6 1.0 fusion.2
  (83 shorter events, 16.4 us)
Async XLA Ops:
  24.4 26.9 %copy-start.2 = (bf16[8,32,768]{2,1,0:T(8,128)(2,1)}, bf16[8,32,768]{2,1,0:T(8,128)(2,1)S(1)}, u32[]{:S(2)}) copy-start(bf16[8,32,768]{2,1,0:T(8,128)(2,1)S(1)} %all_to_all.19) | copy-start | bytes 1179652
  24.4 13.9 %collective-permute-start.2 = (bf16[256,768]{1,0:T(8,128)(2,1)S(1)}, bf16[256,768]{1,0:T(8,128)(2,1)S(1)}, u32[]{:S(2)}, u32[]{:S(2)}) collective-permute-start(bf16[256,768]{1,0:T(8,128)(2,1)S(1)} %bitcast.29), channel_id=1, source_target_pairs={{0,8},{8,16},{16,24},{24,0},{1,9},{9,17},{17,25},{25,1},{2,10},{10... | collective-permute-start | bytes 1179656 | tf_op jit(solution)/shard_map/ppermute | solution.py:198
  25.9 12.8 %collective-permute-start = (bf16[256,768]{1,0:T(8,128)(2,1)S(1)}, bf16[256,768]{1,0:T(8,128)(2,1)S(1)}, u32[]{:S(2)}, u32[]{:S(2)}) collective-permute-start(bf16[256,768]{1,0:T(8,128)(2,1)S(1)} %bitcast.30), channel_id=1, source_target_pairs={{0,24},{8,0},{16,8},{24,16},{1,25},{9,1},{17,9},{25,17},{2,26},{10... | collective-permute-start | bytes 1179656 | tf_op jit(solution)/shard_map/ppermute | solution.py:198
  38.3 13.1 %copy-start.5 = (f32[3,2048]{1,0:T(4,128)}, f32[3,2048]{1,0:T(4,128)S(1)}, u32[]{:S(2)}) copy-start(f32[3,2048]{1,0:T(4,128)S(1)} %get-tuple-element.25.refs_3_.refs_4_) | copy-start | bytes 73732
  38.3 4.1 %copy-start.7 = (bf16[256,768]{1,0:T(8,128)(2,1)}, bf16[256,768]{1,0:T(8,128)(2,1)S(1)}, u32[]{:S(2)}) copy-start(bf16[256,768]{1,0:T(8,128)(2,1)S(1)} %collective-permute-done.2.refs_1_.refs_4_) | copy-start | bytes 1179652
  38.3 13.0 %collective-permute-start.3 = (bf16[128,768]{1,0:T(8,128)(2,1)S(1)}, bf16[128,768]{1,0:T(8,128)(2,1)S(1)}, u32[]{:S(2)}, u32[]{:S(2)}) collective-permute-start(bf16[128,768]{1,0:T(8,128)(2,1)S(1)} %slice.55), channel_id=1, source_target_pairs={{0,8},{8,16},{16,24},{24,0},{1,9},{9,17},{17,25},{25,1},{2,10},{10... | collective-permute-start | bytes 589832 | tf_op jit(solution)/shard_map/ppermute | solution.py:198
  39.5 11.9 %collective-permute-start.1 = (bf16[128,768]{1,0:T(8,128)(2,1)S(1)}, bf16[128,768]{1,0:T(8,128)(2,1)S(1)}, u32[]{:S(2)}, u32[]{:S(2)}) collective-permute-start(bf16[128,768]{1,0:T(8,128)(2,1)S(1)} %slice.54), channel_id=1, source_target_pairs={{0,24},{8,0},{16,8},{24,16},{1,25},{9,1},{17,9},{25,17},{2,26},{10... | collective-permute-start | bytes 589832 | tf_op jit(solution)/shard_map/ppermute | solution.py:198
  47.6 3.7 %copy-start.1 = (bf16[2048,768]{1,0:T(8,128)(2,1)S(1)}, bf16[2048,768]{1,0:T(8,128)(2,1)}, u32[]{:S(2)}) copy-start(bf16[2048,768]{1,0:T(8,128)(2,1)} %refs_3_.3) | copy-start | bytes 9437188
  54.4 12.5 %all-to-all-start.1 = ((f32[8,2,2048]{2,1,0:T(2,128)}), f32[8,2,2048]{2,1,0:T(2,128)S(1)}, u32[]{:S(2)}, u32[]{:S(2)}) async-start(f32[8,2,2048]{2,1,0:T(2,128)} %tile.5), calls=%async_computation.1 | async-start | bytes 262144 | tf_op jit(solution)/shard_map/all_to_all | solution.py:202
  66.8 20.7 %collective-permute-start.4 = (bf16[4,96,2048]{2,1,0:T(8,128)(2,1)}, bf16[4,96,2048]{2,1,0:T(8,128)(2,1)}, u32[]{:S(2)}, u32[]{:S(2)}) collective-permute-start(bf16[4,96,2048]{2,1,0:T(8,128)(2,1)} %get-tuple-element.37), channel_id=1, source_target_pairs={{0,32},{32,0},{1,33},{33,1},{2,34},{34,2},{3,35},{35,3},{4,36},{36... | collective-permute-start | bytes 4718600 | tf_op jit(solution)/shard_map/ppermute | solution.py:198
  67.7 41.9 %copy-start.17 = (f32[1,2048]{1,0:T(1,128)}, f32[1,2048]{1,0:T(1,128)S(1)}, u32[]{:S(2)}) copy-start(f32[1,2048]{1,0:T(1,128)S(1)} %fusion.3) | copy-start | bytes 24580
  70.2 4.4 %copy-start.19 = (bf16[256,2048]{1,0:T(8,128)(2,1)S(1)}, bf16[256,2048]{1,0:T(8,128)(2,1)}, u32[]{:S(2)}) copy-start(bf16[256,2048]{1,0:T(8,128)(2,1)} %get-tuple-element.34.refs_7_) | copy-start | bytes 3145732
  71.2 7.9 %copy-start.18 = (bf16[256,2048]{1,0:T(8,128)(2,1)S(1)}, bf16[256,2048]{1,0:T(8,128)(2,1)}, u32[]{:S(2)}) copy-start(bf16[256,2048]{1,0:T(8,128)(2,1)} %get-tuple-element.32.refs_5_) | copy-start | bytes 3145732
  71.3 19.6 %collective-permute-start.11 = (bf16[128,768]{1,0:T(8,128)(2,1)S(1)}, bf16[128,768]{1,0:T(8,128)(2,1)S(1)}, u32[]{:S(2)}, u32[]{:S(2)}) collective-permute-start(bf16[128,768]{1,0:T(8,128)(2,1)S(1)} %slice.81), channel_id=1, source_target_pairs={{0,8},{8,16},{16,24},{24,0},{1,9},{9,17},{17,25},{25,1},{2,10},{10... | collective-permute-start | bytes 589832 | tf_op jit(solution)/shard_map/ppermute | solution.py:198
  71.3 20.4 %collective-permute-start.10 = (bf16[128,768]{1,0:T(8,128)(2,1)S(1)}, bf16[128,768]{1,0:T(8,128)(2,1)S(1)}, u32[]{:S(2)}, u32[]{:S(2)}) collective-permute-start(bf16[128,768]{1,0:T(8,128)(2,1)S(1)} %slice.82), channel_id=1, source_target_pairs={{0,24},{8,0},{16,8},{24,16},{1,25},{9,1},{17,9},{25,17},{2,26},{10... | collective-permute-start | bytes 589832 | tf_op jit(solution)/shard_map/ppermute | solution.py:198
  75.6 8.4 %collective-permute-start.8 = (bf16[128,768]{1,0:T(8,128)(2,1)S(1)}, bf16[128,768]{1,0:T(8,128)(2,1)S(1)}, u32[]{:S(2)}, u32[]{:S(2)}) collective-permute-start(bf16[128,768]{1,0:T(8,128)(2,1)S(1)} %get-tuple-element.49), channel_id=1, source_target_pairs={{0,8},{8,16},{16,24},{24,0},{1,9},{9,17},{17,25},{25,1},{2,10},{10... | collective-permute-start | bytes 589832 | tf_op jit(solution)/shard_map/ppermute | solution.py:198
  75.9 11.5 %copy-start.16 = (bf16[4,96,2048]{2,1,0:T(8,128)(2,1)S(1)}, bf16[4,96,2048]{2,1,0:T(8,128)(2,1)}, u32[]{:S(2)}) copy-start(bf16[4,96,2048]{2,1,0:T(8,128)(2,1)} %get-tuple-element.36) | copy-start | bytes 4718596
  75.9 8.2 %collective-permute-start.12 = (bf16[128,768]{1,0:T(8,128)(2,1)S(1)}, bf16[128,768]{1,0:T(8,128)(2,1)S(1)}, u32[]{:S(2)}, u32[]{:S(2)}) collective-permute-start(bf16[128,768]{1,0:T(8,128)(2,1)S(1)} %get-tuple-element.50), channel_id=1, source_target_pairs={{0,24},{8,0},{16,8},{24,16},{1,25},{9,1},{17,9},{25,17},{2,26},{10... | collective-permute-start | bytes 589832 | tf_op jit(solution)/shard_map/ppermute | solution.py:198
  84.0 8.4 %collective-permute-start.9 = (bf16[128,768]{1,0:T(8,128)(2,1)S(1)}, bf16[128,768]{1,0:T(8,128)(2,1)S(1)}, u32[]{:S(2)}, u32[]{:S(2)}) collective-permute-start(bf16[128,768]{1,0:T(8,128)(2,1)S(1)} %fusion.1), channel_id=1, source_target_pairs={{0,8},{8,16},{16,24},{24,0},{1,9},{9,17},{17,25},{25,1},{2,10},{10... | collective-permute-start | bytes 589832 | tf_op jit(solution)/shard_map/ppermute | solution.py:198
  84.2 8.3 %collective-permute-start.13 = (bf16[128,768]{1,0:T(8,128)(2,1)S(1)}, bf16[128,768]{1,0:T(8,128)(2,1)S(1)}, u32[]{:S(2)}, u32[]{:S(2)}) collective-permute-start(bf16[128,768]{1,0:T(8,128)(2,1)S(1)} %fusion), channel_id=1, source_target_pairs={{0,24},{8,0},{16,8},{24,16},{1,25},{9,1},{17,9},{25,17},{2,26},{10... | collective-permute-start | bytes 589832 | tf_op jit(solution)/shard_map/ppermute | solution.py:198
  89.6 12.1 %collective-permute-start.5 = (bf16[96,2048]{1,0:T(8,128)(2,1)S(1)}, bf16[96,2048]{1,0:T(8,128)(2,1)S(1)}, u32[]{:S(2)}, u32[]{:S(2)}) collective-permute-start(bf16[96,2048]{1,0:T(8,128)(2,1)S(1)} %get-tuple-element.39), channel_id=1, source_target_pairs={{0,64},{64,128},{128,192},{192,0},{1,65},{65,129},{129,193},{193,1... | collective-permute-start | bytes 1179656 | tf_op jit(solution)/shard_map/ppermute | solution.py:198
  90.8 16.9 %collective-permute-start.6 = (bf16[96,2048]{1,0:T(8,128)(2,1)S(1)}, bf16[96,2048]{1,0:T(8,128)(2,1)S(1)}, u32[]{:S(2)}, u32[]{:S(2)}) collective-permute-start(bf16[96,2048]{1,0:T(8,128)(2,1)S(1)} %get-tuple-element.40), channel_id=1, source_target_pairs={{0,128},{64,192},{128,0},{192,64},{1,129},{65,193},{129,1},{193,65... | collective-permute-start | bytes 1179656 | tf_op jit(solution)/shard_map/ppermute | solution.py:198
  91.7 17.9 %collective-permute-start.7 = (bf16[96,2048]{1,0:T(8,128)(2,1)S(1)}, bf16[96,2048]{1,0:T(8,128)(2,1)S(1)}, u32[]{:S(2)}, u32[]{:S(2)}) collective-permute-start(bf16[96,2048]{1,0:T(8,128)(2,1)S(1)} %get-tuple-element.41), channel_id=1, source_target_pairs={{0,192},{64,0},{128,64},{192,128},{1,193},{65,1},{129,65},{193,129... | collective-permute-start | bytes 1179656 | tf_op jit(solution)/shard_map/ppermute | solution.py:198
  93.3 17.3 %all-to-all-start.2 = ((bf16[8,32,768]{2,1,0:T(8,128)(2,1)}), bf16[8,32,768]{2,1,0:T(8,128)(2,1)S(1)}, u32[]{:S(2)}, u32[]{:S(2)}) async-start(bf16[8,32,768]{2,1,0:T(8,128)(2,1)} %bitcast.15), calls=%async_computation.2 | async-start | bytes 786432 | tf_op jit(solution)/shard_map/all_to_all | solution.py:202
  (14 other events, 17.4 us)

commit v6 on v1

--- a/solution.py
+++ b/solution.py
@@ -22,7 +22,7 @@
     return lax.dot_general(a, b, (dims, ((), ())), preferred_element_type=F32)
 
 
-def words_kernel(at_ref, ids_ref, count_ref, words_ref, obs_ref, *, width):
+def words_kernel(at_ref, ids_ref, count_ref, _, words_ref, obs_ref, *, width):
     slots, rows = ids_ref.shape
     lanes = lax.broadcasted_iota(jnp.int32, (LANES, LANES), 1)
     slot = lax.broadcasted_iota(jnp.int32, (slots, LANES), 0)
@@ -48,11 +48,12 @@
         )
 
 
-def words_call(at, ids, count, width):
+def words_call(at, ids, count, w):
+    width = w.shape[0]
     rows = ids.shape[1]
     return pl.pallas_call(
         functools.partial(words_kernel, width=width),
-        in_specs=[pl.BlockSpec(memory_space=pltpu.SMEM)] + in_vmem(2),
+        in_specs=[pl.BlockSpec(memory_space=pltpu.SMEM)] + in_vmem(3),
         out_specs=in_vmem(2),
         out_shape=[
             jax.ShapeDtypeStruct((rows, LANES), jnp.int32),
@@ -63,7 +64,7 @@
         ),
         compiler_params=pltpu.CompilerParams(vmem_limit_bytes=16 << 20),
         name="words",
-    )(at, ids, count)
+    )(at, ids, count, w)
 
 
 def score_kernel(*refs, at, parts, tile):
@@ -210,7 +211,7 @@
 
     own = exchange(jnp.tile(embeddings, (NZ, 1)), "z")
     at = jnp.stack([offset, x_at * block])
-    words, obs = words_call(at, label_ids.T, label_count[None, :], width)
+    words, obs = words_call(at, label_ids.T, label_count[None, :], class_weight)
     prior = bin_prior(label_bins, prior_mean)
 
     half = block // 2

time: 113 us -> 114 us (level)
    unnamed x38, local copies, waits for them, and re-layouts: 7.44 us -> 4.93 us
    slice x2, local copies, waits for them, and re-layouts: 0.03 us -> 1.88 us  [body(): far = (shift(front[:half], 'x', NX, -1), shift(back[half:], 'x', NX, 1))]
  transfers between devices with their start and end apart: 17 -> 17, of which waited for: 5 -> 5; matrix products, arithmetic and copies ran while one was open for 9% -> 11% of each run, Pallas kernels for 18% -> 19%
where the time goes in v6:
time: 114 us; the launch traced here: 112 us
  starting transfers between devices  36.7 us (32%)
  waiting for transfers between devices  31.3 us (27%)
  Pallas kernels  23.1 us (20%)
  local copies, waits for them, and re-layouts  9.28 us (8%)
  other arithmetic  6.72 us (6%)
  matrix products  3.9 us (3%)
    ppermute x14, starting transfers between devices, shift(): return lax.ppermute(v, axis, ring(n, d))  19.9 us
    all_to_all x3, starting transfers between devices, exchange(): return lax.all_to_all(v, axis, split_axis=0, concat_axis=0, tiled=True)  16.7 us
    ppermute x14, waiting for transfers between devices, shift(): return lax.ppermute(v, axis, ring(n, d))  16.6 us
    all_to_all x3, waiting for transfers between devices, exchange(): return lax.all_to_all(v, axis, split_axis=0, concat_axis=0, tiled=True)  14.7 us
    pallas_call x3, Pallas kernels, score_call(): pl.pallas_call(functools.partial(score_kernel, at=at, parts=parts, tile=t...  9.35 us
    pallas_call x1, Pallas kernels, weight_call(): pl.pallas_call(functools.partial(weight_kernel, count=len(xs)), grid=(wid...  7.56 us
    pallas_call x1, Pallas kernels, words_call(): pl.pallas_call(functools.partial(words_kernel, width=width), in_specs=[pl...  6.19 us
    unnamed x38, local copies, waits for them, and re-layouts  4.93 us
  transfers between devices with their start and end apart: 17, of which 5 were waited for; matrix products, arithmetic and copies ran while one was open for 11% of the time, Pallas kernels for 19%

profile of v6, /device:TPU:16, one launch (start us, length us, event | category | flops | bytes accessed | tf_op | source)
XLA Modules:
  0.0 112.0 jit_solution(7650757214283267563)
XLA Ops:
  0.7 1.6 %tile.4 = bf16[8,32,768]{2,1,0:T(8,128)(2,1)} broadcast(bf16[32,768]{1,0:T(8,128)(2,1)} %param.8), dimensions={1,2} | broadcast | bytes 442368 | tf_op jit(solution)/shard_map/tile | solution.py:212
  2.2 8.5 %all-to-all-start = ((bf16[8,32,768]{2,1,0:T(8,128)(2,1)}), bf16[8,32,768]{2,1,0:T(8,128)(2,1)S(1)}, u32[]{:S(2)}, u32[]{:S(2)}) async-start(bf16[8,32,768]{2,1,0:T(8,128)(2,1)} %tile.4), calls=%async_computation | async-start | bytes 786432 | tf_op jit(solution)/shard_map/all_to_all | solution.py:199
  10.7 14.7 %all-to-all-done = bf16[8,32,768]{2,1,0:T(8,128)(2,1)S(1)} async-done(((bf16[8,32,768]{2,1,0:T(8,128)(2,1)}), bf16[8,32,768]{2,1,0:T(8,128)(2,1)S(1)}, u32[]{:S(2)}, u32[]{:S(2)}) %all-to-all-start) | async-done | bytes 393248 | tf_op jit(solution)/shard_map/all_to_all | solution.py:199
  25.4 1.5 %collective-permute-start.2 = (bf16[256,768]{1,0:T(8,128)(2,1)S(1)}, bf16[256,768]{1,0:T(8,128)(2,1)}, u32[]{:S(2)}, u32[]{:S(2)}) collective-permute-start(bf16[256,768]{1,0:T(8,128)(2,1)S(1)} %bitcast.29), channel_id=1, source_target_pairs={{0,8},{8,16},{16,24},{24,0},{1,9},{9,17},{17,25},{25,1},{2,10},{10... | collective-permute-start | bytes 1179656 | tf_op jit(solution)/shard_map/ppermute | solution.py:195
  26.9 1.7 %collective-permute-start = (bf16[256,768]{1,0:T(8,128)(2,1)S(1)}, bf16[256,768]{1,0:T(8,128)(2,1)}, u32[]{:S(2)}, u32[]{:S(2)}) collective-permute-start(bf16[256,768]{1,0:T(8,128)(2,1)S(1)} %bitcast.30), channel_id=1, source_target_pairs={{0,24},{8,0},{16,8},{24,16},{1,25},{9,1},{17,9},{25,17},{2,26},{10... | collective-permute-start | bytes 1179656 | tf_op jit(solution)/shard_map/ppermute | solution.py:195
  29.2 1.9 %copy-done = bf16[2048,768]{1,0:T(8,128)(2,1)S(1)} copy-done((bf16[2048,768]{1,0:T(8,128)(2,1)S(1)}, bf16[2048,768]{1,0:T(8,128)(2,1)}, u32[]{:S(2)}) %copy-start) | copy-done | bytes 3145752
  33.3 6.2 %words.1 = (s32[1024,128]{1,0:T(8,128)S(1)}, f32[1,2048]{1,0:T(1,128)S(1)}) custom-call(s32[2]{0:T(128)S(1)} %copy-done.9, s32[32,1024]{1,0:T(8,128)S(1)} %bitcast.33, s32[1,1024]{1,0:T(1,128)S(1)} %bitcast.40, bf16[2048,768]{1,0:T(8,128)(2,1)S(1)} %copy-done), custom_call_target="tpu_custom_call" | custom-call | flops 26214400 | bytes 1048576 | tf_op jit(solution)/shard_map/words/pallas_call | solution.py:54
  42.5 3.2 %collective-permute-start.1 = (bf16[128,768]{1,0:T(8,128)(2,1)S(1)}, bf16[128,768]{1,0:T(8,128)(2,1)S(1)}, u32[]{:S(2)}, u32[]{:S(2)}) collective-permute-start(bf16[128,768]{1,0:T(8,128)(2,1)S(1)} %slice.50), channel_id=1, source_target_pairs={{0,24},{8,0},{16,8},{24,16},{1,25},{9,1},{17,9},{25,17},{2,26},{10... | collective-permute-start | bytes 589832 | tf_op jit(solution)/shard_map/ppermute | solution.py:195
  45.7 2.3 %scores.3 = (bf16[256,2048]{1,0:T(8,128)(2,1)}, f32[1,2048]{1,0:T(1,128)S(1)}) custom-call(bf16[256,768]{1,0:T(8,128)(2,1)S(1)} %bitcast.31, s32[1024,128]{1,0:T(8,128)S(1)} %get-tuple-element.23.refs_1_.refs_2_, bf16[2048,768]{1,0:T(8,128)(2,1)S(1)} %copy-done.1, f32[1,2048]{1,0:T(1,128)S(1)} %bitcast.34, f32[1,2048]{1,0:T(1,128)S(1)} %bitcast.37), custom_call_target="tpu_custom_call" | custom-call | flops 805306368 | bytes 4587520 | tf_op jit(solution)/shard_map/scores/pallas_call | solution.py:117
  48.0 4.7 %scores.4 = (bf16[256,2048]{1,0:T(8,128)(2,1)}, bf16[256,2048]{1,0:T(8,128)(2,1)}, f32[1,2048]{1,0:T(1,128)S(1)}) custom-call(bf16[256,768]{1,0:T(8,128)(2,1)} %collective-permute-done.refs_0_.refs_1_, bf16[256,768]{1,0:T(8,128)(2,1)} %collective-permute-done.2.refs_1_.refs_4_, s32[1024,128]{1,0:T(8,128)S(1)} %get-tuple-element.23.refs_1_.refs_2_, ...), custom_call_target="tpu_custom_call" | custom-call | flops 1610612736 | bytes 6029312 | tf_op jit(solution)/shard_map/scores/pallas_call | solution.py:117
  52.8 2.3 %scores.5 = (bf16[256,2048]{1,0:T(8,128)(2,1)}, f32[1,2048]{1,0:T(1,128)S(1)}) custom-call(bf16[128,768]{1,0:T(8,128)(2,1)S(1)} %collective-permute-done.1.refs_0_.refs_2_, bf16[128,768]{1,0:T(8,128)(2,1)S(1)} %collective-permute-done.3.refs_1_.refs_3_, s32[1024,128]{1,0:T(8,128)S(1)} %get-tuple-element.23.refs_1_.refs_2_, bf16[2048,768]{1,0:T(8,128)(2,1)S(1)} %copy-done.1, ...), custom_call_target="tpu_custom_call" | custom-call | flops 805306368 | bytes 4587520 | tf_op jit(solution)/shard_map/scores/pallas_call | solution.py:117
  55.9 4.8 %all-to-all-start.1 = ((f32[8,2,2048]{2,1,0:T(2,128)}), f32[8,2,2048]{2,1,0:T(2,128)S(1)}, u32[]{:S(2)}, u32[]{:S(2)}) async-start(f32[8,2,2048]{2,1,0:T(2,128)} %tile.5), calls=%async_computation.1 | async-start | bytes 262144 | tf_op jit(solution)/shard_map/all_to_all | solution.py:199
  60.7 7.6 %weights.1 = (bf16[4,96,2048]{2,1,0:T(8,128)(2,1)}, bf16[4,96,2048]{2,1,0:T(8,128)(2,1)}) custom-call(s32[1]{0:T(128)} %bitcast.9.core_ref, bf16[256,768]{1,0:T(8,128)(2,1)} %bitcast.32, bf16[256,768]{1,0:T(8,128)(2,1)} %collective-permute-done.refs_0_.refs_1_, bf16[128,768]{1,0:T(8,128)(2,1)} %copy-done.4, bf16[128,768]{1,0:T(8,128)(2,1)} %copy-done.3, ...), custom_call_target="tpu_custom_call" | custom-call | flops 3221225472 | bytes 8912896 | tf_op jit(solution)/shard_map/weights/pallas_call | solution.py:165
  72.1 3.2 %collective-permute-start.10 = (bf16[128,768]{1,0:T(8,128)(2,1)S(1)}, bf16[128,768]{1,0:T(8,128)(2,1)S(1)}, u32[]{:S(2)}, u32[]{:S(2)}) collective-permute-start(bf16[128,768]{1,0:T(8,128)(2,1)S(1)} %slice.77), channel_id=1, source_target_pairs={{0,24},{8,0},{16,8},{24,16},{1,25},{9,1},{17,9},{25,17},{2,26},{10... | collective-permute-start | bytes 589832 | tf_op jit(solution)/shard_map/ppermute | solution.py:195
  76.6 3.2 %collective-permute-start.12 = (bf16[128,768]{1,0:T(8,128)(2,1)S(1)}, bf16[128,768]{1,0:T(8,128)(2,1)S(1)}, u32[]{:S(2)}, u32[]{:S(2)}) collective-permute-start(bf16[128,768]{1,0:T(8,128)(2,1)S(1)} %get-tuple-element.48), channel_id=1, source_target_pairs={{0,24},{8,0},{16,8},{24,16},{1,25},{9,1},{17,9},{25,17},{2,26},{10... | collective-permute-start | bytes 589832 | tf_op jit(solution)/shard_map/ppermute | solution.py:195
  80.8 3.8 %collective-permute-done.8 = bf16[128,768]{1,0:T(8,128)(2,1)S(1)} collective-permute-done((bf16[128,768]{1,0:T(8,128)(2,1)S(1)}, bf16[128,768]{1,0:T(8,128)(2,1)S(1)}, u32[]{:S(2)}, u32[]{:S(2)}) %collective-permute-start.8) | collective-permute-done | bytes 196640 | tf_op jit(solution)/shard_map/ppermute | solution.py:195
  84.9 3.3 %collective-permute-start.13 = (bf16[128,768]{1,0:T(8,128)(2,1)S(1)}, bf16[128,768]{1,0:T(8,128)(2,1)S(1)}, u32[]{:S(2)}, u32[]{:S(2)}) collective-permute-start(bf16[128,768]{1,0:T(8,128)(2,1)S(1)} %fusion), channel_id=1, source_target_pairs={{0,24},{8,0},{16,8},{24,16},{1,25},{9,1},{17,9},{25,17},{2,26},{10... | collective-permute-start | bytes 589832 | tf_op jit(solution)/shard_map/ppermute | solution.py:195
  88.2 2.0 %add_convert_fusion = bf16[4,96,2048]{2,1,0:T(8,128)(2,1)S(1)} fusion(bf16[4,96,2048]{2,1,0:T(8,128)(2,1)} %collective-permute-done.4, bf16[4,96,2048]{2,1,0:T(8,128)(2,1)S(1)} %copy-done.10), kind=kLoop, calls=%fused_computation.1 | loop fusion | flops 3145728 | bytes 4718592 | tf_op jit(solution)/shard_map/convert_element_type | solution.py:233
  90.3 1.2 %collective-permute-start.5 = (bf16[96,2048]{1,0:T(8,128)(2,1)S(1)}, bf16[96,2048]{1,0:T(8,128)(2,1)S(1)}, u32[]{:S(2)}, u32[]{:S(2)}) collective-permute-start(bf16[96,2048]{1,0:T(8,128)(2,1)S(1)} %get-tuple-element.37), channel_id=1, source_target_pairs={{0,64},{64,128},{128,192},{192,0},{1,65},{65,129},{129,193},{193,1... | collective-permute-start | bytes 1179656 | tf_op jit(solution)/shard_map/ppermute | solution.py:195
  94.1 3.5 %all-to-all-start.2 = ((bf16[8,32,768]{2,1,0:T(8,128)(2,1)}), bf16[8,32,768]{2,1,0:T(8,128)(2,1)S(1)}, u32[]{:S(2)}, u32[]{:S(2)}) async-start(bf16[8,32,768]{2,1,0:T(8,128)(2,1)} %bitcast.15), calls=%async_computation.2 | async-start | bytes 786432 | tf_op jit(solution)/shard_map/all_to_all | solution.py:199
  97.5 4.9 %collective-permute-done.5 = bf16[96,2048]{1,0:T(8,128)(2,1)S(1)} collective-permute-done((bf16[96,2048]{1,0:T(8,128)(2,1)S(1)}, bf16[96,2048]{1,0:T(8,128)(2,1)S(1)}, u32[]{:S(2)}, u32[]{:S(2)}) %collective-permute-start.5) | collective-permute-done | bytes 393248 | tf_op jit(solution)/shard_map/ppermute | solution.py:195
  102.4 6.1 %collective-permute-done.6 = bf16[96,2048]{1,0:T(8,128)(2,1)S(1)} collective-permute-done((bf16[96,2048]{1,0:T(8,128)(2,1)S(1)}, bf16[96,2048]{1,0:T(8,128)(2,1)S(1)}, u32[]{:S(2)}, u32[]{:S(2)}) %collective-permute-start.6) | collective-permute-done | bytes 393248 | tf_op jit(solution)/shard_map/ppermute | solution.py:195
  108.5 1.8 %collective-permute-done.7 = bf16[96,2048]{1,0:T(8,128)(2,1)S(1)} collective-permute-done((bf16[96,2048]{1,0:T(8,128)(2,1)S(1)}, bf16[96,2048]{1,0:T(8,128)(2,1)S(1)}, u32[]{:S(2)}, u32[]{:S(2)}) %collective-permute-start.7) | collective-permute-done | bytes 393248 | tf_op jit(solution)/shard_map/ppermute | solution.py:195
  110.3 1.0 fusion.2
  (80 shorter events, 16.0 us)
Async XLA Ops:
  0.6 45.1 %copy-start.7 = (f32[2048]{0:T(1024)S(1)}, f32[2048]{0:T(1024)}, u32[]{:S(2)}) copy-start(f32[2048]{0:T(1024)} %param.11) | copy-start | bytes 24580
  0.6 45.1 %copy-start.6 = (f32[2048]{0:T(1024)S(1)}, f32[2048]{0:T(1024)}, u32[]{:S(2)}) copy-start(f32[2048]{0:T(1024)} %param.10) | copy-start | bytes 24580
  2.2 23.2 %all-to-all-start = ((bf16[8,32,768]{2,1,0:T(8,128)(2,1)}), bf16[8,32,768]{2,1,0:T(8,128)(2,1)S(1)}, u32[]{:S(2)}, u32[]{:S(2)}) async-start(bf16[8,32,768]{2,1,0:T(8,128)(2,1)} %tile.4), calls=%async_computation | async-start | bytes 786432 | tf_op jit(solution)/shard_map/all_to_all | solution.py:199
  25.4 22.6 %copy-start.2 = (bf16[8,32,768]{2,1,0:T(8,128)(2,1)}, bf16[8,32,768]{2,1,0:T(8,128)(2,1)S(1)}, u32[]{:S(2)}) copy-start(bf16[8,32,768]{2,1,0:T(8,128)(2,1)S(1)} %all-to-all-done) | copy-start | bytes 1179652
  25.4 14.8 %collective-permute-start.2 = (bf16[256,768]{1,0:T(8,128)(2,1)S(1)}, bf16[256,768]{1,0:T(8,128)(2,1)}, u32[]{:S(2)}, u32[]{:S(2)}) collective-permute-start(bf16[256,768]{1,0:T(8,128)(2,1)S(1)} %bitcast.29), channel_id=1, source_target_pairs={{0,8},{8,16},{16,24},{24,0},{1,9},{9,17},{17,25},{25,1},{2,10},{10... | collective-permute-start | bytes 1179656 | tf_op jit(solution)/shard_map/ppermute | solution.py:195
  26.9 14.6 %collective-permute-start = (bf16[256,768]{1,0:T(8,128)(2,1)S(1)}, bf16[256,768]{1,0:T(8,128)(2,1)}, u32[]{:S(2)}, u32[]{:S(2)}) collective-permute-start(bf16[256,768]{1,0:T(8,128)(2,1)S(1)} %bitcast.30), channel_id=1, source_target_pairs={{0,24},{8,0},{16,8},{24,16},{1,25},{9,1},{17,9},{25,17},{2,26},{10... | collective-permute-start | bytes 1179656 | tf_op jit(solution)/shard_map/ppermute | solution.py:195
  29.2 10.3 %copy-start.14 = (f32[16]{0:T(128)S(1)}, f32[16]{0:T(128)}, u32[]{:S(2)}) copy-start(f32[16]{0:T(128)} %param.15) | copy-start | bytes 196
  33.3 12.4 %copy-start.1 = (bf16[2048,768]{1,0:T(8,128)(2,1)S(1)}, bf16[2048,768]{1,0:T(8,128)(2,1)}, u32[]{:S(2)}) copy-start(bf16[2048,768]{1,0:T(8,128)(2,1)} %refs_3_.3) | copy-start | bytes 9437188
  41.2 11.6 %collective-permute-start.3 = (bf16[128,768]{1,0:T(8,128)(2,1)S(1)}, bf16[128,768]{1,0:T(8,128)(2,1)S(1)}, u32[]{:S(2)}, u32[]{:S(2)}) collective-permute-start(bf16[128,768]{1,0:T(8,128)(2,1)S(1)} %slice.51), channel_id=1, source_target_pairs={{0,8},{8,16},{16,24},{24,0},{1,9},{9,17},{17,25},{25,1},{2,10},{10... | collective-permute-start | bytes 589832 | tf_op jit(solution)/shard_map/ppermute | solution.py:195
  42.5 10.3 %collective-permute-start.1 = (bf16[128,768]{1,0:T(8,128)(2,1)S(1)}, bf16[128,768]{1,0:T(8,128)(2,1)S(1)}, u32[]{:S(2)}, u32[]{:S(2)}) collective-permute-start(bf16[128,768]{1,0:T(8,128)(2,1)S(1)} %slice.50), channel_id=1, source_target_pairs={{0,24},{8,0},{16,8},{24,16},{1,25},{9,1},{17,9},{25,17},{2,26},{10... | collective-permute-start | bytes 589832 | tf_op jit(solution)/shard_map/ppermute | solution.py:195
  55.9 12.5 %all-to-all-start.1 = ((f32[8,2,2048]{2,1,0:T(2,128)}), f32[8,2,2048]{2,1,0:T(2,128)S(1)}, u32[]{:S(2)}, u32[]{:S(2)}) async-start(f32[8,2,2048]{2,1,0:T(2,128)} %tile.5), calls=%async_computation.1 | async-start | bytes 262144 | tf_op jit(solution)/shard_map/all_to_all | solution.py:199
  68.2 19.9 %collective-permute-start.4 = (bf16[4,96,2048]{2,1,0:T(8,128)(2,1)}, bf16[4,96,2048]{2,1,0:T(8,128)(2,1)}, u32[]{:S(2)}, u32[]{:S(2)}) collective-permute-start(bf16[4,96,2048]{2,1,0:T(8,128)(2,1)} %get-tuple-element.35), channel_id=1, source_target_pairs={{0,32},{32,0},{1,33},{33,1},{2,34},{34,2},{3,35},{35,3},{4,36},{36... | collective-permute-start | bytes 4718600 | tf_op jit(solution)/shard_map/ppermute | solution.py:195
  68.5 41.8 %copy-start.11 = (f32[1,2048]{1,0:T(1,128)}, f32[1,2048]{1,0:T(1,128)S(1)}, u32[]{:S(2)}) copy-start(f32[1,2048]{1,0:T(1,128)S(1)} %fusion.3) | copy-start | bytes 24580
  72.0 19.6 %collective-permute-start.11 = (bf16[128,768]{1,0:T(8,128)(2,1)S(1)}, bf16[128,768]{1,0:T(8,128)(2,1)S(1)}, u32[]{:S(2)}, u32[]{:S(2)}) collective-permute-start(bf16[128,768]{1,0:T(8,128)(2,1)S(1)} %slice.76), channel_id=1, source_target_pairs={{0,8},{8,16},{16,24},{24,0},{1,9},{9,17},{17,25},{25,1},{2,10},{10... | collective-permute-start | bytes 589832 | tf_op jit(solution)/shard_map/ppermute | solution.py:195
  72.1 20.4 %collective-permute-start.10 = (bf16[128,768]{1,0:T(8,128)(2,1)S(1)}, bf16[128,768]{1,0:T(8,128)(2,1)S(1)}, u32[]{:S(2)}, u32[]{:S(2)}) collective-permute-start(bf16[128,768]{1,0:T(8,128)(2,1)S(1)} %slice.77), channel_id=1, source_target_pairs={{0,24},{8,0},{16,8},{24,16},{1,25},{9,1},{17,9},{25,17},{2,26},{10... | collective-permute-start | bytes 589832 | tf_op jit(solution)/shard_map/ppermute | solution.py:195
  76.3 8.4 %collective-permute-start.8 = (bf16[128,768]{1,0:T(8,128)(2,1)S(1)}, bf16[128,768]{1,0:T(8,128)(2,1)S(1)}, u32[]{:S(2)}, u32[]{:S(2)}) collective-permute-start(bf16[128,768]{1,0:T(8,128)(2,1)S(1)} %get-tuple-element.47), channel_id=1, source_target_pairs={{0,8},{8,16},{16,24},{24,0},{1,9},{9,17},{17,25},{25,1},{2,10},{10... | collective-permute-start | bytes 589832 | tf_op jit(solution)/shard_map/ppermute | solution.py:195
  76.6 11.5 %copy-start.10 = (bf16[4,96,2048]{2,1,0:T(8,128)(2,1)S(1)}, bf16[4,96,2048]{2,1,0:T(8,128)(2,1)}, u32[]{:S(2)}) copy-start(bf16[4,96,2048]{2,1,0:T(8,128)(2,1)} %get-tuple-element.34) | copy-start | bytes 4718596
  76.6 8.2 %collective-permute-start.12 = (bf16[128,768]{1,0:T(8,128)(2,1)S(1)}, bf16[128,768]{1,0:T(8,128)(2,1)S(1)}, u32[]{:S(2)}, u32[]{:S(2)}) collective-permute-start(bf16[128,768]{1,0:T(8,128)(2,1)S(1)} %get-tuple-element.48), channel_id=1, source_target_pairs={{0,24},{8,0},{16,8},{24,16},{1,25},{9,1},{17,9},{25,17},{2,26},{10... | collective-permute-start | bytes 589832 | tf_op jit(solution)/shard_map/ppermute | solution.py:195
  84.7 8.4 %collective-permute-start.9 = (bf16[128,768]{1,0:T(8,128)(2,1)S(1)}, bf16[128,768]{1,0:T(8,128)(2,1)S(1)}, u32[]{:S(2)}, u32[]{:S(2)}) collective-permute-start(bf16[128,768]{1,0:T(8,128)(2,1)S(1)} %fusion.1), channel_id=1, source_target_pairs={{0,8},{8,16},{16,24},{24,0},{1,9},{9,17},{17,25},{25,1},{2,10},{10... | collective-permute-start | bytes 589832 | tf_op jit(solution)/shard_map/ppermute | solution.py:195
  84.9 8.3 %collective-permute-start.13 = (bf16[128,768]{1,0:T(8,128)(2,1)S(1)}, bf16[128,768]{1,0:T(8,128)(2,1)S(1)}, u32[]{:S(2)}, u32[]{:S(2)}) collective-permute-start(bf16[128,768]{1,0:T(8,128)(2,1)S(1)} %fusion), channel_id=1, source_target_pairs={{0,24},{8,0},{16,8},{24,16},{1,25},{9,1},{17,9},{25,17},{2,26},{10... | collective-permute-start | bytes 589832 | tf_op jit(solution)/shard_map/ppermute | solution.py:195
  90.3 12.1 %collective-permute-start.5 = (bf16[96,2048]{1,0:T(8,128)(2,1)S(1)}, bf16[96,2048]{1,0:T(8,128)(2,1)S(1)}, u32[]{:S(2)}, u32[]{:S(2)}) collective-permute-start(bf16[96,2048]{1,0:T(8,128)(2,1)S(1)} %get-tuple-element.37), channel_id=1, source_target_pairs={{0,64},{64,128},{128,192},{192,0},{1,65},{65,129},{129,193},{193,1... | collective-permute-start | bytes 1179656 | tf_op jit(solution)/shard_map/ppermute | solution.py:195
  91.6 16.9 %collective-permute-start.6 = (bf16[96,2048]{1,0:T(8,128)(2,1)S(1)}, bf16[96,2048]{1,0:T(8,128)(2,1)S(1)}, u32[]{:S(2)}, u32[]{:S(2)}) collective-permute-start(bf16[96,2048]{1,0:T(8,128)(2,1)S(1)} %get-tuple-element.38), channel_id=1, source_target_pairs={{0,128},{64,192},{128,0},{192,64},{1,129},{65,193},{129,1},{193,65... | collective-permute-start | bytes 1179656 | tf_op jit(solution)/shard_map/ppermute | solution.py:195
  92.4 17.9 %collective-permute-start.7 = (bf16[96,2048]{1,0:T(8,128)(2,1)S(1)}, bf16[96,2048]{1,0:T(8,128)(2,1)S(1)}, u32[]{:S(2)}, u32[]{:S(2)}) collective-permute-start(bf16[96,2048]{1,0:T(8,128)(2,1)S(1)} %get-tuple-element.39), channel_id=1, source_target_pairs={{0,192},{64,0},{128,64},{192,128},{1,193},{65,1},{129,65},{193,129... | collective-permute-start | bytes 1179656 | tf_op jit(solution)/shard_map/ppermute | solution.py:195
  94.1 17.2 %all-to-all-start.2 = ((bf16[8,32,768]{2,1,0:T(8,128)(2,1)}), bf16[8,32,768]{2,1,0:T(8,128)(2,1)S(1)}, u32[]{:S(2)}, u32[]{:S(2)}) async-start(bf16[8,32,768]{2,1,0:T(8,128)(2,1)} %bitcast.15), calls=%async_computation.2 | async-start | bytes 786432 | tf_op jit(solution)/shard_map/all_to_all | solution.py:199
  (12 other events, 37.5 us)
